TPU v7x, 128 devices: a whole 4x4x4 slice. The times are simulated.
128 devices in a mesh: stretch: 32 (over z, y, core), section: 4 (over x).
Axes of the slice: x: 4, y: 4, z: 4, core: 2. Of those that a mesh axis runs over, the one named last changes fastest.
Arguments:
- hidden: bfloat16 [4, 16384, 4096], P('section', 'stretch'), may hold values from -64 to 64
- norm_gain: float32 [4, 4096], P('section'), may hold values from 0.5 to 1.5
- queries: bfloat16 [4, 16384, 2048], P('section', 'stretch'), may hold values from -110 to 110
- cache: bfloat16 [4, 512, 32, 4096], P('section', 'stretch'), may hold values from -35 to 35
- nbr_shard: int32 [256, 2], P('stretch'), may hold values from 0 to 31, as said below
- nbr_slot: int32 [256, 2], P('stretch'), may hold values from 0 to 15
- grad_heads: bfloat16 [4, 16384, 2048], P('section', 'stretch'), may hold values from -24 to 24
- grad_out: bfloat16 [4, 16384, 4096], P('section', 'stretch'), may hold values from -3 to 3
- query_weight: bfloat16 [4, 4096, 2048], P('section', 'stretch'), may hold values from -0.09375 to 0.09375
Outputs:
- section_grads: bfloat16 [4, 16384, 4096], P('section', 'stretch')
Inputs may be any that keep to these rules, and one draw needn't show every extreme that they name: `nbr_shard`: the 2 shards of a stretch differ. In the 8 stretches of one device (aligned blocks of rows) no shard is named more than 1 times; one shard is named exactly 1 times in every such block.
All inputs are finite; a program needn't handle non-finite values.
Results may differ from a plain program's by a relative error of at most 0.0067.
Values may be sent and summed in bfloat16 or wider, within the bound.
No kernel may reach another device: no remote copies, remote signals or barrier semaphores. Data moves between devices by JAX's collectives and lax.ppermute only.
A program may use at most 192 MiB of HBM per device.

v0:
```python
import jax
import jax.numpy as jnp
from jax import lax
from jax.sharding import PartitionSpec as P

HEAD_DIM = 128
STRETCH = 64


norm_eps = 1e-05


def passed_along(value, axis, steps):
    count = lax.axis_size(axis)
    pairs = [(source, (source + steps) % count) for source in range(count)]
    return lax.ppermute(value, axis, pairs)


def slot_ranks(owners):
    count = owners.shape[0]
    positions = jnp.arange(count)
    same_owner = owners[:, None] == owners[None, :]
    earlier = positions[:, None] > positions[None, :]
    return jnp.sum((same_owner & earlier).astype(jnp.int32), axis=1)


def request_table(owners, slot_rank, slot_ids, shards, capacity):
    matched = (owners[:, None, None] == jnp.arange(shards)[None, :, None]) & (
        slot_rank[:, None, None] == jnp.arange(capacity)[None, None, :]
    )
    return jnp.sum(jnp.where(matched, slot_ids[:, None, None] + 1, 0), axis=0) - 1


def local(
    hidden, norm_gain, queries, cache, nbr_shard, nbr_slot, grad_heads, grad_out, query_weight
):
    shards = lax.axis_size("stretch")
    tokens_here = hidden.shape[1]
    qwidth = queries.shape[2]
    head_count = qwidth // HEAD_DIM
    stretches_here = nbr_shard.shape[0]
    neighbours = nbr_shard.shape[1]
    capacity = (neighbours * stretches_here + shards - 1) // shards
    nbr_span = cache.shape[2]
    cache_table = cache[0]
    owners = nbr_shard.reshape(-1)
    slot_ids = nbr_slot.reshape(-1)
    slot_rank = slot_ranks(owners)
    wanted = request_table(owners, slot_rank, slot_ids, shards, capacity)
    picked = cache_table[
        jnp.maximum(lax.all_to_all(wanted, "stretch", split_axis=0, concat_axis=0, tiled=True), 0)
    ]
    fetched = lax.all_to_all(picked, "stretch", split_axis=0, concat_axis=0, tiled=True)
    gathered_rows = fetched[owners, slot_rank].reshape(
        stretches_here, neighbours * nbr_span, 2 * qwidth
    )
    factor = HEAD_DIM ** (-0.5)
    key_heads = gathered_rows[:, :, :qwidth].reshape(
        stretches_here, neighbours * nbr_span, head_count, HEAD_DIM
    )
    value_heads = gathered_rows[:, :, qwidth:].reshape(
        stretches_here, neighbours * nbr_span, head_count, HEAD_DIM
    )
    query_heads = queries[0].reshape(stretches_here, STRETCH, head_count, HEAD_DIM)
    grad_split = grad_heads[0].reshape(stretches_here, STRETCH, head_count, HEAD_DIM)
    scores = (
        jnp.einsum("cqhd,ckhd->chqk", query_heads, key_heads, preferred_element_type=jnp.float32)
        * factor
    )
    row_max = jnp.max(scores, axis=-1, keepdims=True)
    exp_scores = jnp.exp(scores - row_max)
    attn_probs = exp_scores / jnp.sum(exp_scores, axis=-1, keepdims=True)
    dprob = jnp.einsum(
        "cqhd,ckhd->chqk", grad_split, value_heads, preferred_element_type=jnp.float32
    )
    row_inner = jnp.sum(attn_probs * dprob, axis=-1, keepdims=True)
    dscore = (factor * attn_probs * (dprob - row_inner)).astype(jnp.bfloat16)
    query_grad = jnp.einsum(
        "chqk,ckhd->cqhd", dscore, key_heads, preferred_element_type=jnp.float32
    )
    query_grad = query_grad.astype(jnp.bfloat16).reshape(tokens_here, qwidth)
    weight_rows = query_weight[0]
    norm_grad = lax.dot_general(
        query_grad,
        lax.all_gather(weight_rows, "stretch", axis=0, tiled=True),
        (((1,), (1,)), ((), ())),
        preferred_element_type=jnp.float32,
    )
    values_in = hidden[0].astype(jnp.float32)
    inv_rms = lax.rsqrt(jnp.mean(values_in * values_in, axis=-1, keepdims=True) + norm_eps)
    normed = values_in * inv_rms
    scaled_grad = norm_grad * norm_gain[0][None, :]
    mean_term = jnp.mean(scaled_grad * normed, axis=-1, keepdims=True)
    layer_result = grad_out[0].astype(jnp.float32) + inv_rms * (scaled_grad - normed * mean_term)
    outgoing = layer_result.astype(jnp.bfloat16)[None]
    return passed_along(outgoing, "section", -1)


def solution(mesh):
    in_specs = (
        P("section", "stretch", None),
        P("section", None),
        P("section", "stretch", None),
        P("section", "stretch", None, None),
        P("stretch", None),
        P("stretch", None),
        P("section", "stretch", None),
        P("section", "stretch", None),
        P("section", "stretch", None),
    )
    out_specs = P("section", "stretch", None)
    return jax.shard_map(local, mesh=mesh, in_specs=in_specs, out_specs=out_specs, check_vma=False)
```

profile of v0, /device:TPU:14, one launch (start us, length us, event | category | flops | bytes accessed | tf_op | source)
XLA Modules:
  0.0 322.5 jit_solution(963560321363143230)
XLA Ops:
  6.5 0.7 all-gather.3.cloned.1.call-update
  7.3 0.8 copy.52
  8.1 0.7 broadcast_add_fusion
  8.9 0.2 convert_reduce_fusion
  9.3 14.5 %all_to_all.11 = s32[32,1,1]{2,1,0:T(1,128)S(1)} all-to-all(s32[32,1,1]{2,1,0:T(1,128)S(1)} %copy.54), channel_id=1, replica_groups=mesh['stretch'=32,'section'=4] {'stretch'}, dimensions={0} | all-to-all | bytes 256 | tf_op jit(solution)/shard_map/all_to_all | solution.py:51
  23.8 0.7 maximum_reduce_fusion
  24.5 7.2 %gather_fusion = bf16[32,32,4096]{2,1,0:T(8,128)(2,1)} fusion(bf16[16,32,4096]{2,1,0:T(8,128)(2,1)} %bitcast.84, s32[1024]{0:T(1024)S(1)} %pad_clamp_fusion), kind=kCustom, calls=%fused_computation | custom fusion | bytes 16777344 | tf_op jit(solution)/shard_map/gather | solution.py:50
  31.7 6.1 %all-to-all-start.1 = ((bf16[32,1,32,4096]{3,2,1,0:T(8,128)(2,1)}), bf16[32,1,32,4096]{3,2,1,0:T(8,128)(2,1)}, u32[]{:S(2)}, u32[]{:S(2)}) async-start(bf16[32,1,32,4096]{3,2,1,0:T(8,128)(2,1)} %bitcast.83), calls=%async_computation.1 | async-start | bytes 16777216 | tf_op jit(solution)/shard_map/all_to_all | solution.py:53
  37.9 1.9 copy.68
  39.8 2.0 copy.67
  41.8 0.9 fusion.11
  42.7 123.9 %all-to-all-done.1 = bf16[32,1,32,4096]{3,2,1,0:T(8,128)(2,1)} async-done(((bf16[32,1,32,4096]{3,2,1,0:T(8,128)(2,1)}), bf16[32,1,32,4096]{3,2,1,0:T(8,128)(2,1)}, u32[]{:S(2)}, u32[]{:S(2)}) %all-to-all-start.1) | async-done | bytes 8388640 | tf_op jit(solution)/shard_map/all_to_all | solution.py:53
  166.6 6.2 %gather_fusion.1 = bf16[16,32,4096]{2,1,0:T(8,128)(2,1)} fusion(bf16[32,1,32,4096]{3,2,1,0:T(8,128)(2,1)} %all-to-all-done.1, s32[16]{0:T(128)S(1)} %fusion.50), kind=kCustom, calls=%fused_computation.1 | custom fusion | bytes 8388736 | tf_op jit(solution)/shard_map/gather | solution.py:54
  172.9 2.8 slice_bitcast_fusion.1
  175.7 3.2 %fusion.26 = f32[8,16,64,64]{3,2,1,0:T(8,128)} fusion(bf16[8,8,16,8,128]{4,3,2,1,0:T(8,128)(2,1)S(1)} %get-tuple-element.6, bf16[8,64,16,128]{3,2,1,0:T(8,128)(2,1)S(1)} %bitcast.87), kind=kOutput, calls=%fused_computation.31 | convolution fusion | flops 134217728 | bytes 6291456 | tf_op jit(solution)/shard_map/cqhd,ckhd->chqk/dot_general | solution.py:73
  179.0 3.2 fusion.29
  182.1 8.4 %fusion.13 = (f32[8,16,64]{2,1,0:T(8,128)S(1)}, f32[8,16,64,64]{2,3,1,0:T(8,128)}) fusion(f32[8,16,64,64]{3,2,1,0:T(8,128)} %fusion.26, f32[8,16,64,64]{3,2,1,0:T(8,128)} %fusion.29), kind=kOutput, calls=%fused_computation.19 | output fusion | flops 3154046 | bytes 6324224 | tf_op jit(solution)/shard_map/div | solution.py:72
  190.5 4.5 %convert_bitcast_fusion = bf16[8,64,16,128]{3,1,2,0:T(8,128)(2,1)S(1)} fusion(f32[8,16,64,64]{3,2,1,0:T(8,128)} %fusion.26, f32[8,16,64,64]{2,3,1,0:T(8,128)} %get-tuple-element.8, f32[8,16,64]{2,1,0:T(8,128)S(1)} %get-tuple-element.7, bf16[8,8,16,8,128]{4,3,2,1,0:T(8,128)(2,1)S(1)} %get-tuple-element.5), kind=kOutput, calls=%fused_computation.42 | convolution fusion | flops 137363456 | bytes 8421376 | tf_op jit(solution)/shard_map/chqk,ckhd->cqhd/dot_general | solution.py:78
  195.1 2.8 copy.63
  197.8 16.3 %fusion.6 = (f32[512]{0:T(512)S(1)}, f32[512,4096]{1,0:T(8,128)}) fusion(bf16[1,512,4096]{2,1,0:T(8,128)(2,1)} %param.9, f32[4096]{0:T(1024)S(1)} %bitcast.91, f32[512]{0:T(512)S(1)} %add_rsqrt_fusion, bf16[1,4096,2048]{2,1,0:T(8,128)(2,1)} %all-gather.3.cloned.1.call-done, bf16[64,8,16,128]{3,2,1,0:T(8,128)(2,1)} %bitcast.90), kind=kOutput, calls=%fused_computation.10 | convolution fusion | flops 8600420352 | bytes 31477760 | tf_op jit(solution)/shard_map/dot_general | solution.py:83
  214.2 6.3 %fusion.12 = bf16[1,512,4096]{2,1,0:T(8,128)(2,1)S(1)} fusion(f32[512,4096]{1,0:T(8,128)} %get-tuple-element.10, bf16[1,512,4096]{2,1,0:T(8,128)(2,1)} %param.16, bf16[1,512,4096]{2,1,0:T(8,128)(2,1)S(1)} %copy-done.1, f32[512]{0:T(512)S(1)} %broadcast_multiply_fusion, f32[4096]{0:T(1024)S(1)} %bitcast.92, f32[512]{0:T(512)S(1)} %add_rsqrt_fusion), kind=kLoop, calls=%fused_computation.16 | loop fusion | flops 18874368 | bytes 20992000 | tf_op jit(solution)/shard_map/broadcast_in_dim | solution.py:95
  220.5 0.9 collective-permute-start
  221.4 92.2 %collective-permute-done = bf16[1,512,4096]{2,1,0:T(8,128)(2,1)S(1)} collective-permute-done((bf16[1,512,4096]{2,1,0:T(8,128)(2,1)S(1)}, bf16[1,512,4096]{2,1,0:T(8,128)(2,1)S(1)}, u32[]{:S(2)}, u32[]{:S(2)}) %collective-permute-start) | collective-permute-done | bytes 4194336 | tf_op jit(solution)/shard_map/ppermute | solution.py:16
  313.6 2.0 copy.93
  (28 shorter events, 0.7 us)
Async XLA Ops:
  6.5 191.3 %all-gather.3.cloned.1.call-start = ((), (), s32[]{:S(2)}) async-start(), calls=%async_computation.2 | async-start | bytes 17301504 | tf_op jit(solution)/shard_map/all_gather | solution.py:85
  31.7 6.2 %copy-start.4 = (bf16[1,512,2048]{2,1,0:T(8,128)(2,1)S(1)}, bf16[1,512,2048]{2,1,0:T(8,128)(2,1)}, u32[]{:S(2)}) copy-start(bf16[1,512,2048]{2,1,0:T(8,128)(2,1)} %param.15) | copy-start | bytes 6291460
  31.7 135.0 %all-to-all-start.1 = ((bf16[32,1,32,4096]{3,2,1,0:T(8,128)(2,1)}), bf16[32,1,32,4096]{3,2,1,0:T(8,128)(2,1)}, u32[]{:S(2)}, u32[]{:S(2)}) async-start(bf16[32,1,32,4096]{3,2,1,0:T(8,128)(2,1)} %bitcast.83), calls=%async_computation.1 | async-start | bytes 16777216 | tf_op jit(solution)/shard_map/all_to_all | solution.py:53
  37.9 2.0 copy-start.5
  37.9 4.0 %copy-start = (bf16[1,512,4096]{2,1,0:T(8,128)(2,1)S(1)}, bf16[1,512,4096]{2,1,0:T(8,128)(2,1)}, u32[]{:S(2)}) copy-start(bf16[1,512,4096]{2,1,0:T(8,128)(2,1)} %param.9) | copy-start | bytes 12582916
  172.9 2.9 copy-start.3
  175.7 3.2 %copy-start.2 = (bf16[64,8,16,128]{3,2,1,0:T(8,128)(2,1)S(1)}, bf16[64,8,16,128]{3,2,1,0:T(8,128)(2,1)}, u32[]{:S(2)}) copy-start(bf16[64,8,16,128]{3,2,1,0:T(8,128)(2,1)} %copy.67) | copy-start | bytes 6291460
  195.1 2.8 copy-start.6
  197.8 16.4 %copy-start.1 = (bf16[1,512,4096]{2,1,0:T(8,128)(2,1)S(1)}, bf16[1,512,4096]{2,1,0:T(8,128)(2,1)}, u32[]{:S(2)}) copy-start(bf16[1,512,4096]{2,1,0:T(8,128)(2,1)} %param.9) | copy-start | bytes 12582916
  220.5 93.1 %collective-permute-start = (bf16[1,512,4096]{2,1,0:T(8,128)(2,1)S(1)}, bf16[1,512,4096]{2,1,0:T(8,128)(2,1)S(1)}, u32[]{:S(2)}, u32[]{:S(2)}) collective-permute-start(bf16[1,512,4096]{2,1,0:T(8,128)(2,1)S(1)} %fusion.12), channel_id=1, source_target_pairs={{0,3},{1,0},{2,1},{3,2},{4,7},{5,4},{6,5},{7,6},{8,11},{9,8},{10,9... | collective-permute-start | bytes 12582920 | tf_op jit(solution)/shard_map/ppermute | solution.py:16
Sparse Core Ops, SparseCore 0:
  9.6 156.4 all-gather.2
where the time goes:
time: 323 us; the launch traced here: 322 us
  waiting for transfers between devices  217 us (67%)
  matrix products  27.3 us (8%)
  local copies, waits for them, and re-layouts  26.1 us (8%)
  other arithmetic  17.3 us (5%)
  blocking collectives  14.5 us (4%)
  between operations  13.5 us (4%)
  starting transfers between devices  7.01 us (2%)
    all_to_all x1, waiting for transfers between devices, local(): lax.all_to_all(picked, 'stretch', split_axis=0, concat_axis=0, tiled=True)  124 us
    ppermute x1, waiting for transfers between devices, passed_along(): return lax.ppermute(value, axis, pairs)  92.2 us
    dot_general x1, matrix products, local(): lax.dot_general(query_grad, lax.all_gather(weight_rows, 'stretch', axis=0...  16.3 us
    all_to_all x1, blocking collectives, local(): lax.all_to_all(wanted, 'stretch', split_axis=0, concat_axis=0, tiled=True)  14.5 us
    unnamed x19, local copies, waits for them, and re-layouts  9.58 us
    div x1, other arithmetic, local(): attn_probs = exp_scores / jnp.sum(exp_scores, axis=-1, keepdims=True)  8.41 us
    gather x1, local copies, waits for them, and re-layouts, local(): cache_table[jnp.maximum(lax.all_to_all(wanted, 'stretch', split_axis=0, c...  7.17 us
  transfers between devices with their start and end apart: 3, of which 2 were waited for; matrix products, arithmetic and copies ran while one was open for 14% of the time, Pallas kernels for 0%

commit v1 on v0

v1 whole, which is shorter than its diff:
```python
import functools

import jax
import jax.numpy as jnp
from jax import lax
from jax.experimental import pallas as pl
from jax.experimental.pallas import tpu as pltpu
from jax.sharding import PartitionSpec as P

HEAD_DIM = 128
STRETCH = 64
norm_eps = 1e-05
CHUNKS = (8, 4, 4)
DIRECT_ROWS = 192
COLUMNS = 512


def passed_along(value, axis, steps):
    count = lax.axis_size(axis)
    pairs = [(source, (source + steps) % count) for source in range(count)]
    return lax.ppermute(value, axis, pairs)


def pick_kernel(key_at, value_at, width, picks, table, out, sem):
    for place in range(out.shape[0]):
        row = picks[place]
        pltpu.make_async_copy(
            table.at[row, :, pl.ds(key_at, width)], out.at[place, :, pl.ds(0, width)], sem
        ).start()
        pltpu.make_async_copy(
            table.at[row, :, pl.ds(value_at, width)], out.at[place, :, pl.ds(width, width)], sem
        ).start()
    pltpu.make_async_copy(out, out, sem).wait()


def picked_rows(picks, table, first, width, qwidth):
    places = picks.shape[0]
    span = table.shape[1]
    size = places * span * 2 * width
    return pl.pallas_call(
        functools.partial(pick_kernel, first, qwidth + first, width),
        out_shape=jax.ShapeDtypeStruct((places, span, 2 * width), table.dtype),
        grid_spec=pltpu.PrefetchScalarGridSpec(
            num_scalar_prefetch=1,
            grid=(1,),
            in_specs=[pl.BlockSpec(memory_space=pl.ANY)],
            out_specs=pl.BlockSpec(memory_space=pl.ANY),
            scratch_shapes=[pltpu.SemaphoreType.DMA],
        ),
        cost_estimate=pl.CostEstimate(flops=0, transcendentals=0, bytes_accessed=4 * size),
        name="pick_rows",
    )(picks, table)


def attention_kernel(heads, owners, first, second, query, grad, out):
    factor = HEAD_DIM ** (-0.5)
    width = heads * HEAD_DIM
    for head in range(heads):
        cols = slice(head * HEAD_DIM, (head + 1) * HEAD_DIM)
        vcols = slice(width + head * HEAD_DIM, width + (head + 1) * HEAD_DIM)
        keys = jnp.concatenate([first[0, :, cols], second[0, :, cols]], axis=0)
        values = jnp.concatenate([first[0, :, vcols], second[0, :, vcols]], axis=0)
        across = (((1,), (1,)), ((), ()))
        scores = (
            lax.dot_general(query[:, cols], keys, across, preferred_element_type=jnp.float32)
            * factor
        )
        dprob = lax.dot_general(
            grad[:, cols], values, across, preferred_element_type=jnp.float32
        )
        exp_scores = jnp.exp(scores - jnp.max(scores, axis=-1, keepdims=True))
        probs = exp_scores / jnp.sum(exp_scores, axis=-1, keepdims=True)
        inner = jnp.sum(probs * dprob, axis=-1, keepdims=True)
        dscore = (factor * probs * (dprob - inner)).astype(jnp.bfloat16)
        out[:, cols] = jnp.dot(dscore, keys, preferred_element_type=jnp.float32).astype(
            jnp.bfloat16
        )


def query_gradient(owners, fetched, queries, grads, first, heads):
    width = heads * HEAD_DIM
    tokens = queries.shape[0]
    stretches = tokens // STRETCH
    span = fetched.shape[1]
    block = first // width
    return pl.pallas_call(
        functools.partial(attention_kernel, heads),
        out_shape=jax.ShapeDtypeStruct((tokens, width), jnp.bfloat16),
        grid_spec=pltpu.PrefetchScalarGridSpec(
            num_scalar_prefetch=1,
            grid=(stretches,),
            in_specs=[
                pl.BlockSpec((1, span, 2 * width), lambda c, own: (own[2 * c], 0, 0)),
                pl.BlockSpec((1, span, 2 * width), lambda c, own: (own[2 * c + 1], 0, 0)),
                pl.BlockSpec((STRETCH, width), lambda c, own: (c, block)),
                pl.BlockSpec((STRETCH, width), lambda c, own: (c, block)),
            ],
            out_specs=pl.BlockSpec((STRETCH, width), lambda c, own: (c, 0)),
        ),
        cost_estimate=pl.CostEstimate(
            flops=6 * tokens * STRETCH * width,
            transcendentals=tokens * STRETCH * heads,
            bytes_accessed=2 * (3 * tokens * width + 2 * stretches * span * 2 * width),
        ),
        name="query_gradient",
    )(owners, fetched, fetched, queries, grads)


def finish_kernel(widths, near, blocks, *refs):
    parts = refs[: len(widths)]
    weight, gain, hidden_near, hidden_far, grad_out, out, scaled, dots, squares = refs[len(widths) :]
    phase, block = pl.program_id(0), pl.program_id(1)
    model = blocks * COLUMNS

    @pl.when(phase == 0)
    def _():
        total = None
        start = 0
        for part, width in zip(parts, widths):
            product = lax.dot_general(
                part[...],
                weight[:, start : start + width],
                (((1,), (1,)), ((), ())),
                preferred_element_type=jnp.float32,
            )
            total = product if total is None else total + product
            start += width
        grad = total * gain[...]
        scaled[block] = grad
        for ref, rows in ((hidden_near, slice(0, near)), (hidden_far, slice(near, None))):
            values = ref[...].astype(jnp.float32)
            cross = grad[rows] * values
            square = values * values
            dot = cross[:, :128]
            norm = square[:, :128]
            for lane in range(128, COLUMNS, 128):
                dot = dot + cross[:, lane : lane + 128]
                norm = norm + square[:, lane : lane + 128]
            size = values.shape[0]
            at = pl.ds(rows.start, size)

            @pl.when(block == 0)
            def _():
                dots[at, :] = dot
                squares[at, :] = norm

            @pl.when(block > 0)
            def _():
                dots[at, :] += dot
                squares[at, :] += norm

    @pl.when((phase == 1) & (block == 0))
    def _():
        inv = lax.rsqrt(jnp.sum(squares[...], axis=-1, keepdims=True) / model + norm_eps)
        mean = inv * jnp.sum(dots[...], axis=-1, keepdims=True) / model
        squares[...] = jnp.broadcast_to(inv, squares.shape)
        dots[...] = jnp.broadcast_to(inv * inv * mean, dots.shape)

    @pl.when(phase == 1)
    def _():
        grad = scaled[block]
        for ref, rows in ((hidden_near, slice(0, near)), (hidden_far, slice(near, None))):
            size = ref.shape[0]
            at = pl.ds(rows.start, size)
            inv = squares[at, :1]
            pull = dots[at, :1]
            out[at, :] = (
                grad_out[at, :].astype(jnp.float32)
                + inv * grad[rows]
                - pull * ref[...].astype(jnp.float32)
            ).astype(out.dtype)


def finished(parts, weight, gain, hidden_near, hidden_far, grad_out):
    tokens, model = grad_out.shape
    near, far = hidden_near.shape[0], hidden_far.shape[0]
    widths = tuple(part.shape[1] for part in parts)
    blocks = model // COLUMNS

    def early(phase, block):
        return jnp.where(phase == 0, block, blocks - 1)

    def late(phase, block):
        return jnp.where(phase == 0, 0, block)

    whole = [pl.BlockSpec((tokens, width), lambda p, b: (0, 0)) for width in widths]
    return pl.pallas_call(
        functools.partial(finish_kernel, widths, near, blocks),
        out_shape=jax.ShapeDtypeStruct((tokens, model), jnp.bfloat16),
        grid=(2, blocks),
        in_specs=whole
        + [
            pl.BlockSpec((COLUMNS, weight.shape[1]), lambda p, b: (early(p, b), 0)),
            pl.BlockSpec((1, COLUMNS), lambda p, b: (0, early(p, b))),
            pl.BlockSpec((near, COLUMNS), lambda p, b: (0, b)),
            pl.BlockSpec((far, COLUMNS), lambda p, b: (0, b)),
            pl.BlockSpec((tokens, COLUMNS), lambda p, b: (0, late(p, b))),
        ],
        out_specs=pl.BlockSpec((tokens, COLUMNS), lambda p, b: (0, late(p, b))),
        scratch_shapes=[
            pltpu.VMEM((blocks, tokens, COLUMNS), jnp.float32),
            pltpu.VMEM((tokens, 128), jnp.float32),
            pltpu.VMEM((tokens, 128), jnp.float32),
        ],
        compiler_params=pltpu.CompilerParams(vmem_limit_bytes=40 << 20),
        cost_estimate=pl.CostEstimate(
            flops=2 * tokens * model * weight.shape[1],
            transcendentals=0,
            bytes_accessed=2 * (model * weight.shape[1] + 4 * tokens * model),
        ),
        name="finish",
    )(*parts, weight, gain, hidden_near, hidden_far, grad_out)


def local(
    hidden, norm_gain, queries, cache, nbr_shard, nbr_slot, grad_heads, grad_out, query_weight
):
    shards = lax.axis_size("stretch")
    qwidth = queries.shape[2]
    weight_here = passed_along(query_weight[0], "section", -1)
    gain = passed_along(norm_gain, "section", -1)
    far = hidden[0, DIRECT_ROWS:]
    for _ in range(lax.axis_size("section") - 1):
        far = passed_along(far, "section", 1)
    near = passed_along(hidden[0, :DIRECT_ROWS], "section", -1)
    grads = passed_along(grad_out[0], "section", -1)

    owners = nbr_shard.reshape(-1)
    asked = owners[:, None] == jnp.arange(shards)[None, :]
    wanted = jnp.sum(jnp.where(asked, nbr_slot.reshape(-1)[:, None], 0), axis=0)
    picks = lax.all_to_all(wanted, "stretch", split_axis=0, concat_axis=0, tiled=True)
    weight_here, picks = lax.optimization_barrier((weight_here, picks))
    weight = lax.all_gather(weight_here, "stretch", axis=0, tiled=True)

    parts = []
    first_head = 0
    for heads in CHUNKS:
        first, width = first_head * HEAD_DIM, heads * HEAD_DIM
        first_head += heads
        rows = picked_rows(picks, cache[0], first, width, qwidth)
        fetched = lax.all_to_all(rows, "stretch", split_axis=0, concat_axis=0, tiled=True)
        part = query_gradient(owners, fetched, queries[0], grad_heads[0], first, heads)
        parts.append(passed_along(part, "section", -1))
    return finished(parts, weight, gain, near, far, grads)[None]


def solution(mesh):
    in_specs = (
        P("section", "stretch", None),
        P("section", None),
        P("section", "stretch", None),
        P("section", "stretch", None, None),
        P("stretch", None),
        P("stretch", None),
        P("section", "stretch", None),
        P("section", "stretch", None),
        P("section", "stretch", None),
    )
    out_specs = P("section", "stretch", None)
    return jax.shard_map(local, mesh=mesh, in_specs=in_specs, out_specs=out_specs, check_vma=False)
```

time: 323 us -> 449 us (1.39)
  Pallas kernels: 0 us -> 323 us
  waiting for transfers between devices: 217 us -> 54.1 us
  matrix products: 27.3 us -> 0 us
  starting transfers between devices: 7.01 us -> 29 us
  other arithmetic: 17.3 us -> 1.29 us
  local copies, waits for them, and re-layouts: 26.1 us -> 12 us
    pallas_call x0 -> x7, Pallas kernels: none -> 323 us  [the longest x3 259 us: picked_rows(): pl.pallas_call(functools.partial(pick_kernel, first, qwidth + first, widt...]
    all_to_all x1 -> x3, waiting for transfers between devices: 124 us -> 0.01 us  [local(): lax.all_to_all(rows, 'stretch', split_axis=0, concat_axis=0, tiled=True)]
    ppermute x1 -> x10, waiting for transfers between devices: 92.2 us -> 54 us  [passed_along(): return lax.ppermute(value, axis, pairs)]
    dot_general x4 -> x0, matrix products: 27.3 us -> none  [the longest x1 16.3 us: local(): lax.dot_general(query_grad, lax.all_gather(weight_rows, 'stretch', axis=0...]
    all_to_all x1 -> x3, starting transfers between devices: 6.12 us -> 20.3 us  [local(): lax.all_to_all(rows, 'stretch', split_axis=0, concat_axis=0, tiled=True)]
    gather x2 -> x0, local copies, waits for them, and re-layouts: 13.4 us -> none  [the longest x1 7.17 us: local(): cache_table[jnp.maximum(lax.all_to_all(wanted, 'stretch', split_axis=0, c...]
    div x2 -> x0, other arithmetic: 8.42 us -> none  [the longest x1 8.41 us: local(): attn_probs = exp_scores / jnp.sum(exp_scores, axis=-1, keepdims=True)]
    ppermute x1 -> x10, starting transfers between devices: 0.89 us -> 8.72 us  [passed_along(): return lax.ppermute(value, axis, pairs)]
  transfers between devices with their start and end apart: 3 -> 14, of which waited for: 2 -> 3; matrix products, arithmetic and copies ran while one was open for 14% -> 2% of each run, Pallas kernels for 0% -> 67%
where the time goes in v1:
time: 449 us; the launch traced here: 448 us
  Pallas kernels  323 us (72%)
  waiting for transfers between devices  54.1 us (12%)
  starting transfers between devices  29 us (6%)
  blocking collectives  14.5 us (3%)
  between operations  13.5 us (3%)
  local copies, waits for them, and re-layouts  12 us (3%)
    pallas_call x3, Pallas kernels, picked_rows(): pl.pallas_call(functools.partial(pick_kernel, first, qwidth + first, widt...  259 us
    ppermute x10, waiting for transfers between devices, passed_along(): return lax.ppermute(value, axis, pairs)  54 us
    pallas_call x3, Pallas kernels, query_gradient(): pl.pallas_call(functools.partial(attention_kernel, heads), out_shape=jax....  41.5 us
    pallas_call x1, Pallas kernels, finished(): pl.pallas_call(functools.partial(finish_kernel, widths, near, blocks), ou...  22.4 us
    all_to_all x3, starting transfers between devices, local(): lax.all_to_all(rows, 'stretch', split_axis=0, concat_axis=0, tiled=True)  20.3 us
    all_to_all x1, blocking collectives, local(): lax.all_to_all(wanted, 'stretch', split_axis=0, concat_axis=0, tiled=True)  14.5 us
  transfers between devices with their start and end apart: 14, of which 3 were waited for; matrix products, arithmetic and copies ran while one was open for 2% of the time, Pallas kernels for 67%

profile of v1, /device:TPU:14, one launch (start us, length us, event | category | flops | bytes accessed | tf_op | source)
XLA Modules:
  0.0 447.7 jit_solution(12010609505030820681)
XLA Ops:
  6.5 0.8 collective-permute-start
  9.2 14.5 %all_to_all.27 = s32[32,1,1]{2,1,0:T(1,128)S(1)} all-to-all(s32[32,1,1]{2,1,0:T(1,128)S(1)} %copy.22), channel_id=1, replica_groups=mesh['stretch'=32,'section'=4] {'stretch'}, dimensions={0} | all-to-all | bytes 256 | tf_op jit(solution)/shard_map/all_to_all | solution.py:231
  23.7 1.2 reduce.picks
  24.9 0.8 copy-done.3
  25.8 65.3 %pick_rows.5 = bf16[32,32,1024]{2,1,0:T(8,128)(2,1)} custom-call(s32[32]{0:T(128)} %reduce.picks, bf16[16,32,4096]{2,1,0:T(8,128)(2,1)} %bitcast.11), custom_call_target="tpu_custom_call" | custom-call | bytes 4194304 | tf_op jit(solution)/shard_map/pick_rows/pallas_call | solution.py:40
  91.1 5.3 %all-to-all-start.3 = ((bf16[32,32,1024]{2,1,0:T(8,128)(2,1)}), bf16[32,32,1024]{2,1,0:T(8,128)(2,1)S(1)}, u32[]{:S(2)}, u32[]{:S(2)}) async-start(bf16[32,32,1024]{2,1,0:T(8,128)(2,1)} %pick_rows.5), calls=%async_computation.3 | async-start | bytes 4194304 | tf_op jit(solution)/shard_map/all_to_all | solution.py:241
  96.4 3.6 slice_bitcast_fusion
  100.0 2.3 collective-permute-start.6
  102.2 128.8 %pick_rows.3 = bf16[32,32,2048]{2,1,0:T(8,128)(2,1)} custom-call(s32[32]{0:T(128)} %reduce.picks, bf16[16,32,4096]{2,1,0:T(8,128)(2,1)} %bitcast.12), custom_call_target="tpu_custom_call" | custom-call | bytes 8388608 | tf_op jit(solution)/shard_map/pick_rows/pallas_call | solution.py:40
  231.1 1.3 copy-done.2
  232.4 7.5 %all-to-all-start.1 = ((bf16[32,32,2048]{2,1,0:T(8,128)(2,1)}), bf16[32,32,2048]{2,1,0:T(8,128)(2,1)}, u32[]{:S(2)}, u32[]{:S(2)}) async-start(bf16[32,32,2048]{2,1,0:T(8,128)(2,1)} %pick_rows.3), calls=%async_computation.1 | async-start | bytes 8388608 | tf_op jit(solution)/shard_map/all_to_all | solution.py:241
  240.0 2.0 collective-permute-start.9
  242.0 65.3 %pick_rows.4 = bf16[32,32,1024]{2,1,0:T(8,128)(2,1)} custom-call(s32[32]{0:T(128)} %reduce.picks, bf16[16,32,4096]{2,1,0:T(8,128)(2,1)} %bitcast.13), custom_call_target="tpu_custom_call" | custom-call | bytes 4194304 | tf_op jit(solution)/shard_map/pick_rows/pallas_call | solution.py:40
  307.4 1.4 collective-permute-start.8
  308.7 7.4 %all-to-all-start.2 = ((bf16[32,32,1024]{2,1,0:T(8,128)(2,1)}), bf16[32,32,1024]{2,1,0:T(8,128)(2,1)}, u32[]{:S(2)}, u32[]{:S(2)}) async-start(bf16[32,32,1024]{2,1,0:T(8,128)(2,1)} %pick_rows.4), calls=%async_computation.2 | async-start | bytes 4194304 | tf_op jit(solution)/shard_map/all_to_all | solution.py:241
  316.2 2.7 slice_bitcast_fusion.1
  319.6 18.6 %query_gradient.3 = bf16[512,1024]{1,0:T(8,128)(2,1)} custom-call(s32[16]{0:T(128)} %copy-done.4, bf16[32,32,2048]{2,1,0:T(8,128)(2,1)} %all-to-all-done.1.first.second, bf16[32,32,2048]{2,1,0:T(8,128)(2,1)} %all-to-all-done.1.first.second, bf16[512,2048]{1,0:T(8,128)(2,1)} %bitcast.14, bf16[512,2048]{1,0:T(8,128)(2,1)} %bitcast.17), custom_call_target="tpu_custom_call" | custom-call | flops 201326592 | bytes 5242880 | tf_op jit(solution)/shard_map/query_gradient/pallas_call | solution.py:86
  338.9 11.4 %query_gradient.5 = bf16[512,512]{1,0:T(8,128)(2,1)} custom-call(s32[16]{0:T(128)} %copy-done.4, bf16[32,32,1024]{2,1,0:T(8,128)(2,1)} %copy-done.2, bf16[32,32,1024]{2,1,0:T(8,128)(2,1)} %copy-done.2, bf16[512,2048]{1,0:T(8,128)(2,1)} %bitcast.15, bf16[512,2048]{1,0:T(8,128)(2,1)} %bitcast.18), custom_call_target="tpu_custom_call" | custom-call | flops 100663296 | bytes 2621440 | tf_op jit(solution)/shard_map/query_gradient/pallas_call | solution.py:86
  350.4 11.4 %query_gradient.4 = bf16[512,512]{1,0:T(8,128)(2,1)} custom-call(s32[16]{0:T(128)} %copy-done.4, bf16[32,32,1024]{2,1,0:T(8,128)(2,1)} %all-to-all-done.2.first.second, bf16[32,32,1024]{2,1,0:T(8,128)(2,1)} %all-to-all-done.2.first.second, bf16[512,2048]{1,0:T(8,128)(2,1)} %bitcast.16, bf16[512,2048]{1,0:T(8,128)(2,1)} %bitcast.19), custom_call_target="tpu_custom_call" | custom-call | flops 100663296 | bytes 2621440 | tf_op jit(solution)/shard_map/query_gradient/pallas_call | solution.py:86
  361.8 28.8 %collective-permute-done.4.refs_4_ = f32[1,4096]{1,0:T(1,128)S(1)} collective-permute-done((f32[1,4096]{1,0:T(1,128)S(1)}, f32[1,4096]{1,0:T(1,128)S(1)}, u32[]{:S(2)}, u32[]{:S(2)}) %collective-permute-start.4) | collective-permute-done | bytes 16416 | tf_op jit(solution)/shard_map/ppermute | solution.py:21
  391.4 15.5 %collective-permute-done.3.refs_2_ = bf16[512,512]{1,0:T(8,128)(2,1)S(1)} collective-permute-done((bf16[512,512]{1,0:T(8,128)(2,1)}, bf16[512,512]{1,0:T(8,128)(2,1)S(1)}, u32[]{:S(2)}, u32[]{:S(2)}) %collective-permute-start.3) | collective-permute-done | bytes 524320 | tf_op jit(solution)/shard_map/ppermute | solution.py:21
  406.9 9.6 %collective-permute-done.2.refs_1_ = bf16[512,512]{1,0:T(8,128)(2,1)S(1)} collective-permute-done((bf16[512,512]{1,0:T(8,128)(2,1)}, bf16[512,512]{1,0:T(8,128)(2,1)S(1)}, u32[]{:S(2)}, u32[]{:S(2)}) %collective-permute-start.2) | collective-permute-done | bytes 524320 | tf_op jit(solution)/shard_map/ppermute | solution.py:21
  417.4 1.0 copy-done.1
  418.5 22.4 %finish.1 = bf16[512,4096]{1,0:T(8,128)(2,1)} custom-call(bf16[512,1024]{1,0:T(8,128)(2,1)} %collective-permute-done.1.refs_0_, bf16[512,512]{1,0:T(8,128)(2,1)S(1)} %copy-done.1, bf16[512,512]{1,0:T(8,128)(2,1)S(1)} %collective-permute-done.3.refs_2_, bf16[4096,2048]{1,0:T(8,128)(2,1)} %all-gather.2.cloned.1.call-done.refs_3_, ...), custom_call_target="tpu_custom_call" | custom-call | flops 8589934592 | bytes 33554432 | tf_op jit(solution)/shard_map/finish/pallas_call | solution.py:187
  (34 shorter events, 5.0 us)
Async XLA Ops:
  6.5 410.9 %all-gather.2.cloned.1.call-start = ((), (), s32[]{:S(2)}) async-start(), calls=%async_computation.4 | async-start | bytes 17301504 | tf_op jit(solution)/shard_map/all_gather | solution.py:233
  6.5 18.4 %collective-permute-start = (bf16[128,2048]{1,0:T(8,128)(2,1)}, bf16[128,2048]{1,0:T(8,128)(2,1)S(1)}, u32[]{:S(2)}, u32[]{:S(2)}) collective-permute-start(bf16[128,2048]{1,0:T(8,128)(2,1)} %bitcast.22), channel_id=1, source_target_pairs={{0,3},{1,0},{2,1},{3,2},{4,7},{5,4},{6,5},{7,6},{8,11},{9,8},{10,9... | collective-permute-start | bytes 1572872 | tf_op jit(solution)/shard_map/ppermute | solution.py:21
  8.2 82.9 %copy-start.4 = (s32[16]{0:T(128)}, s32[16]{0:T(128)S(1)}, u32[]{:S(2)}) copy-start(s32[16]{0:T(128)S(1)} %reshape.7.owners) | copy-start | bytes 196
  24.9 0.8 copy-start.3
  91.1 140.0 %all-to-all-start.3 = ((bf16[32,32,1024]{2,1,0:T(8,128)(2,1)}), bf16[32,32,1024]{2,1,0:T(8,128)(2,1)S(1)}, u32[]{:S(2)}, u32[]{:S(2)}) async-start(bf16[32,32,1024]{2,1,0:T(8,128)(2,1)} %pick_rows.5), calls=%async_computation.3 | async-start | bytes 4194304 | tf_op jit(solution)/shard_map/all_to_all | solution.py:241
  100.0 140.0 %collective-permute-start.6 = (bf16[320,4096]{1,0:T(8,128)(2,1)}, bf16[320,4096]{1,0:T(8,128)(2,1)}, u32[]{:S(2)}, u32[]{:S(2)}) collective-permute-start(bf16[320,4096]{1,0:T(8,128)(2,1)} %slice_bitcast_fusion), channel_id=1, source_target_pairs={{0,1},{1,2},{2,3},{3,0},{4,5},{5,6},{6,7},{7,4},{8,9},{9,10},{10,1... | collective-permute-start | bytes 7864328 | tf_op jit(solution)/shard_map/ppermute | solution.py:21
  231.1 1.3 copy-start.2
  232.4 76.3 %all-to-all-start.1 = ((bf16[32,32,2048]{2,1,0:T(8,128)(2,1)}), bf16[32,32,2048]{2,1,0:T(8,128)(2,1)}, u32[]{:S(2)}, u32[]{:S(2)}) async-start(bf16[32,32,2048]{2,1,0:T(8,128)(2,1)} %pick_rows.3), calls=%async_computation.1 | async-start | bytes 8388608 | tf_op jit(solution)/shard_map/all_to_all | solution.py:241
  239.9 67.4 %collective-permute-start.7 = (bf16[320,4096]{1,0:T(8,128)(2,1)}, bf16[320,4096]{1,0:T(8,128)(2,1)}, u32[]{:S(2)}, u32[]{:S(2)}) collective-permute-start(bf16[320,4096]{1,0:T(8,128)(2,1)} %collective-permute-done.6), channel_id=1, source_target_pairs={{0,1},{1,2},{2,3},{3,0},{4,5},{5,6},{6,7},{7,4},{8,9},{9,10},{10,1... | collective-permute-start | bytes 7864328 | tf_op jit(solution)/shard_map/ppermute | solution.py:21
  240.0 177.4 %collective-permute-start.9 = (bf16[512,4096]{1,0:T(8,128)(2,1)}, bf16[512,4096]{1,0:T(8,128)(2,1)}, u32[]{:S(2)}, u32[]{:S(2)}) collective-permute-start(bf16[512,4096]{1,0:T(8,128)(2,1)} %bitcast.21), channel_id=1, source_target_pairs={{0,3},{1,0},{2,1},{3,2},{4,7},{5,4},{6,5},{7,6},{8,11},{9,8},{10,9... | collective-permute-start | bytes 12582920 | tf_op jit(solution)/shard_map/ppermute | solution.py:21
  307.4 110.0 %collective-permute-start.8 = (bf16[320,4096]{1,0:T(8,128)(2,1)}, bf16[320,4096]{1,0:T(8,128)(2,1)S(1)}, u32[]{:S(2)}, u32[]{:S(2)}) collective-permute-start(bf16[320,4096]{1,0:T(8,128)(2,1)} %collective-permute-done.7), channel_id=1, source_target_pairs={{0,1},{1,2},{2,3},{3,0},{4,5},{5,6},{6,7},{7,4},{8,9},{9,10},{10,1... | collective-permute-start | bytes 7864328 | tf_op jit(solution)/shard_map/ppermute | solution.py:21
  308.7 41.7 %all-to-all-start.2 = ((bf16[32,32,1024]{2,1,0:T(8,128)(2,1)}), bf16[32,32,1024]{2,1,0:T(8,128)(2,1)}, u32[]{:S(2)}, u32[]{:S(2)}) async-start(bf16[32,32,1024]{2,1,0:T(8,128)(2,1)} %pick_rows.4), calls=%async_computation.2 | async-start | bytes 4194304 | tf_op jit(solution)/shard_map/all_to_all | solution.py:241
  318.9 72.3 %collective-permute-start.5 = (bf16[192,4096]{1,0:T(8,128)(2,1)}, bf16[192,4096]{1,0:T(8,128)(2,1)}, u32[]{:S(2)}, u32[]{:S(2)}) collective-permute-start(bf16[192,4096]{1,0:T(8,128)(2,1)} %slice_bitcast_fusion.1), channel_id=1, source_target_pairs={{0,3},{1,0},{2,1},{3,2},{4,7},{5,4},{6,5},{7,6},{8,11},{9,8},{10,9... | collective-permute-start | bytes 4718600 | tf_op jit(solution)/shard_map/ppermute | solution.py:21
  319.6 18.6 %copy-start.5 = (f32[1,4096]{1,0:T(1,128)S(1)}, f32[1,4096]{1,0:T(1,128)}, u32[]{:S(2)}) copy-start(f32[1,4096]{1,0:T(1,128)} %param.10) | copy-start | bytes 49156
  338.2 79.2 %collective-permute-start.1 = (bf16[512,1024]{1,0:T(8,128)(2,1)}, bf16[512,1024]{1,0:T(8,128)(2,1)}, u32[]{:S(2)}, u32[]{:S(2)}) collective-permute-start(bf16[512,1024]{1,0:T(8,128)(2,1)} %query_gradient.3), channel_id=1, source_target_pairs={{0,3},{1,0},{2,1},{3,2},{4,7},{5,4},{6,5},{7,6},{8,11},{9,8},{10,9... | collective-permute-start | bytes 3145736 | tf_op jit(solution)/shard_map/ppermute | solution.py:21
  338.2 52.5 %collective-permute-start.4 = (f32[1,4096]{1,0:T(1,128)S(1)}, f32[1,4096]{1,0:T(1,128)S(1)}, u32[]{:S(2)}, u32[]{:S(2)}) collective-permute-start(f32[1,4096]{1,0:T(1,128)S(1)} %copy-done.5), channel_id=1, source_target_pairs={{0,3},{1,0},{2,1},{3,2},{4,7},{5,4},{6,5},{7,6},{8,11},{9,8},{10,9... | collective-permute-start | bytes 49160 | tf_op jit(solution)/shard_map/ppermute | solution.py:21
  390.7 16.3 %collective-permute-start.3 = (bf16[512,512]{1,0:T(8,128)(2,1)}, bf16[512,512]{1,0:T(8,128)(2,1)S(1)}, u32[]{:S(2)}, u32[]{:S(2)}) collective-permute-start(bf16[512,512]{1,0:T(8,128)(2,1)} %query_gradient.5), channel_id=1, source_target_pairs={{0,3},{1,0},{2,1},{3,2},{4,7},{5,4},{6,5},{7,6},{8,11},{9,8},{10,9... | collective-permute-start | bytes 1572872 | tf_op jit(solution)/shard_map/ppermute | solution.py:21
  391.1 25.5 %collective-permute-start.2 = (bf16[512,512]{1,0:T(8,128)(2,1)}, bf16[512,512]{1,0:T(8,128)(2,1)S(1)}, u32[]{:S(2)}, u32[]{:S(2)}) collective-permute-start(bf16[512,512]{1,0:T(8,128)(2,1)} %query_gradient.4), channel_id=1, source_target_pairs={{0,3},{1,0},{2,1},{3,2},{4,7},{5,4},{6,5},{7,6},{8,11},{9,8},{10,9... | collective-permute-start | bytes 1572872 | tf_op jit(solution)/shard_map/ppermute | solution.py:21
  416.6 0.8 copy-start
  417.4 1.0 copy-start.1
Sparse Core Ops, SparseCore 0:
  25.9 71.2 all-gather.1

commit v2 on v1

--- a/solution.py
+++ b/solution.py
@@ -21,22 +21,32 @@
     return lax.ppermute(value, axis, pairs)
 
 
-def pick_kernel(key_at, value_at, width, picks, table, out, sem):
-    for place in range(out.shape[0]):
+def pick_kernel(key_at, value_at, width, picks, table, out, rows, arrived, left):
+    groups = arrived.shape[0]
+    per = rows.shape[0] // groups
+    for place in range(rows.shape[0]):
         row = picks[place]
-        pltpu.make_async_copy(
-            table.at[row, :, pl.ds(key_at, width)], out.at[place, :, pl.ds(0, width)], sem
-        ).start()
-        pltpu.make_async_copy(
-            table.at[row, :, pl.ds(value_at, width)], out.at[place, :, pl.ds(width, width)], sem
-        ).start()
-    pltpu.make_async_copy(out, out, sem).wait()
+        for start, at in ((key_at, 0), (value_at, width)):
+            pltpu.make_async_copy(
+                table.at[row, :, pl.ds(start, width)],
+                rows.at[place, :, pl.ds(at, width)],
+                arrived.at[place // per],
+            ).start()
+    moves = []
+    for group in range(groups):
+        slab = pl.ds(group * per, per)
+        pltpu.make_async_copy(rows.at[slab], rows.at[slab], arrived.at[group]).wait()
+        moves.append(pltpu.make_async_copy(rows.at[slab], out.at[slab], left.at[group]))
+        moves[-1].start()
+    for move in moves:
+        move.wait()
 
 
 def picked_rows(picks, table, first, width, qwidth):
     places = picks.shape[0]
     span = table.shape[1]
     size = places * span * 2 * width
+    groups = 4
     return pl.pallas_call(
         functools.partial(pick_kernel, first, qwidth + first, width),
         out_shape=jax.ShapeDtypeStruct((places, span, 2 * width), table.dtype),
@@ -45,34 +55,48 @@
             grid=(1,),
             in_specs=[pl.BlockSpec(memory_space=pl.ANY)],
             out_specs=pl.BlockSpec(memory_space=pl.ANY),
-            scratch_shapes=[pltpu.SemaphoreType.DMA],
+            scratch_shapes=[
+                pltpu.VMEM((places, span, 2 * width), table.dtype),
+                pltpu.SemaphoreType.DMA((groups,)),
+                pltpu.SemaphoreType.DMA((groups,)),
+            ],
         ),
         cost_estimate=pl.CostEstimate(flops=0, transcendentals=0, bytes_accessed=4 * size),
         name="pick_rows",
     )(picks, table)
 
 
+def side_by_side(block, left):
+    right = left + HEAD_DIM
+    zeros = jnp.zeros((STRETCH, HEAD_DIM), block.dtype)
+    above = jnp.concatenate([block[:, left:right], zeros], axis=1)
+    below = jnp.concatenate([zeros, block[:, right : right + HEAD_DIM]], axis=1)
+    return jnp.concatenate([above, below], axis=0)
+
+
 def attention_kernel(heads, owners, first, second, query, grad, out):
     factor = HEAD_DIM ** (-0.5)
     width = heads * HEAD_DIM
-    for head in range(heads):
-        cols = slice(head * HEAD_DIM, (head + 1) * HEAD_DIM)
-        vcols = slice(width + head * HEAD_DIM, width + (head + 1) * HEAD_DIM)
+    across = (((1,), (1,)), ((), ()))
+    down = (((0,), (0,)), ((), ()))
+    for left in range(0, width, 2 * HEAD_DIM):
+        cols = slice(left, left + 2 * HEAD_DIM)
+        vcols = slice(width + left, width + left + 2 * HEAD_DIM)
         keys = jnp.concatenate([first[0, :, cols], second[0, :, cols]], axis=0)
         values = jnp.concatenate([first[0, :, vcols], second[0, :, vcols]], axis=0)
-        across = (((1,), (1,)), ((), ()))
-        scores = (
-            lax.dot_general(query[:, cols], keys, across, preferred_element_type=jnp.float32)
-            * factor
+        scores = lax.dot_general(
+            keys, side_by_side(query, left), across, preferred_element_type=jnp.float32
         )
         dprob = lax.dot_general(
-            grad[:, cols], values, across, preferred_element_type=jnp.float32
+            values, side_by_side(grad, left), across, preferred_element_type=jnp.float32
         )
-        exp_scores = jnp.exp(scores - jnp.max(scores, axis=-1, keepdims=True))
-        probs = exp_scores / jnp.sum(exp_scores, axis=-1, keepdims=True)
-        inner = jnp.sum(probs * dprob, axis=-1, keepdims=True)
-        dscore = (factor * probs * (dprob - inner)).astype(jnp.bfloat16)
-        out[:, cols] = jnp.dot(dscore, keys, preferred_element_type=jnp.float32).astype(
+        exp_scores = jnp.exp((scores - jnp.max(scores, axis=0, keepdims=True)) * factor)
+        share = 1.0 / jnp.sum(exp_scores, axis=0, keepdims=True)
+        inner = jnp.sum(exp_scores * dprob, axis=0, keepdims=True) * share
+        dscore = (exp_scores * (dprob - inner) * (share * factor)).astype(jnp.bfloat16)
+        both = lax.dot_general(dscore, keys, down, preferred_element_type=jnp.float32)
+        out[:, left : left + HEAD_DIM] = both[:STRETCH, :HEAD_DIM].astype(jnp.bfloat16)
+        out[:, left + HEAD_DIM : left + 2 * HEAD_DIM] = both[STRETCH:, HEAD_DIM:].astype(
             jnp.bfloat16
         )
 

time: 449 us -> 309 us (0.69)
  Pallas kernels: 323 us -> 63.7 us
  waiting for transfers between devices: 54.1 us -> 172 us
    pallas_call x3, Pallas kernels: 259 us -> 12.5 us  [picked_rows(): pl.pallas_call(functools.partial(pick_kernel, first, qwidth + first, widt...]
    ppermute x10, waiting for transfers between devices: 54 us -> 143 us  [passed_along(): return lax.ppermute(value, axis, pairs)]
    all_to_all x3, waiting for transfers between devices: 0.01 us -> 29 us  [local(): lax.all_to_all(rows, 'stretch', split_axis=0, concat_axis=0, tiled=True)]
    pallas_call x3, Pallas kernels: 41.5 us -> 28.7 us  [query_gradient(): pl.pallas_call(functools.partial(attention_kernel, heads), out_shape=jax....]
  transfers between devices with their start and end apart: 14 -> 14, of which waited for: 3 -> 8; matrix products, arithmetic and copies ran while one was open for 2% -> 3% of each run, Pallas kernels for 67% -> 13%
where the time goes in v2:
time: 309 us; the launch traced here: 307 us
  waiting for transfers between devices  172 us (56%)
  Pallas kernels  63.7 us (21%)
  starting transfers between devices  30.3 us (10%)
  blocking collectives  14.5 us (5%)
  between operations  13.5 us (4%)
  local copies, waits for them, and re-layouts  12.1 us (4%)
    ppermute x10, waiting for transfers between devices, passed_along(): return lax.ppermute(value, axis, pairs)  143 us
    all_to_all x3, waiting for transfers between devices, local(): lax.all_to_all(rows, 'stretch', split_axis=0, concat_axis=0, tiled=True)  29 us
    pallas_call x3, Pallas kernels, query_gradient(): pl.pallas_call(functools.partial(attention_kernel, heads), out_shape=jax....  28.7 us
    pallas_call x1, Pallas kernels, finished(): pl.pallas_call(functools.partial(finish_kernel, widths, near, blocks), ou...  22.4 us
    all_to_all x3, starting transfers between devices, local(): lax.all_to_all(rows, 'stretch', split_axis=0, concat_axis=0, tiled=True)  19.1 us
    all_to_all x1, blocking collectives, local(): lax.all_to_all(wanted, 'stretch', split_axis=0, concat_axis=0, tiled=True)  14.5 us
    pallas_call x3, Pallas kernels, picked_rows(): pl.pallas_call(functools.partial(pick_kernel, first, qwidth + first, widt...  12.5 us
    ppermute x10, starting transfers between devices, passed_along(): return lax.ppermute(value, axis, pairs)  11.2 us
  transfers between devices with their start and end apart: 14, of which 8 were waited for; matrix products, arithmetic and copies ran while one was open for 3% of the time, Pallas kernels for 13%

profile of v2, /device:TPU:14, one launch (start us, length us, event | category | flops | bytes accessed | tf_op | source)
XLA Modules:
  0.0 307.0 jit_solution(5485808707119285253)
XLA Ops:
  9.2 14.5 %all_to_all.27 = s32[32,1,1]{2,1,0:T(1,128)S(1)} all-to-all(s32[32,1,1]{2,1,0:T(1,128)S(1)} %copy.22), channel_id=1, replica_groups=mesh['stretch'=32,'section'=4] {'stretch'}, dimensions={0} | all-to-all | bytes 256 | tf_op jit(solution)/shard_map/all_to_all | solution.py:255
  25.8 4.0 %pick_rows.5 = bf16[32,32,1024]{2,1,0:T(8,128)(2,1)} custom-call(s32[32]{0:T(128)} %reduce.picks, bf16[16,32,4096]{2,1,0:T(8,128)(2,1)} %bitcast.11), custom_call_target="tpu_custom_call" | custom-call | bytes 4194304 | tf_op jit(solution)/shard_map/pick_rows/pallas_call | solution.py:50
  29.7 5.8 %all-to-all-start.3 = ((bf16[32,32,1024]{2,1,0:T(8,128)(2,1)}), bf16[32,32,1024]{2,1,0:T(8,128)(2,1)S(1)}, u32[]{:S(2)}, u32[]{:S(2)}) async-start(bf16[32,32,1024]{2,1,0:T(8,128)(2,1)} %pick_rows.5), calls=%async_computation.3 | async-start | bytes 4194304 | tf_op jit(solution)/shard_map/all_to_all | solution.py:265
  35.5 3.7 %slice_bitcast_fusion = bf16[320,4096]{1,0:T(8,128)(2,1)} fusion(bf16[1,512,4096]{2,1,0:T(8,128)(2,1)} %param.9), kind=kLoop, calls=%fused_computation | loop fusion | bytes 5242880 | tf_op jit(solution)/shard_map/squeeze | solution.py:246
  39.2 2.0 collective-permute-start.6
  41.2 4.7 %pick_rows.3 = bf16[32,32,2048]{2,1,0:T(8,128)(2,1)} custom-call(s32[32]{0:T(128)} %reduce.picks, bf16[16,32,4096]{2,1,0:T(8,128)(2,1)} %bitcast.12), custom_call_target="tpu_custom_call" | custom-call | bytes 8388608 | tf_op jit(solution)/shard_map/pick_rows/pallas_call | solution.py:50
  45.9 25.3 %all-to-all-done.3.first.second = bf16[32,32,1024]{2,1,0:T(8,128)(2,1)S(1)} async-done(((bf16[32,32,1024]{2,1,0:T(8,128)(2,1)}), bf16[32,32,1024]{2,1,0:T(8,128)(2,1)S(1)}, u32[]{:S(2)}, u32[]{:S(2)}) %all-to-all-start.3) | async-done | bytes 2097184 | tf_op jit(solution)/shard_map/all_to_all | solution.py:265
  72.6 6.0 %all-to-all-start.1 = ((bf16[32,32,2048]{2,1,0:T(8,128)(2,1)}), bf16[32,32,2048]{2,1,0:T(8,128)(2,1)}, u32[]{:S(2)}, u32[]{:S(2)}) async-start(bf16[32,32,2048]{2,1,0:T(8,128)(2,1)} %pick_rows.3), calls=%async_computation.1 | async-start | bytes 8388608 | tf_op jit(solution)/shard_map/all_to_all | solution.py:265
  78.6 19.9 %collective-permute-done.6 = bf16[320,4096]{1,0:T(8,128)(2,1)} collective-permute-done((bf16[320,4096]{1,0:T(8,128)(2,1)}, bf16[320,4096]{1,0:T(8,128)(2,1)}, u32[]{:S(2)}, u32[]{:S(2)}) %collective-permute-start.6) | collective-permute-done | bytes 2621472 | tf_op jit(solution)/shard_map/ppermute | solution.py:21
  98.4 3.2 %collective-permute-start.7 = (bf16[320,4096]{1,0:T(8,128)(2,1)}, bf16[320,4096]{1,0:T(8,128)(2,1)}, u32[]{:S(2)}, u32[]{:S(2)}) collective-permute-start(bf16[320,4096]{1,0:T(8,128)(2,1)} %collective-permute-done.6), channel_id=1, source_target_pairs={{0,1},{1,2},{2,3},{3,0},{4,5},{5,6},{6,7},{7,4},{8,9},{9,10},{10,1... | collective-permute-start | bytes 7864328 | tf_op jit(solution)/shard_map/ppermute | solution.py:21
  101.7 3.9 %pick_rows.4 = bf16[32,32,1024]{2,1,0:T(8,128)(2,1)} custom-call(s32[32]{0:T(128)} %reduce.picks, bf16[16,32,4096]{2,1,0:T(8,128)(2,1)} %bitcast.13), custom_call_target="tpu_custom_call" | custom-call | bytes 4194304 | tf_op jit(solution)/shard_map/pick_rows/pallas_call | solution.py:50
  105.5 52.0 %collective-permute-done.7 = bf16[320,4096]{1,0:T(8,128)(2,1)} collective-permute-done((bf16[320,4096]{1,0:T(8,128)(2,1)}, bf16[320,4096]{1,0:T(8,128)(2,1)}, u32[]{:S(2)}, u32[]{:S(2)}) %collective-permute-start.7) | collective-permute-done | bytes 2621472 | tf_op jit(solution)/shard_map/ppermute | solution.py:21
  157.6 3.7 %collective-permute-start.8 = (bf16[320,4096]{1,0:T(8,128)(2,1)}, bf16[320,4096]{1,0:T(8,128)(2,1)S(1)}, u32[]{:S(2)}, u32[]{:S(2)}) collective-permute-start(bf16[320,4096]{1,0:T(8,128)(2,1)} %collective-permute-done.7), channel_id=1, source_target_pairs={{0,1},{1,2},{2,3},{3,0},{4,5},{5,6},{6,7},{7,4},{8,9},{9,10},{10,1... | collective-permute-start | bytes 7864328 | tf_op jit(solution)/shard_map/ppermute | solution.py:21
  161.4 7.4 %all-to-all-start.2 = ((bf16[32,32,1024]{2,1,0:T(8,128)(2,1)}), bf16[32,32,1024]{2,1,0:T(8,128)(2,1)}, u32[]{:S(2)}, u32[]{:S(2)}) async-start(bf16[32,32,1024]{2,1,0:T(8,128)(2,1)} %pick_rows.4), calls=%async_computation.2 | async-start | bytes 4194304 | tf_op jit(solution)/shard_map/all_to_all | solution.py:265
  168.7 2.7 slice_bitcast_fusion.1
  171.4 11.7 %query_gradient.3 = bf16[512,1024]{1,0:T(8,128)(2,1)} custom-call(s32[16]{0:T(128)} %copy-done.4, bf16[32,32,2048]{2,1,0:T(8,128)(2,1)} %all-to-all-done.1.first.second, bf16[32,32,2048]{2,1,0:T(8,128)(2,1)} %all-to-all-done.1.first.second, bf16[512,2048]{1,0:T(8,128)(2,1)} %bitcast.14, bf16[512,2048]{1,0:T(8,128)(2,1)} %bitcast.17), custom_call_target="tpu_custom_call" | custom-call | flops 201326592 | bytes 5242880 | tf_op jit(solution)/shard_map/query_gradient/pallas_call | solution.py:110
  183.2 1.4 collective-permute-start.4
  184.6 8.5 %query_gradient.5 = bf16[512,512]{1,0:T(8,128)(2,1)} custom-call(s32[16]{0:T(128)} %copy-done.4, bf16[32,32,1024]{2,1,0:T(8,128)(2,1)} %copy-done.2, bf16[32,32,1024]{2,1,0:T(8,128)(2,1)} %copy-done.2, bf16[512,2048]{1,0:T(8,128)(2,1)} %bitcast.15, bf16[512,2048]{1,0:T(8,128)(2,1)} %bitcast.18), custom_call_target="tpu_custom_call" | custom-call | flops 100663296 | bytes 2621440 | tf_op jit(solution)/shard_map/query_gradient/pallas_call | solution.py:110
  193.1 3.6 %all-to-all-done.2.first.second = bf16[32,32,1024]{2,1,0:T(8,128)(2,1)} async-done(((bf16[32,32,1024]{2,1,0:T(8,128)(2,1)}), bf16[32,32,1024]{2,1,0:T(8,128)(2,1)}, u32[]{:S(2)}, u32[]{:S(2)}) %all-to-all-start.2) | async-done | bytes 2097184 | tf_op jit(solution)/shard_map/all_to_all | solution.py:265
  196.7 8.5 %query_gradient.4 = bf16[512,512]{1,0:T(8,128)(2,1)} custom-call(s32[16]{0:T(128)} %copy-done.4, bf16[32,32,1024]{2,1,0:T(8,128)(2,1)} %all-to-all-done.2.first.second, bf16[32,32,1024]{2,1,0:T(8,128)(2,1)} %all-to-all-done.2.first.second, bf16[512,2048]{1,0:T(8,128)(2,1)} %bitcast.16, bf16[512,2048]{1,0:T(8,128)(2,1)} %bitcast.19), custom_call_target="tpu_custom_call" | custom-call | flops 100663296 | bytes 2621440 | tf_op jit(solution)/shard_map/query_gradient/pallas_call | solution.py:110
  205.1 46.0 %collective-permute-done.4.refs_4_ = f32[1,4096]{1,0:T(1,128)S(1)} collective-permute-done((f32[1,4096]{1,0:T(1,128)S(1)}, f32[1,4096]{1,0:T(1,128)S(1)}, u32[]{:S(2)}, u32[]{:S(2)}) %collective-permute-start.4) | collective-permute-done | bytes 16416 | tf_op jit(solution)/shard_map/ppermute | solution.py:21
  251.1 16.3 %collective-permute-done.3.refs_2_ = bf16[512,512]{1,0:T(8,128)(2,1)S(1)} collective-permute-done((bf16[512,512]{1,0:T(8,128)(2,1)}, bf16[512,512]{1,0:T(8,128)(2,1)S(1)}, u32[]{:S(2)}, u32[]{:S(2)}) %collective-permute-start.3) | collective-permute-done | bytes 524320 | tf_op jit(solution)/shard_map/ppermute | solution.py:21
  267.4 8.4 %collective-permute-done.2.refs_1_ = bf16[512,512]{1,0:T(8,128)(2,1)S(1)} collective-permute-done((bf16[512,512]{1,0:T(8,128)(2,1)}, bf16[512,512]{1,0:T(8,128)(2,1)S(1)}, u32[]{:S(2)}, u32[]{:S(2)}) %collective-permute-start.2) | collective-permute-done | bytes 524320 | tf_op jit(solution)/shard_map/ppermute | solution.py:21
  277.7 22.4 %finish.1 = bf16[512,4096]{1,0:T(8,128)(2,1)} custom-call(bf16[512,1024]{1,0:T(8,128)(2,1)} %collective-permute-done.1.refs_0_, bf16[512,512]{1,0:T(8,128)(2,1)S(1)} %copy-done.1, bf16[512,512]{1,0:T(8,128)(2,1)S(1)} %collective-permute-done.3.refs_2_, bf16[4096,2048]{1,0:T(8,128)(2,1)} %all-gather.2.cloned.1.call-done.refs_3_, ...), custom_call_target="tpu_custom_call" | custom-call | flops 8589934592 | bytes 33554432 | tf_op jit(solution)/shard_map/finish/pallas_call | solution.py:211
  (34 shorter events, 8.0 us)
Async XLA Ops:
  6.5 270.1 %all-gather.2.cloned.1.call-start = ((), (), s32[]{:S(2)}) async-start(), calls=%async_computation.4 | async-start | bytes 17301504 | tf_op jit(solution)/shard_map/all_gather | solution.py:257
  6.5 18.4 %collective-permute-start = (bf16[128,2048]{1,0:T(8,128)(2,1)}, bf16[128,2048]{1,0:T(8,128)(2,1)S(1)}, u32[]{:S(2)}, u32[]{:S(2)}) collective-permute-start(bf16[128,2048]{1,0:T(8,128)(2,1)} %bitcast.22), channel_id=1, source_target_pairs={{0,3},{1,0},{2,1},{3,2},{4,7},{5,4},{6,5},{7,6},{8,11},{9,8},{10,9... | collective-permute-start | bytes 1572872 | tf_op jit(solution)/shard_map/ppermute | solution.py:21
  8.2 21.5 %copy-start.4 = (s32[16]{0:T(128)}, s32[16]{0:T(128)S(1)}, u32[]{:S(2)}) copy-start(s32[16]{0:T(128)S(1)} %reshape.7.owners) | copy-start | bytes 196
  24.9 0.8 copy-start.3
  29.7 41.5 %all-to-all-start.3 = ((bf16[32,32,1024]{2,1,0:T(8,128)(2,1)}), bf16[32,32,1024]{2,1,0:T(8,128)(2,1)S(1)}, u32[]{:S(2)}, u32[]{:S(2)}) async-start(bf16[32,32,1024]{2,1,0:T(8,128)(2,1)} %pick_rows.5), calls=%async_computation.3 | async-start | bytes 4194304 | tf_op jit(solution)/shard_map/all_to_all | solution.py:265
  39.2 59.3 %collective-permute-start.6 = (bf16[320,4096]{1,0:T(8,128)(2,1)}, bf16[320,4096]{1,0:T(8,128)(2,1)}, u32[]{:S(2)}, u32[]{:S(2)}) collective-permute-start(bf16[320,4096]{1,0:T(8,128)(2,1)} %slice_bitcast_fusion), channel_id=1, source_target_pairs={{0,1},{1,2},{2,3},{3,0},{4,5},{5,6},{6,7},{7,4},{8,9},{9,10},{10,1... | collective-permute-start | bytes 7864328 | tf_op jit(solution)/shard_map/ppermute | solution.py:21
  71.3 1.3 copy-start.2
  72.6 88.8 %all-to-all-start.1 = ((bf16[32,32,2048]{2,1,0:T(8,128)(2,1)}), bf16[32,32,2048]{2,1,0:T(8,128)(2,1)}, u32[]{:S(2)}, u32[]{:S(2)}) async-start(bf16[32,32,2048]{2,1,0:T(8,128)(2,1)} %pick_rows.3), calls=%async_computation.1 | async-start | bytes 8388608 | tf_op jit(solution)/shard_map/all_to_all | solution.py:265
  98.4 59.1 %collective-permute-start.7 = (bf16[320,4096]{1,0:T(8,128)(2,1)}, bf16[320,4096]{1,0:T(8,128)(2,1)}, u32[]{:S(2)}, u32[]{:S(2)}) collective-permute-start(bf16[320,4096]{1,0:T(8,128)(2,1)} %collective-permute-done.6), channel_id=1, source_target_pairs={{0,1},{1,2},{2,3},{3,0},{4,5},{5,6},{6,7},{7,4},{8,9},{9,10},{10,1... | collective-permute-start | bytes 7864328 | tf_op jit(solution)/shard_map/ppermute | solution.py:21
  101.7 175.0 %collective-permute-start.9 = (bf16[512,4096]{1,0:T(8,128)(2,1)}, bf16[512,4096]{1,0:T(8,128)(2,1)}, u32[]{:S(2)}, u32[]{:S(2)}) collective-permute-start(bf16[512,4096]{1,0:T(8,128)(2,1)} %bitcast.21), channel_id=1, source_target_pairs={{0,3},{1,0},{2,1},{3,2},{4,7},{5,4},{6,5},{7,6},{8,11},{9,8},{10,9... | collective-permute-start | bytes 12582920 | tf_op jit(solution)/shard_map/ppermute | solution.py:21
  157.6 119.0 %collective-permute-start.8 = (bf16[320,4096]{1,0:T(8,128)(2,1)}, bf16[320,4096]{1,0:T(8,128)(2,1)S(1)}, u32[]{:S(2)}, u32[]{:S(2)}) collective-permute-start(bf16[320,4096]{1,0:T(8,128)(2,1)} %collective-permute-done.7), channel_id=1, source_target_pairs={{0,1},{1,2},{2,3},{3,0},{4,5},{5,6},{6,7},{7,4},{8,9},{9,10},{10,1... | collective-permute-start | bytes 7864328 | tf_op jit(solution)/shard_map/ppermute | solution.py:21
  161.4 35.3 %all-to-all-start.2 = ((bf16[32,32,1024]{2,1,0:T(8,128)(2,1)}), bf16[32,32,1024]{2,1,0:T(8,128)(2,1)}, u32[]{:S(2)}, u32[]{:S(2)}) async-start(bf16[32,32,1024]{2,1,0:T(8,128)(2,1)} %pick_rows.4), calls=%async_computation.2 | async-start | bytes 4194304 | tf_op jit(solution)/shard_map/all_to_all | solution.py:265
  171.4 79.7 %collective-permute-start.5 = (bf16[192,4096]{1,0:T(8,128)(2,1)}, bf16[192,4096]{1,0:T(8,128)(2,1)}, u32[]{:S(2)}, u32[]{:S(2)}) collective-permute-start(bf16[192,4096]{1,0:T(8,128)(2,1)} %slice_bitcast_fusion.1), channel_id=1, source_target_pairs={{0,3},{1,0},{2,1},{3,2},{4,7},{5,4},{6,5},{7,6},{8,11},{9,8},{10,9... | collective-permute-start | bytes 4718600 | tf_op jit(solution)/shard_map/ppermute | solution.py:21
  171.4 11.8 %copy-start.5 = (f32[1,4096]{1,0:T(1,128)S(1)}, f32[1,4096]{1,0:T(1,128)}, u32[]{:S(2)}) copy-start(f32[1,4096]{1,0:T(1,128)} %param.10) | copy-start | bytes 49156
  183.2 93.4 %collective-permute-start.1 = (bf16[512,1024]{1,0:T(8,128)(2,1)}, bf16[512,1024]{1,0:T(8,128)(2,1)}, u32[]{:S(2)}, u32[]{:S(2)}) collective-permute-start(bf16[512,1024]{1,0:T(8,128)(2,1)} %query_gradient.3), channel_id=1, source_target_pairs={{0,3},{1,0},{2,1},{3,2},{4,7},{5,4},{6,5},{7,6},{8,11},{9,8},{10,9... | collective-permute-start | bytes 3145736 | tf_op jit(solution)/shard_map/ppermute | solution.py:21
  183.2 67.9 %collective-permute-start.4 = (f32[1,4096]{1,0:T(1,128)S(1)}, f32[1,4096]{1,0:T(1,128)S(1)}, u32[]{:S(2)}, u32[]{:S(2)}) collective-permute-start(f32[1,4096]{1,0:T(1,128)S(1)} %copy-done.5), channel_id=1, source_target_pairs={{0,3},{1,0},{2,1},{3,2},{4,7},{5,4},{6,5},{7,6},{8,11},{9,8},{10,9... | collective-permute-start | bytes 49160 | tf_op jit(solution)/shard_map/ppermute | solution.py:21
  251.1 16.3 %collective-permute-start.3 = (bf16[512,512]{1,0:T(8,128)(2,1)}, bf16[512,512]{1,0:T(8,128)(2,1)S(1)}, u32[]{:S(2)}, u32[]{:S(2)}) collective-permute-start(bf16[512,512]{1,0:T(8,128)(2,1)} %query_gradient.5), channel_id=1, source_target_pairs={{0,3},{1,0},{2,1},{3,2},{4,7},{5,4},{6,5},{7,6},{8,11},{9,8},{10,9... | collective-permute-start | bytes 1572872 | tf_op jit(solution)/shard_map/ppermute | solution.py:21
  251.1 24.7 %collective-permute-start.2 = (bf16[512,512]{1,0:T(8,128)(2,1)}, bf16[512,512]{1,0:T(8,128)(2,1)S(1)}, u32[]{:S(2)}, u32[]{:S(2)}) collective-permute-start(bf16[512,512]{1,0:T(8,128)(2,1)} %query_gradient.4), channel_id=1, source_target_pairs={{0,3},{1,0},{2,1},{3,2},{4,7},{5,4},{6,5},{7,6},{8,11},{9,8},{10,9... | collective-permute-start | bytes 1572872 | tf_op jit(solution)/shard_map/ppermute | solution.py:21
  275.8 0.8 copy-start
  276.7 1.0 copy-start.1
Sparse Core Ops, SparseCore 0:
  25.9 134.0 all-gather.1

commit v3 on v2

v3 whole, which is shorter than its diff:
```python
import functools

import jax
import jax.numpy as jnp
from jax import lax
from jax.experimental import pallas as pl
from jax.experimental.pallas import tpu as pltpu
from jax.sharding import PartitionSpec as P

HEAD_DIM = 128
STRETCH = 64
norm_eps = 1e-05
CHUNKS = ((0, 2), (4, 4), (8, 8), (2, 2))
HIDDEN_SPLIT = 224
GRAD_SPLIT = 368
COLUMNS = 512
VMEM = 60 << 20
SHARD = 128
STEP = 2


def passed_along(value, axis, steps):
    count = lax.axis_size(axis)
    pairs = [(source, (source + steps) % count) for source in range(count)]
    return lax.ppermute(value, axis, pairs)


def after(value, *before):
    return lax.optimization_barrier((value, *before))[0] if before else value


def pick_kernel(key_at, value_at, width, picks, table, out, rows, arrived, left):
    groups = arrived.shape[0]
    per = rows.shape[0] // groups
    for place in range(rows.shape[0]):
        row = picks[place]
        for start, at in ((key_at, 0), (value_at, width)):
            pltpu.make_async_copy(
                table.at[row, :, pl.ds(start, width)],
                rows.at[place, :, pl.ds(at, width)],
                arrived.at[place // per],
            ).start()
    moves = []
    for group in range(groups):
        slab = pl.ds(group * per, per)
        pltpu.make_async_copy(rows.at[slab], rows.at[slab], arrived.at[group]).wait()
        moves.append(pltpu.make_async_copy(rows.at[slab], out.at[slab], left.at[group]))
        moves[-1].start()
    for move in moves:
        move.wait()


def picked_rows(picks, table, first, width, qwidth):
    places = picks.shape[0]
    span = table.shape[1]
    size = places * span * 2 * width
    groups = 4
    return pl.pallas_call(
        functools.partial(pick_kernel, first, qwidth + first, width),
        out_shape=jax.ShapeDtypeStruct((places, span, 2 * width), table.dtype),
        grid_spec=pltpu.PrefetchScalarGridSpec(
            num_scalar_prefetch=1,
            grid=(1,),
            in_specs=[pl.BlockSpec(memory_space=pl.ANY)],
            out_specs=pl.BlockSpec(memory_space=pl.ANY),
            scratch_shapes=[
                pltpu.VMEM((places, span, 2 * width), table.dtype),
                pltpu.SemaphoreType.DMA((groups,)),
                pltpu.SemaphoreType.DMA((groups,)),
            ],
        ),
        compiler_params=pltpu.CompilerParams(vmem_limit_bytes=VMEM),
        cost_estimate=pl.CostEstimate(flops=0, transcendentals=0, bytes_accessed=4 * size),
        name="pick_rows",
    )(picks, table)


def side_by_side(block, left):
    right = left + HEAD_DIM
    zeros = jnp.zeros((STRETCH, HEAD_DIM), block.dtype)
    above = jnp.concatenate([block[:, left:right], zeros], axis=1)
    below = jnp.concatenate([zeros, block[:, right : right + HEAD_DIM]], axis=1)
    return jnp.concatenate([above, below], axis=0)


def attention_kernel(heads, owners, *refs):
    *rows, query, grad, out = refs
    for stretch in range(query.shape[0] // STRETCH):
        at = pl.ds(stretch * STRETCH, STRETCH)
        one_stretch(heads, *rows[2 * stretch : 2 * stretch + 2], query.at[at], grad.at[at], out.at[at])


def one_stretch(heads, first, second, query, grad, out):
    factor = HEAD_DIM ** (-0.5)
    width = heads * HEAD_DIM
    across = (((1,), (1,)), ((), ()))
    down = (((0,), (0,)), ((), ()))
    for left in range(0, width, 2 * HEAD_DIM):
        cols = slice(left, left + 2 * HEAD_DIM)
        vcols = slice(width + left, width + left + 2 * HEAD_DIM)
        keys = jnp.concatenate([first[0, :, cols], second[0, :, cols]], axis=0)
        values = jnp.concatenate([first[0, :, vcols], second[0, :, vcols]], axis=0)
        scores = lax.dot_general(
            keys, side_by_side(query, left), across, preferred_element_type=jnp.float32
        )
        dprob = lax.dot_general(
            values, side_by_side(grad, left), across, preferred_element_type=jnp.float32
        )
        exp_scores = jnp.exp((scores - jnp.max(scores, axis=0, keepdims=True)) * factor)
        share = 1.0 / jnp.sum(exp_scores, axis=0, keepdims=True)
        inner = jnp.sum(exp_scores * dprob, axis=0, keepdims=True) * share
        dscore = (exp_scores * (dprob - inner) * (share * factor)).astype(jnp.bfloat16)
        both = lax.dot_general(dscore, keys, down, preferred_element_type=jnp.float32)
        out[:, left : left + HEAD_DIM] = both[:STRETCH, :HEAD_DIM].astype(jnp.bfloat16)
        out[:, left + HEAD_DIM : left + 2 * HEAD_DIM] = both[STRETCH:, HEAD_DIM:].astype(
            jnp.bfloat16
        )


def query_gradient(owners, fetched, queries, grads, first, heads):
    width = heads * HEAD_DIM
    tokens = queries.shape[0]
    stretches = tokens // STRETCH
    span = fetched.shape[1]
    block = first // width
    rows = 2 * STEP

    def fetched_row(place):
        return pl.BlockSpec((1, span, 2 * width), lambda c, own: (own[rows * c + place], 0, 0))

    tokens_step = STEP * STRETCH
    return pl.pallas_call(
        functools.partial(attention_kernel, heads),
        out_shape=jax.ShapeDtypeStruct((tokens, width), jnp.bfloat16),
        grid_spec=pltpu.PrefetchScalarGridSpec(
            num_scalar_prefetch=1,
            grid=(stretches // STEP,),
            in_specs=[fetched_row(place) for place in range(rows)]
            + [
                pl.BlockSpec((tokens_step, width), lambda c, own: (c, block)),
                pl.BlockSpec((tokens_step, width), lambda c, own: (c, block)),
            ],
            out_specs=pl.BlockSpec((tokens_step, width), lambda c, own: (c, 0)),
        ),
        compiler_params=pltpu.CompilerParams(vmem_limit_bytes=VMEM),
        cost_estimate=pl.CostEstimate(
            flops=6 * tokens * STRETCH * width,
            transcendentals=tokens * STRETCH * heads,
            bytes_accessed=2 * (3 * tokens * width + 2 * stretches * span * 2 * width),
        ),
        name="query_gradient",
    )(owners, *([fetched] * rows), queries, grads)


def stacked(refs):
    start = 0
    for ref in refs:
        yield ref, slice(start, start + ref.shape[0])
        start += ref.shape[0]


def finish_kernel(widths, counts, blocks, core, *refs):
    refs = list(refs)
    parts, hiddens, grads = ([refs.pop(0) for _ in range(count)] for count in counts)
    own, other, gain, out, scaled, dots, squares, whole = refs
    phase, block = pl.program_id(0), pl.program_id(1)
    model = blocks * COLUMNS

    @pl.when((phase == 0) & (block == 0))
    def _():
        for part, (first, width) in zip(parts, widths):
            whole[:, first : first + width] = part[...]

    @pl.when(phase == 0)
    def _():
        totals = []
        for weight in (own, other):
            totals.append(
                lax.dot_general(
                    whole[...],
                    weight[...],
                    (((1,), (1,)), ((), ())),
                    preferred_element_type=jnp.float32,
                )
            )
        ahead = core[0] == 0
        even = jnp.where(ahead, totals[0], totals[1])
        odd = jnp.where(ahead, totals[1], totals[0])
        tiles = []
        for lane in range(0, COLUMNS // 2, SHARD):
            tiles += [even[:, lane : lane + SHARD], odd[:, lane : lane + SHARD]]
        total = jnp.concatenate(tiles, axis=1)
        grad = total * gain[...]
        scaled[block] = grad
        for ref, rows in stacked(hiddens):
            values = ref[...].astype(jnp.float32)
            cross = grad[rows] * values
            square = values * values
            dot = cross[:, :128]
            norm = square[:, :128]
            for lane in range(128, COLUMNS, 128):
                dot = dot + cross[:, lane : lane + 128]
                norm = norm + square[:, lane : lane + 128]
            at = rows

            @pl.when(block == 0)
            def _():
                dots[at, :] = dot
                squares[at, :] = norm

            @pl.when(block > 0)
            def _():
                dots[at, :] += dot
                squares[at, :] += norm

    @pl.when((phase == 1) & (block == 0))
    def _():
        inv = lax.rsqrt(jnp.sum(squares[...], axis=-1, keepdims=True) / model + norm_eps)
        mean = inv * jnp.sum(dots[...], axis=-1, keepdims=True) / model
        squares[...] = jnp.broadcast_to(inv, squares.shape)
        dots[...] = jnp.broadcast_to(inv * inv * mean, dots.shape)

    @pl.when(phase == 1)
    def _():
        grad = scaled.at[block]
        across = COLUMNS // 128
        for values, rows in stacked(hiddens):
            for added, others in stacked(grads):
                start, stop = max(rows.start, others.start), min(rows.stop, others.stop)
                if start < stop:
                    at = slice(start, stop)
                    held = values[start - rows.start : stop - rows.start]
                    sent = added[start - others.start : stop - others.start]
                    inv = jnp.concatenate([squares[at, :]] * across, axis=1)
                    pull = jnp.concatenate([dots[at, :]] * across, axis=1)
                    out[at, :] = (
                        sent.astype(jnp.float32)
                        + inv * grad[at]
                        - pull * held.astype(jnp.float32)
                    ).astype(out.dtype)


def finished(parts, hiddens, grads, own, other, core, gain):
    tokens = sum(piece.shape[0] for piece in grads)
    model = gain.shape[1]
    widths = tuple((first * HEAD_DIM, heads * HEAD_DIM) for first, heads in CHUNKS)
    blocks = model // COLUMNS
    qwidth = own.shape[1]

    def early(phase, block):
        return jnp.where(phase == 0, block, blocks - 1)

    def late(phase, block):
        return jnp.where(phase == 0, 0, block)

    whole = [pl.BlockSpec((tokens, width), lambda p, b, c: (0, 0)) for _, width in widths]
    return pl.pallas_call(
        functools.partial(finish_kernel, widths, tuple(map(len, (parts, hiddens, grads))), blocks),
        out_shape=jax.ShapeDtypeStruct((tokens, model), jnp.bfloat16),
        grid_spec=pltpu.PrefetchScalarGridSpec(
            num_scalar_prefetch=1,
            grid=(2, blocks),
            in_specs=whole
            + [pl.BlockSpec((piece.shape[0], COLUMNS), lambda p, b, c: (0, b)) for piece in hiddens]
            + [
                pl.BlockSpec((piece.shape[0], COLUMNS), lambda p, b, c: (0, late(p, b)))
                for piece in grads
            ]
            + [pl.BlockSpec((COLUMNS // 2, qwidth), lambda p, b, c: (early(p, b), 0))] * 2
            + [pl.BlockSpec((1, COLUMNS), lambda p, b, c: (0, early(p, b)))],
            out_specs=pl.BlockSpec((tokens, COLUMNS), lambda p, b, c: (0, late(p, b))),
            scratch_shapes=[
                pltpu.VMEM((blocks, tokens, COLUMNS), jnp.float32),
                pltpu.VMEM((tokens, 128), jnp.float32),
                pltpu.VMEM((tokens, 128), jnp.float32),
                pltpu.VMEM((tokens, qwidth), jnp.bfloat16),
            ],
        ),
        compiler_params=pltpu.CompilerParams(vmem_limit_bytes=VMEM),
        cost_estimate=pl.CostEstimate(
            flops=2 * tokens * model * qwidth,
            transcendentals=0,
            bytes_accessed=2 * (model * qwidth + 4 * tokens * model),
        ),
        name="finish",
    )(core, *parts, *hiddens, *grads, own, other, gain)


def local(
    hidden, norm_gain, queries, cache, nbr_shard, nbr_slot, grad_heads, grad_out, query_weight
):
    shards = lax.axis_size("stretch")
    qwidth = queries.shape[2]
    together = lax.optimization_barrier

    def back(value):
        return passed_along(value, "section", -1)

    def ahead(value):
        return passed_along(value, "section", 1)

    def picked(chunk, picks):
        first_head, heads = CHUNKS[chunk]
        return picked_rows(picks, cache[0], first_head * HEAD_DIM, heads * HEAD_DIM, qwidth)

    def exchanged(rows):
        return lax.all_to_all(rows, "stretch", split_axis=0, concat_axis=0, tiled=True)

    def gradient(chunk, fetched):
        first_head, heads = CHUNKS[chunk]
        return query_gradient(
            owners, fetched, queries[0], grad_heads[0], first_head * HEAD_DIM, heads
        )

    here = hidden[0], grad_out[0]
    near = HIDDEN_SPLIT
    owners = nbr_shard.reshape(-1)
    asked = owners[:, None] == jnp.arange(shards)[None, :]
    wanted = jnp.sum(jnp.where(asked, nbr_slot.reshape(-1)[:, None], 0), axis=0)
    core = lax.rem(lax.axis_index("stretch"), 2).reshape(1)

    gain, weight_here = back(norm_gain), back(query_weight[0])
    hidden_near, far = back(here[0][:near]), ahead(here[0][near:])
    grads_soon = back(here[1][:GRAD_SPLIT])
    weight_here, wanted = together((weight_here, wanted))
    kinds = [list(range(kind, shards, 2)) for kind in range(2)]
    own = lax.all_gather(weight_here, "stretch", axis=0, tiled=True, axis_index_groups=kinds)
    picks = lax.all_to_all(wanted, "stretch", split_axis=0, concat_axis=0, tiled=True)
    picks, core = together((picks, core))
    rows = picked(0, picks)
    fetched = exchanged(rows)
    rows = picked(1, after(picks, rows))

    hidden_near, far, rows, picks, fetched = together((hidden_near, far, rows, picks, fetched))
    far = ahead(far)
    local0 = gradient(0, fetched)
    fetched = exchanged(rows)
    rows = picked(2, picks)

    here, gain, grads_soon, far, rows, picks, fetched, local0 = together(
        (here, gain, grads_soon, far, rows, picks, fetched, local0)
    )
    far, grads, part0 = ahead(far), back(here[1][GRAD_SPLIT:]), back(local0)
    local1 = gradient(1, fetched)
    fetched = exchanged(rows)
    rows = picked(3, picks)
    part1 = back(local1)

    rows, fetched, own, grads, far, part0, part1 = together(
        (rows, fetched, own, grads, far, part0, part1)
    )
    local2 = gradient(2, fetched)
    fetched = exchanged(rows)
    part2 = back(local2)
    other = lax.ppermute(own, "stretch", [(place, place ^ 1) for place in range(shards)])

    local2, fetched = together((local2, fetched))
    part3 = back(gradient(3, fetched))
    return finished(
        (part0, part1, part2, part3),
        (hidden_near, far),
        (grads_soon, grads),
        own,
        other,
        core,
        gain,
    )[None]


def solution(mesh):
    in_specs = (
        P("section", "stretch", None),
        P("section", None),
        P("section", "stretch", None),
        P("section", "stretch", None, None),
        P("stretch", None),
        P("stretch", None),
        P("section", "stretch", None),
        P("section", "stretch", None),
        P("section", "stretch", None),
    )
    out_specs = P("section", "stretch", None)
    return jax.shard_map(local, mesh=mesh, in_specs=in_specs, out_specs=out_specs, check_vma=False)
```

time: 309 us -> 282 us (0.913)
  waiting for transfers between devices: 172 us -> 133 us
  starting transfers between devices: 30.3 us -> 45.2 us
  blocking collectives: 14.5 us -> 0 us
  Pallas kernels: 63.7 us -> 71.5 us
  local copies, waits for them, and re-layouts: 12.1 us -> 15.8 us
    ppermute x10 -> x12, waiting for transfers between devices: 143 us -> 106 us  [passed_along(): return lax.ppermute(value, axis, pairs)]
    all_to_all x3 -> x5, starting transfers between devices: 19.1 us -> 35.8 us  [the longest x4 27.2 us: exchanged(): lax.all_to_all(rows, 'stretch', split_axis=0, concat_axis=0, tiled=True)]
    all_to_all x1 -> x0, blocking collectives: 14.5 us -> none  [local(): lax.all_to_all(wanted, 'stretch', split_axis=0, concat_axis=0, tiled=True)]
    slice x0 -> x4, local copies, waits for them, and re-layouts: none -> 10.1 us  [the longest x2 4.94 us: local(): hidden_near, far = (back(here[0][:near]), ahead(here[0][near:]))]
    pallas_call x3 -> x4, Pallas kernels: 12.5 us -> 19.2 us  [picked_rows(): pl.pallas_call(functools.partial(pick_kernel, first, qwidth + first, widt...]
    squeeze x2 -> x0, local copies, waits for them, and re-layouts: 6.37 us -> none  [the longest x1 3.66 us: local(): far = hidden[0, DIRECT_ROWS:]]
    all_to_all x3 -> x5, waiting for transfers between devices: 29 us -> 27 us  [the longest x4 20.9 us: exchanged(): lax.all_to_all(rows, 'stretch', split_axis=0, concat_axis=0, tiled=True)]
    ppermute x10 -> x12, starting transfers between devices: 11.2 us -> 9.33 us  [passed_along(): return lax.ppermute(value, axis, pairs)]
  transfers between devices with their start and end apart: 14 -> 19, of which waited for: 8 -> 10; matrix products, arithmetic and copies ran while one was open for 3% -> 5% of each run, Pallas kernels for 13% -> 17%
where the time goes in v3:
time: 282 us; the launch traced here: 280 us
  waiting for transfers between devices  133 us (47%)
  Pallas kernels  71.5 us (25%)
  starting transfers between devices  45.2 us (16%)
  local copies, waits for them, and re-layouts  15.8 us (6%)
  between operations  13.6 us (5%)
    ppermute x12, waiting for transfers between devices, passed_along(): return lax.ppermute(value, axis, pairs)  106 us
    pallas_call x4, Pallas kernels, query_gradient(): pl.pallas_call(functools.partial(attention_kernel, heads), out_shape=jax....  28.7 us
    all_to_all x4, starting transfers between devices, exchanged(): lax.all_to_all(rows, 'stretch', split_axis=0, concat_axis=0, tiled=True)  27.2 us
    pallas_call x1, Pallas kernels, finished(): pl.pallas_call(functools.partial(finish_kernel, widths, tuple(map(len, (p...  23.5 us
    all_to_all x4, waiting for transfers between devices, exchanged(): lax.all_to_all(rows, 'stretch', split_axis=0, concat_axis=0, tiled=True)  20.9 us
    pallas_call x4, Pallas kernels, picked_rows(): pl.pallas_call(functools.partial(pick_kernel, first, qwidth + first, widt...  19.2 us
    ppermute x12, starting transfers between devices, passed_along(): return lax.ppermute(value, axis, pairs)  9.33 us
    all_to_all x1, starting transfers between devices, local(): lax.all_to_all(wanted, 'stretch', split_axis=0, concat_axis=0, tiled=True)  8.55 us
  transfers between devices with their start and end apart: 19, of which 10 were waited for; matrix products, arithmetic and copies ran while one was open for 5% of the time, Pallas kernels for 17%

profile of v3, /device:TPU:14, one launch (start us, length us, event | category | flops | bytes accessed | tf_op | source)
XLA Modules:
  0.0 280.1 jit_solution(9591445173860362086)
XLA Ops:
  9.1 12.5 %collective-permute-done = bf16[128,2048]{1,0:T(8,128)(2,1)S(1)} collective-permute-done((bf16[128,2048]{1,0:T(8,128)(2,1)}, bf16[128,2048]{1,0:T(8,128)(2,1)S(1)}, u32[]{:S(2)}, u32[]{:S(2)}) %collective-permute-start) | collective-permute-done | bytes 524320 | tf_op jit(solution)/shard_map/ppermute | solution.py:25
  30.2 8.5 %all-to-all-start = ((s32[32,1,1]{2,1,0:T(1,128)}), s32[32,1,1]{2,1,0:T(1,128)S(1)}, u32[]{:S(2)}, u32[]{:S(2)}) async-start(s32[32,1,1]{2,1,0:T(1,128)} %copy.22), calls=%async_computation | async-start | bytes 32768 | tf_op jit(solution)/shard_map/all_to_all | solution.py:328
  38.7 6.2 %all-to-all-done = s32[32,1,1]{2,1,0:T(1,128)S(1)} async-done(((s32[32,1,1]{2,1,0:T(1,128)}), s32[32,1,1]{2,1,0:T(1,128)S(1)}, u32[]{:S(2)}, u32[]{:S(2)}) %all-to-all-start) | async-done | bytes 160 | tf_op jit(solution)/shard_map/all_to_all | solution.py:328
  46.1 4.0 %pick_rows.4 = bf16[32,32,512]{2,1,0:T(8,128)(2,1)} custom-call(s32[32]{0:T(128)} %reduce.picks, bf16[16,32,4096]{2,1,0:T(8,128)(2,1)} %bitcast.14), custom_call_target="tpu_custom_call" | custom-call | bytes 2097152 | tf_op jit(solution)/shard_map/pick_rows/pallas_call | solution.py:58
  50.2 5.6 %all-to-all-start.1 = ((bf16[32,32,512]{2,1,0:T(8,128)(2,1)}), bf16[32,32,512]{2,1,0:T(8,128)(2,1)S(1)}, u32[]{:S(2)}, u32[]{:S(2)}) async-start(bf16[32,32,512]{2,1,0:T(8,128)(2,1)} %pick_rows.4), calls=%async_computation.1 | async-start | bytes 2097152 | tf_op jit(solution)/shard_map/all_to_all | solution.py:307
  55.8 3.8 %slice_bitcast_fusion = bf16[368,4096]{1,0:T(8,128)(2,1)} fusion(bf16[1,512,4096]{2,1,0:T(8,128)(2,1)} %param.16), kind=kLoop, calls=%fused_computation | loop fusion | bytes 6029312 | tf_op jit(solution)/shard_map/slice | solution.py:324
  59.7 5.0 %pick_rows.5 = bf16[32,32,1024]{2,1,0:T(8,128)(2,1)} custom-call(s32[32]{0:T(128)} %reduce.picks, bf16[16,32,4096]{2,1,0:T(8,128)(2,1)} %bitcast.15), custom_call_target="tpu_custom_call" | custom-call | bytes 4194304 | tf_op jit(solution)/shard_map/pick_rows/pallas_call | solution.py:58
  64.7 16.4 %all-to-all-done.1.refs_0_.refs_1_.refs_2_.refs_3_ = bf16[32,32,512]{2,1,0:T(8,128)(2,1)S(1)} async-done(((bf16[32,32,512]{2,1,0:T(8,128)(2,1)}), bf16[32,32,512]{2,1,0:T(8,128)(2,1)S(1)}, u32[]{:S(2)}, u32[]{:S(2)}) %all-to-all-start.1) | async-done | bytes 1048608 | tf_op jit(solution)/shard_map/all_to_all | solution.py:307
  83.0 5.5 %all-to-all-start.2 = ((bf16[32,32,1024]{2,1,0:T(8,128)(2,1)}), bf16[32,32,1024]{2,1,0:T(8,128)(2,1)S(1)}, u32[]{:S(2)}, u32[]{:S(2)}) async-start(bf16[32,32,1024]{2,1,0:T(8,128)(2,1)} %pick_rows.5), calls=%async_computation.2 | async-start | bytes 4194304 | tf_op jit(solution)/shard_map/all_to_all | solution.py:307
  88.9 5.4 %pick_rows.6 = bf16[32,32,2048]{2,1,0:T(8,128)(2,1)} custom-call(s32[32]{0:T(128)} %reduce.picks, bf16[16,32,4096]{2,1,0:T(8,128)(2,1)} %bitcast.16), custom_call_target="tpu_custom_call" | custom-call | bytes 8388608 | tf_op jit(solution)/shard_map/pick_rows/pallas_call | solution.py:58
  94.2 5.3 %query_gradient.4 = bf16[512,256]{1,0:T(8,128)(2,1)} custom-call(s32[16]{0:T(128)} %copy-done.5, bf16[32,32,512]{2,1,0:T(8,128)(2,1)} %copy-done.1, bf16[32,32,512]{2,1,0:T(8,128)(2,1)} %copy-done.1, bf16[32,32,512]{2,1,0:T(8,128)(2,1)} %copy-done.1, bf16[32,32,512]{2,1,0:T(8,128)(2,1)} %copy-done.1, bf16[512,2048]{1,0:T(8,128)(2,1)} %bitcast.18, ...), custom_call_target="tpu_custom_call" | custom-call | flops 50331648 | bytes 1310720 | tf_op jit(solution)/shard_map/query_gradient/pallas_call | solution.py:132
  99.5 35.0 %collective-permute-done.1.refs_10_ = f32[1,4096]{1,0:T(1,128)S(1)} collective-permute-done((f32[1,4096]{1,0:T(1,128)S(1)}, f32[1,4096]{1,0:T(1,128)S(1)}, u32[]{:S(2)}, u32[]{:S(2)}) %collective-permute-start.1) | collective-permute-done | bytes 16416 | tf_op jit(solution)/shard_map/ppermute | solution.py:25
  135.9 8.6 %all-to-all-start.3 = ((bf16[32,32,2048]{2,1,0:T(8,128)(2,1)}), bf16[32,32,2048]{2,1,0:T(8,128)(2,1)}, u32[]{:S(2)}, u32[]{:S(2)}) async-start(bf16[32,32,2048]{2,1,0:T(8,128)(2,1)} %pick_rows.6), calls=%async_computation.3 | async-start | bytes 8388608 | tf_op jit(solution)/shard_map/all_to_all | solution.py:307
  148.1 7.1 %query_gradient.5 = bf16[512,512]{1,0:T(8,128)(2,1)} custom-call(s32[16]{0:T(128)} %copy-done.5, bf16[32,32,1024]{2,1,0:T(8,128)(2,1)} %copy-done, bf16[32,32,1024]{2,1,0:T(8,128)(2,1)} %copy-done, bf16[32,32,1024]{2,1,0:T(8,128)(2,1)} %copy-done, bf16[32,32,1024]{2,1,0:T(8,128)(2,1)} %copy-done, bf16[512,2048]{1,0:T(8,128)(2,1)} %bitcast.19, ...), custom_call_target="tpu_custom_call" | custom-call | flops 100663296 | bytes 2621440 | tf_op jit(solution)/shard_map/query_gradient/pallas_call | solution.py:132
  156.0 4.9 %pick_rows.7 = bf16[32,32,512]{2,1,0:T(8,128)(2,1)} custom-call(s32[32]{0:T(128)} %reduce.picks, bf16[16,32,4096]{2,1,0:T(8,128)(2,1)} %bitcast.17), custom_call_target="tpu_custom_call" | custom-call | bytes 2097152 | tf_op jit(solution)/shard_map/pick_rows/pallas_call | solution.py:58
  160.8 31.4 %collective-permute-done.8.refs_0_ = bf16[512,256]{1,0:T(8,128)(2,1)} collective-permute-done((bf16[512,256]{1,0:T(8,128)(2,1)S(1)}, bf16[512,256]{1,0:T(8,128)(2,1)}, u32[]{:S(2)}, u32[]{:S(2)}) %collective-permute-start.8) | collective-permute-done | bytes 262176 | tf_op jit(solution)/shard_map/ppermute | solution.py:25
  192.3 5.8 %collective-permute-done.7.refs_5_ = bf16[288,4096]{1,0:T(8,128)(2,1)S(1)} collective-permute-done((bf16[288,4096]{1,0:T(8,128)(2,1)}, bf16[288,4096]{1,0:T(8,128)(2,1)S(1)}, u32[]{:S(2)}, u32[]{:S(2)}) %collective-permute-start.7) | collective-permute-done | bytes 2359328 | tf_op jit(solution)/shard_map/ppermute | solution.py:25
  198.2 7.5 %all-to-all-start.4 = ((bf16[32,32,512]{2,1,0:T(8,128)(2,1)}), bf16[32,32,512]{2,1,0:T(8,128)(2,1)S(1)}, u32[]{:S(2)}, u32[]{:S(2)}) async-start(bf16[32,32,512]{2,1,0:T(8,128)(2,1)} %pick_rows.7), calls=%async_computation.4 | async-start | bytes 2097152 | tf_op jit(solution)/shard_map/all_to_all | solution.py:307
  205.7 11.1 %query_gradient.6 = bf16[512,1024]{1,0:T(8,128)(2,1)} custom-call(s32[16]{0:T(128)} %copy-done.5, bf16[32,32,2048]{2,1,0:T(8,128)(2,1)} %all-to-all-done.3.refs_0_.refs_1_.refs_2_.refs_3_, bf16[32,32,2048]{2,1,0:T(8,128)(2,1)} %all-to-all-done.3.refs_0_.refs_1_.refs_2_.refs_3_, bf16[32,32,2048]{2,1,0:T(8,128)(2,1)} %all-to-all-done.3.refs_0_.refs_1_.refs_2_.refs_3_, ...), custom_call_target="tpu_custom_call" | custom-call | flops 201326592 | bytes 5242880 | tf_op jit(solution)/shard_map/query_gradient/pallas_call | solution.py:132
  217.3 4.5 %all-to-all-done.4.refs_0_.refs_1_.refs_2_.refs_3_ = bf16[32,32,512]{2,1,0:T(8,128)(2,1)S(1)} async-done(((bf16[32,32,512]{2,1,0:T(8,128)(2,1)}), bf16[32,32,512]{2,1,0:T(8,128)(2,1)S(1)}, u32[]{:S(2)}, u32[]{:S(2)}) %all-to-all-start.4) | async-done | bytes 1048608 | tf_op jit(solution)/shard_map/all_to_all | solution.py:307
  222.8 5.3 %query_gradient.7 = bf16[512,256]{1,0:T(8,128)(2,1)} custom-call(s32[16]{0:T(128)} %copy-done.5, bf16[32,32,512]{2,1,0:T(8,128)(2,1)} %copy-done.2, bf16[32,32,512]{2,1,0:T(8,128)(2,1)} %copy-done.2, bf16[32,32,512]{2,1,0:T(8,128)(2,1)} %copy-done.2, bf16[32,32,512]{2,1,0:T(8,128)(2,1)} %copy-done.2, bf16[512,2048]{1,0:T(8,128)(2,1)} %bitcast.21, ...), custom_call_target="tpu_custom_call" | custom-call | flops 50331648 | bytes 1310720 | tf_op jit(solution)/shard_map/query_gradient/pallas_call | solution.py:132
  228.6 15.7 %collective-permute-done.10.refs_2_ = bf16[512,1024]{1,0:T(8,128)(2,1)} collective-permute-done((bf16[512,1024]{1,0:T(8,128)(2,1)}, bf16[512,1024]{1,0:T(8,128)(2,1)}, u32[]{:S(2)}, u32[]{:S(2)}) %collective-permute-start.10) | collective-permute-done | bytes 1048608 | tf_op jit(solution)/shard_map/ppermute | solution.py:25
  244.3 4.7 %collective-permute-done.11.refs_3_ = bf16[512,256]{1,0:T(8,128)(2,1)S(1)} collective-permute-done((bf16[512,256]{1,0:T(8,128)(2,1)}, bf16[512,256]{1,0:T(8,128)(2,1)S(1)}, u32[]{:S(2)}, u32[]{:S(2)}) %collective-permute-start.11) | collective-permute-done | bytes 262176 | tf_op jit(solution)/shard_map/ppermute | solution.py:25
  249.7 23.5 %finish.1 = bf16[512,4096]{1,0:T(8,128)(2,1)} custom-call(s32[1]{0:T(128)} %bitcast.2.core, bf16[512,256]{1,0:T(8,128)(2,1)} %collective-permute-done.8.refs_0_, bf16[512,512]{1,0:T(8,128)(2,1)} %collective-permute-done.9.refs_1_, bf16[512,1024]{1,0:T(8,128)(2,1)} %collective-permute-done.10.refs_2_, bf16[512,256]{1,0:T(8,128)(2,1)} %copy-done.7, ...), custom_call_target="tpu_custom_call" | custom-call | flops 8589934592 | bytes 33554432 | tf_op jit(solution)/shard_map/finish/pallas_call | solution.py:257
  (55 shorter events, 23.3 us)
Async XLA Ops:
  6.5 191.6 %all-gather.2.cloned.1.call-start = ((), (), s32[]{:S(2)}) async-start(), calls=%async_computation.5 | async-start | bytes 8912896 | tf_op jit(solution)/shard_map/all_gather | solution.py:327
  6.5 15.1 %collective-permute-start = (bf16[128,2048]{1,0:T(8,128)(2,1)}, bf16[128,2048]{1,0:T(8,128)(2,1)S(1)}, u32[]{:S(2)}, u32[]{:S(2)}) collective-permute-start(bf16[128,2048]{1,0:T(8,128)(2,1)} %bitcast.28), channel_id=1, source_target_pairs={{0,3},{1,0},{2,1},{3,2},{4,7},{5,4},{6,5},{7,6},{8,11},{9,8},{10,9... | collective-permute-start | bytes 1572872 | tf_op jit(solution)/shard_map/ppermute | solution.py:25
  8.2 19.2 %copy-start.5 = (s32[16]{0:T(128)}, s32[16]{0:T(128)S(1)}, u32[]{:S(2)}) copy-start(s32[16]{0:T(128)S(1)} %eq.15.owners) | copy-start | bytes 196
  25.8 55.3 %collective-permute-start.4 = (bf16[288,4096]{1,0:T(8,128)(2,1)}, bf16[288,4096]{1,0:T(8,128)(2,1)}, u32[]{:S(2)}, u32[]{:S(2)}) collective-permute-start(bf16[288,4096]{1,0:T(8,128)(2,1)} %slice_bitcast_fusion.1), channel_id=1, source_target_pairs={{0,1},{1,2},{2,3},{3,0},{4,5},{5,6},{6,7},{7,4},{8,9},{9,10},{10,1... | collective-permute-start | bytes 7077896 | tf_op jit(solution)/shard_map/ppermute | solution.py:25
  27.4 53.6 %collective-permute-start.3 = (bf16[224,4096]{1,0:T(8,128)(2,1)S(1)}, bf16[224,4096]{1,0:T(8,128)(2,1)}, u32[]{:S(2)}, u32[]{:S(2)}) collective-permute-start(bf16[224,4096]{1,0:T(8,128)(2,1)S(1)} %slice_bitcast_fusion.2), channel_id=1, source_target_pairs={{0,3},{1,0},{2,1},{3,2},{4,7},{5,4},{6,5},{7,6},{8,11},{9,8},{10,9... | collective-permute-start | bytes 5505032 | tf_op jit(solution)/shard_map/ppermute | solution.py:25
  30.2 14.7 %all-to-all-start = ((s32[32,1,1]{2,1,0:T(1,128)}), s32[32,1,1]{2,1,0:T(1,128)S(1)}, u32[]{:S(2)}, u32[]{:S(2)}) async-start(s32[32,1,1]{2,1,0:T(1,128)} %copy.22), calls=%async_computation | async-start | bytes 32768 | tf_op jit(solution)/shard_map/all_to_all | solution.py:328
  50.2 30.9 %all-to-all-start.1 = ((bf16[32,32,512]{2,1,0:T(8,128)(2,1)}), bf16[32,32,512]{2,1,0:T(8,128)(2,1)S(1)}, u32[]{:S(2)}, u32[]{:S(2)}) async-start(bf16[32,32,512]{2,1,0:T(8,128)(2,1)} %pick_rows.4), calls=%async_computation.1 | async-start | bytes 2097152 | tf_op jit(solution)/shard_map/all_to_all | solution.py:307
  59.6 74.9 %collective-permute-start.2 = (bf16[368,4096]{1,0:T(8,128)(2,1)}, bf16[368,4096]{1,0:T(8,128)(2,1)}, u32[]{:S(2)}, u32[]{:S(2)}) collective-permute-start(bf16[368,4096]{1,0:T(8,128)(2,1)} %slice_bitcast_fusion), channel_id=1, source_target_pairs={{0,3},{1,0},{2,1},{3,2},{4,7},{5,4},{6,5},{7,6},{8,11},{9,8},{10,9... | collective-permute-start | bytes 9043976 | tf_op jit(solution)/shard_map/ppermute | solution.py:25
  64.7 23.9 %copy-start.8 = (f32[1,4096]{1,0:T(1,128)S(1)}, f32[1,4096]{1,0:T(1,128)}, u32[]{:S(2)}) copy-start(f32[1,4096]{1,0:T(1,128)} %param.10) | copy-start | bytes 49156
  81.0 13.2 %copy-start.1 = (bf16[32,32,512]{2,1,0:T(8,128)(2,1)}, bf16[32,32,512]{2,1,0:T(8,128)(2,1)S(1)}, u32[]{:S(2)}) copy-start(bf16[32,32,512]{2,1,0:T(8,128)(2,1)S(1)} %all-to-all-done.1.refs_0_.refs_1_.refs_2_.refs_3_) | copy-start | bytes 3145732
  81.0 54.0 %collective-permute-start.5 = (bf16[288,4096]{1,0:T(8,128)(2,1)}, bf16[288,4096]{1,0:T(8,128)(2,1)}, u32[]{:S(2)}, u32[]{:S(2)}) collective-permute-start(bf16[288,4096]{1,0:T(8,128)(2,1)} %collective-permute-done.4), channel_id=1, source_target_pairs={{0,1},{1,2},{2,3},{3,0},{4,5},{5,6},{6,7},{7,4},{8,9},{9,10},{10,1... | collective-permute-start | bytes 7077896 | tf_op jit(solution)/shard_map/ppermute | solution.py:25
  83.0 51.5 %all-to-all-start.2 = ((bf16[32,32,1024]{2,1,0:T(8,128)(2,1)}), bf16[32,32,1024]{2,1,0:T(8,128)(2,1)S(1)}, u32[]{:S(2)}, u32[]{:S(2)}) async-start(bf16[32,32,1024]{2,1,0:T(8,128)(2,1)} %pick_rows.5), calls=%async_computation.2 | async-start | bytes 4194304 | tf_op jit(solution)/shard_map/all_to_all | solution.py:307
  88.6 46.0 %collective-permute-start.1 = (f32[1,4096]{1,0:T(1,128)S(1)}, f32[1,4096]{1,0:T(1,128)S(1)}, u32[]{:S(2)}, u32[]{:S(2)}) collective-permute-start(f32[1,4096]{1,0:T(1,128)S(1)} %copy-done.8), channel_id=1, source_target_pairs={{0,3},{1,0},{2,1},{3,2},{4,7},{5,4},{6,5},{7,6},{8,11},{9,8},{10,9... | collective-permute-start | bytes 49160 | tf_op jit(solution)/shard_map/ppermute | solution.py:25
  135.9 62.2 %all-to-all-start.3 = ((bf16[32,32,2048]{2,1,0:T(8,128)(2,1)}), bf16[32,32,2048]{2,1,0:T(8,128)(2,1)}, u32[]{:S(2)}, u32[]{:S(2)}) async-start(bf16[32,32,2048]{2,1,0:T(8,128)(2,1)} %pick_rows.6), calls=%async_computation.3 | async-start | bytes 8388608 | tf_op jit(solution)/shard_map/all_to_all | solution.py:307
  144.5 53.6 %collective-permute-start.7 = (bf16[288,4096]{1,0:T(8,128)(2,1)}, bf16[288,4096]{1,0:T(8,128)(2,1)S(1)}, u32[]{:S(2)}, u32[]{:S(2)}) collective-permute-start(bf16[288,4096]{1,0:T(8,128)(2,1)} %collective-permute-done.5), channel_id=1, source_target_pairs={{0,1},{1,2},{2,3},{3,0},{4,5},{5,6},{6,7},{7,4},{8,9},{9,10},{10,1... | collective-permute-start | bytes 7077896 | tf_op jit(solution)/shard_map/ppermute | solution.py:25
  146.0 9.7 %copy-start.4 = (bf16[512,256]{1,0:T(8,128)(2,1)S(1)}, bf16[512,256]{1,0:T(8,128)(2,1)}, u32[]{:S(2)}) copy-start(bf16[512,256]{1,0:T(8,128)(2,1)} %query_gradient.4) | copy-start | bytes 786436
  146.0 46.3 %collective-permute-start.6 = (bf16[144,4096]{1,0:T(8,128)(2,1)S(1)}, bf16[144,4096]{1,0:T(8,128)(2,1)}, u32[]{:S(2)}, u32[]{:S(2)}) collective-permute-start(bf16[144,4096]{1,0:T(8,128)(2,1)S(1)} %slice.27), channel_id=1, source_target_pairs={{0,3},{1,0},{2,1},{3,2},{4,7},{5,4},{6,5},{7,6},{8,11},{9,8},{10,9... | collective-permute-start | bytes 3538952 | tf_op jit(solution)/shard_map/ppermute | solution.py:25
  155.2 37.1 %collective-permute-start.9 = (bf16[512,512]{1,0:T(8,128)(2,1)}, bf16[512,512]{1,0:T(8,128)(2,1)}, u32[]{:S(2)}, u32[]{:S(2)}) collective-permute-start(bf16[512,512]{1,0:T(8,128)(2,1)} %query_gradient.5), channel_id=1, source_target_pairs={{0,3},{1,0},{2,1},{3,2},{4,7},{5,4},{6,5},{7,6},{8,11},{9,8},{10,9... | collective-permute-start | bytes 1572872 | tf_op jit(solution)/shard_map/ppermute | solution.py:25
  155.7 36.6 %collective-permute-start.8 = (bf16[512,256]{1,0:T(8,128)(2,1)S(1)}, bf16[512,256]{1,0:T(8,128)(2,1)}, u32[]{:S(2)}, u32[]{:S(2)}) collective-permute-start(bf16[512,256]{1,0:T(8,128)(2,1)S(1)} %copy-done.4), channel_id=1, source_target_pairs={{0,3},{1,0},{2,1},{3,2},{4,7},{5,4},{6,5},{7,6},{8,11},{9,8},{10,9... | collective-permute-start | bytes 786440 | tf_op jit(solution)/shard_map/ppermute | solution.py:25
  198.1 18.7 %copy-start.6 = (bf16[288,4096]{1,0:T(8,128)(2,1)}, bf16[288,4096]{1,0:T(8,128)(2,1)S(1)}, u32[]{:S(2)}) copy-start(bf16[288,4096]{1,0:T(8,128)(2,1)S(1)} %collective-permute-done.7.refs_5_) | copy-start | bytes 7077892
  198.1 50.9 %collective-permute-start.12 = (bf16[2048,2048]{1,0:T(8,128)(2,1)}, bf16[2048,2048]{1,0:T(8,128)(2,1)}, u32[]{:S(2)}, u32[]{:S(2)}) collective-permute-start(bf16[2048,2048]{1,0:T(8,128)(2,1)} %all-gather.2.cloned.1.call-done.refs_8_), channel_id=1, source_target_pairs={{0,4},{4,0},{8,12},{12,8},{16,20},{20,16},{24,28},{28,24},{32,36},... | collective-permute-start | bytes 25165832 | tf_op jit(solution)/shard_map/ppermute | solution.py:355
  198.2 23.6 %all-to-all-start.4 = ((bf16[32,32,512]{2,1,0:T(8,128)(2,1)}), bf16[32,32,512]{2,1,0:T(8,128)(2,1)S(1)}, u32[]{:S(2)}, u32[]{:S(2)}) async-start(bf16[32,32,512]{2,1,0:T(8,128)(2,1)} %pick_rows.7), calls=%async_computation.4 | async-start | bytes 2097152 | tf_op jit(solution)/shard_map/all_to_all | solution.py:307
  216.8 27.5 %collective-permute-start.10 = (bf16[512,1024]{1,0:T(8,128)(2,1)}, bf16[512,1024]{1,0:T(8,128)(2,1)}, u32[]{:S(2)}, u32[]{:S(2)}) collective-permute-start(bf16[512,1024]{1,0:T(8,128)(2,1)} %query_gradient.6), channel_id=1, source_target_pairs={{0,3},{1,0},{2,1},{3,2},{4,7},{5,4},{6,5},{7,6},{8,11},{9,8},{10,9... | collective-permute-start | bytes 3145736 | tf_op jit(solution)/shard_map/ppermute | solution.py:25
  228.0 21.0 %collective-permute-start.11 = (bf16[512,256]{1,0:T(8,128)(2,1)}, bf16[512,256]{1,0:T(8,128)(2,1)S(1)}, u32[]{:S(2)}, u32[]{:S(2)}) collective-permute-start(bf16[512,256]{1,0:T(8,128)(2,1)} %query_gradient.7), channel_id=1, source_target_pairs={{0,3},{1,0},{2,1},{3,2},{4,7},{5,4},{6,5},{7,6},{8,11},{9,8},{10,9... | collective-permute-start | bytes 786440 | tf_op jit(solution)/shard_map/ppermute | solution.py:25
  (5 other events, 4.5 us)
Sparse Core Ops, SparseCore 0:
  22.6 103.5 all-gather.1

commit v4 on v3

--- a/solution.py
+++ b/solution.py
@@ -13,7 +13,8 @@
 CHUNKS = ((0, 2), (4, 4), (8, 8), (2, 2))
 HIDDEN_SPLIT = 224
 GRAD_SPLIT = 368
-COLUMNS = 512
+PARTS = ((0, 2), (4, 4), (8, 4), (12, 4), (2, 2))
+COLUMNS = 1024
 VMEM = 60 << 20
 SHARD = 128
 STEP = 2
@@ -87,19 +88,18 @@
     *rows, query, grad, out = refs
     for stretch in range(query.shape[0] // STRETCH):
         at = pl.ds(stretch * STRETCH, STRETCH)
-        one_stretch(heads, *rows[2 * stretch : 2 * stretch + 2], query.at[at], grad.at[at], out.at[at])
-
-
-def one_stretch(heads, first, second, query, grad, out):
+        one_stretch(heads, *rows[4 * stretch : 4 * stretch + 4], query.at[at], grad.at[at], out.at[at])
+
+
+def one_stretch(heads, first_keys, first_values, second_keys, second_values, query, grad, out):
     factor = HEAD_DIM ** (-0.5)
     width = heads * HEAD_DIM
     across = (((1,), (1,)), ((), ()))
     down = (((0,), (0,)), ((), ()))
     for left in range(0, width, 2 * HEAD_DIM):
         cols = slice(left, left + 2 * HEAD_DIM)
-        vcols = slice(width + left, width + left + 2 * HEAD_DIM)
-        keys = jnp.concatenate([first[0, :, cols], second[0, :, cols]], axis=0)
-        values = jnp.concatenate([first[0, :, vcols], second[0, :, vcols]], axis=0)
+        keys = jnp.concatenate([first_keys[0, :, cols], second_keys[0, :, cols]], axis=0)
+        values = jnp.concatenate([first_values[0, :, cols], second_values[0, :, cols]], axis=0)
         scores = lax.dot_general(
             keys, side_by_side(query, left), across, preferred_element_type=jnp.float32
         )
@@ -117,7 +117,7 @@
         )
 
 
-def query_gradient(owners, fetched, queries, grads, first, heads):
+def query_gradient(owners, fetched, queries, grads, first, heads, skipped=0):
     width = heads * HEAD_DIM
     tokens = queries.shape[0]
     stretches = tokens // STRETCH
@@ -125,8 +125,13 @@
     block = first // width
     rows = 2 * STEP
 
-    def fetched_row(place):
-        return pl.BlockSpec((1, span, 2 * width), lambda c, own: (own[rows * c + place], 0, 0))
+    within = fetched.shape[2] // (2 * width)
+
+    def fetched_row(place, kind):
+        return pl.BlockSpec(
+            (1, span, width),
+            lambda c, own: (own[rows * c + place], 0, kind * within + skipped // width),
+        )
 
     tokens_step = STEP * STRETCH
     return pl.pallas_call(
@@ -135,7 +140,7 @@
         grid_spec=pltpu.PrefetchScalarGridSpec(
             num_scalar_prefetch=1,
             grid=(stretches // STEP,),
-            in_specs=[fetched_row(place) for place in range(rows)]
+            in_specs=[fetched_row(place, kind) for place in range(rows) for kind in range(2)]
             + [
                 pl.BlockSpec((tokens_step, width), lambda c, own: (c, block)),
                 pl.BlockSpec((tokens_step, width), lambda c, own: (c, block)),
@@ -149,7 +154,7 @@
             bytes_accessed=2 * (3 * tokens * width + 2 * stretches * span * 2 * width),
         ),
         name="query_gradient",
-    )(owners, *([fetched] * rows), queries, grads)
+    )(owners, *([fetched] * (2 * rows)), queries, grads)
 
 
 def stacked(refs):
@@ -243,7 +248,7 @@
 def finished(parts, hiddens, grads, own, other, core, gain):
     tokens = sum(piece.shape[0] for piece in grads)
     model = gain.shape[1]
-    widths = tuple((first * HEAD_DIM, heads * HEAD_DIM) for first, heads in CHUNKS)
+    widths = tuple((first * HEAD_DIM, heads * HEAD_DIM) for first, heads in PARTS)
     blocks = model // COLUMNS
     qwidth = own.shape[1]
 
@@ -349,15 +354,20 @@
     rows, fetched, own, grads, far, part0, part1 = together(
         (rows, fetched, own, grads, far, part0, part1)
     )
-    local2 = gradient(2, fetched)
+    held = fetched
+    local2 = query_gradient(owners, held, queries[0], grad_heads[0], 8 * HEAD_DIM, 4)
     fetched = exchanged(rows)
     part2 = back(local2)
+    local3 = query_gradient(
+        owners, after(held, local2), queries[0], grad_heads[0], 12 * HEAD_DIM, 4, 4 * HEAD_DIM
+    )
+    part3 = back(local3)
     other = lax.ppermute(own, "stretch", [(place, place ^ 1) for place in range(shards)])
 
-    local2, fetched = together((local2, fetched))
-    part3 = back(gradient(3, fetched))
+    local3, part2, fetched = together((local3, part2, fetched))
+    part4 = back(gradient(3, fetched))
     return finished(
-        (part0, part1, part2, part3),
+        (part0, part1, part2, part3, part4),
         (hidden_near, far),
         (grads_soon, grads),
         own,

time: 282 us -> 277 us (0.982)
  waiting for transfers between devices: 133 us -> 122 us
  Pallas kernels: 71.5 us -> 76.9 us
    all_to_all x4, waiting for transfers between devices: 20.9 us -> 15.4 us  [exchanged(): lax.all_to_all(rows, 'stretch', split_axis=0, concat_axis=0, tiled=True)]
    ppermute x12 -> x13, waiting for transfers between devices: 106 us -> 101 us  [passed_along(): return lax.ppermute(value, axis, pairs)]
    pallas_call x4 -> x5, Pallas kernels: 28.7 us -> 33.2 us  [query_gradient(): pl.pallas_call(functools.partial(attention_kernel, heads), out_shape=jax....]
    ppermute x12 -> x13, starting transfers between devices: 9.33 us -> 9.5 us  [passed_along(): return lax.ppermute(value, axis, pairs)]
  transfers between devices with their start and end apart: 19 -> 20, of which waited for: 10 -> 9; matrix products, arithmetic and copies ran while one was open for 5% -> 5% of each run, Pallas kernels for 17% -> 20%
where the time goes in v4:
time: 277 us; the launch traced here: 275 us
  waiting for transfers between devices  122 us (44%)
  Pallas kernels  76.9 us (28%)
  starting transfers between devices  44.8 us (16%)
  local copies, waits for them, and re-layouts  16.3 us (6%)
  between operations  13.6 us (5%)
    ppermute x13, waiting for transfers between devices, passed_along(): return lax.ppermute(value, axis, pairs)  101 us
    pallas_call x5, Pallas kernels, query_gradient(): pl.pallas_call(functools.partial(attention_kernel, heads), out_shape=jax....  33.2 us
    all_to_all x4, starting transfers between devices, exchanged(): lax.all_to_all(rows, 'stretch', split_axis=0, concat_axis=0, tiled=True)  26.6 us
    pallas_call x1, Pallas kernels, finished(): pl.pallas_call(functools.partial(finish_kernel, widths, tuple(map(len, (p...  22.2 us
    pallas_call x4, Pallas kernels, picked_rows(): pl.pallas_call(functools.partial(pick_kernel, first, qwidth + first, widt...  21.5 us
    all_to_all x4, waiting for transfers between devices, exchanged(): lax.all_to_all(rows, 'stretch', split_axis=0, concat_axis=0, tiled=True)  15.4 us
    ppermute x13, starting transfers between devices, passed_along(): return lax.ppermute(value, axis, pairs)  9.5 us
    all_to_all x1, starting transfers between devices, local(): lax.all_to_all(wanted, 'stretch', split_axis=0, concat_axis=0, tiled=True)  8.55 us
  transfers between devices with their start and end apart: 20, of which 9 were waited for; matrix products, arithmetic and copies ran while one was open for 5% of the time, Pallas kernels for 20%

profile of v4, /device:TPU:14, one launch (start us, length us, event | category | flops | bytes accessed | tf_op | source)
XLA Modules:
  0.0 275.1 jit_solution(2307181558983355622)
XLA Ops:
  9.1 12.5 %collective-permute-done = bf16[128,2048]{1,0:T(8,128)(2,1)S(1)} collective-permute-done((bf16[128,2048]{1,0:T(8,128)(2,1)}, bf16[128,2048]{1,0:T(8,128)(2,1)S(1)}, u32[]{:S(2)}, u32[]{:S(2)}) %collective-permute-start) | collective-permute-done | bytes 524320 | tf_op jit(solution)/shard_map/ppermute | solution.py:26
  30.2 8.5 %all-to-all-start = ((s32[32,1,1]{2,1,0:T(1,128)}), s32[32,1,1]{2,1,0:T(1,128)S(1)}, u32[]{:S(2)}, u32[]{:S(2)}) async-start(s32[32,1,1]{2,1,0:T(1,128)} %copy.22), calls=%async_computation | async-start | bytes 32768 | tf_op jit(solution)/shard_map/all_to_all | solution.py:333
  38.7 6.2 %all-to-all-done = s32[32,1,1]{2,1,0:T(1,128)S(1)} async-done(((s32[32,1,1]{2,1,0:T(1,128)}), s32[32,1,1]{2,1,0:T(1,128)S(1)}, u32[]{:S(2)}, u32[]{:S(2)}) %all-to-all-start) | async-done | bytes 160 | tf_op jit(solution)/shard_map/all_to_all | solution.py:333
  46.1 4.7 %pick_rows.4 = bf16[32,32,512]{2,1,0:T(8,128)(2,1)} custom-call(s32[32]{0:T(128)} %reduce.picks, bf16[16,32,4096]{2,1,0:T(8,128)(2,1)} %bitcast.14), custom_call_target="tpu_custom_call" | custom-call | bytes 2097152 | tf_op jit(solution)/shard_map/pick_rows/pallas_call | solution.py:59
  50.8 4.5 %all-to-all-start.1 = ((bf16[32,32,512]{2,1,0:T(8,128)(2,1)}), bf16[32,32,512]{2,1,0:T(8,128)(2,1)S(1)}, u32[]{:S(2)}, u32[]{:S(2)}) async-start(bf16[32,32,512]{2,1,0:T(8,128)(2,1)} %pick_rows.4), calls=%async_computation.1 | async-start | bytes 2097152 | tf_op jit(solution)/shard_map/all_to_all | solution.py:312
  59.2 5.5 %pick_rows.5 = bf16[32,32,1024]{2,1,0:T(8,128)(2,1)} custom-call(s32[32]{0:T(128)} %reduce.picks, bf16[16,32,4096]{2,1,0:T(8,128)(2,1)} %bitcast.15), custom_call_target="tpu_custom_call" | custom-call | bytes 4194304 | tf_op jit(solution)/shard_map/pick_rows/pallas_call | solution.py:59
  64.7 15.4 %all-to-all-done.1.refs_0_.refs_1_.refs_2_.refs_3_.refs_4_.refs_5_.refs_6_.refs_7_ = bf16[32,32,512]{2,1,0:T(8,128)(2,1)S(1)} async-done(((bf16[32,32,512]{2,1,0:T(8,128)(2,1)}), bf16[32,32,512]{2,1,0:T(8,128)(2,1)S(1)}, u32[]{:S(2)}, u32[]{:S(2)}) %all-to-all-start.1) | async-done | bytes 1048608 | tf_op jit(solution)/shard_map/all_to_all | solution.py:312
  82.2 6.0 %all-to-all-start.2 = ((bf16[32,32,1024]{2,1,0:T(8,128)(2,1)}), bf16[32,32,1024]{2,1,0:T(8,128)(2,1)S(1)}, u32[]{:S(2)}, u32[]{:S(2)}) async-start(bf16[32,32,1024]{2,1,0:T(8,128)(2,1)} %pick_rows.5), calls=%async_computation.2 | async-start | bytes 4194304 | tf_op jit(solution)/shard_map/all_to_all | solution.py:312
  88.9 6.0 %pick_rows.6 = bf16[32,32,2048]{2,1,0:T(8,128)(2,1)} custom-call(s32[32]{0:T(128)} %reduce.picks, bf16[16,32,4096]{2,1,0:T(8,128)(2,1)} %bitcast.16), custom_call_target="tpu_custom_call" | custom-call | bytes 8388608 | tf_op jit(solution)/shard_map/pick_rows/pallas_call | solution.py:59
  94.9 5.5 %query_gradient.5 = bf16[512,256]{1,0:T(8,128)(2,1)} custom-call(s32[16]{0:T(128)} %copy-done.5, bf16[32,32,512]{2,1,0:T(8,128)(2,1)} %copy-done.1, bf16[32,32,512]{2,1,0:T(8,128)(2,1)} %copy-done.1, bf16[32,32,512]{2,1,0:T(8,128)(2,1)} %copy-done.1, bf16[32,32,512]{2,1,0:T(8,128)(2,1)} %copy-done.1, bf16[32,32,512]{2,1,0:T(8,128)(2,1)} %copy-done.1, ...), custom_call_target="tpu_custom_call" | custom-call | flops 50331648 | bytes 1310720 | tf_op jit(solution)/shard_map/query_gradient/pallas_call | solution.py:137
  100.4 34.1 %collective-permute-done.1.refs_11_ = f32[1,4096]{1,0:T(1,128)S(1)} collective-permute-done((f32[1,4096]{1,0:T(1,128)S(1)}, f32[1,4096]{1,0:T(1,128)S(1)}, u32[]{:S(2)}, u32[]{:S(2)}) %collective-permute-start.1) | collective-permute-done | bytes 16416 | tf_op jit(solution)/shard_map/ppermute | solution.py:26
  135.9 8.6 %all-to-all-start.3 = ((bf16[32,32,2048]{2,1,0:T(8,128)(2,1)}), bf16[32,32,2048]{2,1,0:T(8,128)(2,1)}, u32[]{:S(2)}, u32[]{:S(2)}) async-start(bf16[32,32,2048]{2,1,0:T(8,128)(2,1)} %pick_rows.6), calls=%async_computation.3 | async-start | bytes 8388608 | tf_op jit(solution)/shard_map/all_to_all | solution.py:312
  148.1 7.4 %query_gradient.6 = bf16[512,512]{1,0:T(8,128)(2,1)} custom-call(s32[16]{0:T(128)} %copy-done.5, bf16[32,32,1024]{2,1,0:T(8,128)(2,1)} %copy-done, bf16[32,32,1024]{2,1,0:T(8,128)(2,1)} %copy-done, bf16[32,32,1024]{2,1,0:T(8,128)(2,1)} %copy-done, bf16[32,32,1024]{2,1,0:T(8,128)(2,1)} %copy-done, bf16[32,32,1024]{2,1,0:T(8,128)(2,1)} %copy-done, ...), custom_call_target="tpu_custom_call" | custom-call | flops 100663296 | bytes 2621440 | tf_op jit(solution)/shard_map/query_gradient/pallas_call | solution.py:137
  156.3 5.3 %pick_rows.7 = bf16[32,32,512]{2,1,0:T(8,128)(2,1)} custom-call(s32[32]{0:T(128)} %reduce.picks, bf16[16,32,4096]{2,1,0:T(8,128)(2,1)} %bitcast.17), custom_call_target="tpu_custom_call" | custom-call | bytes 2097152 | tf_op jit(solution)/shard_map/pick_rows/pallas_call | solution.py:59
  161.6 30.7 %collective-permute-done.8.refs_0_ = bf16[512,256]{1,0:T(8,128)(2,1)} collective-permute-done((bf16[512,256]{1,0:T(8,128)(2,1)S(1)}, bf16[512,256]{1,0:T(8,128)(2,1)}, u32[]{:S(2)}, u32[]{:S(2)}) %collective-permute-start.8) | collective-permute-done | bytes 262176 | tf_op jit(solution)/shard_map/ppermute | solution.py:26
  192.2 5.8 %collective-permute-done.7.refs_6_ = bf16[288,4096]{1,0:T(8,128)(2,1)S(1)} collective-permute-done((bf16[288,4096]{1,0:T(8,128)(2,1)}, bf16[288,4096]{1,0:T(8,128)(2,1)S(1)}, u32[]{:S(2)}, u32[]{:S(2)}) %collective-permute-start.7) | collective-permute-done | bytes 2359328 | tf_op jit(solution)/shard_map/ppermute | solution.py:26
  198.2 7.5 %all-to-all-start.4 = ((bf16[32,32,512]{2,1,0:T(8,128)(2,1)}), bf16[32,32,512]{2,1,0:T(8,128)(2,1)S(1)}, u32[]{:S(2)}, u32[]{:S(2)}) async-start(bf16[32,32,512]{2,1,0:T(8,128)(2,1)} %pick_rows.7), calls=%async_computation.4 | async-start | bytes 2097152 | tf_op jit(solution)/shard_map/all_to_all | solution.py:312
  205.7 7.4 %query_gradient.7 = bf16[512,512]{1,0:T(8,128)(2,1)} custom-call(s32[16]{0:T(128)} %copy-done.5, bf16[32,32,2048]{2,1,0:T(8,128)(2,1)} %all-to-all-done.3.refs_0_.refs_1_.refs_2_.refs_3_.refs_4_.refs_5_.refs_6_.refs_7_, bf16[32,32,2048]{2,1,0:T(8,128)(2,1)} %all-to-all-done.3.refs_0_.refs_1_.refs_2_.refs_3_.refs_4_.refs_5_.refs_6_.refs_7_, ...), custom_call_target="tpu_custom_call" | custom-call | flops 100663296 | bytes 2621440 | tf_op jit(solution)/shard_map/query_gradient/pallas_call | solution.py:137
  213.7 7.4 %query_gradient.8 = bf16[512,512]{1,0:T(8,128)(2,1)} custom-call(s32[16]{0:T(128)} %copy-done.5, bf16[32,32,2048]{2,1,0:T(8,128)(2,1)} %all-to-all-done.3.refs_0_.refs_1_.refs_2_.refs_3_.refs_4_.refs_5_.refs_6_.refs_7_, bf16[32,32,2048]{2,1,0:T(8,128)(2,1)} %all-to-all-done.3.refs_0_.refs_1_.refs_2_.refs_3_.refs_4_.refs_5_.refs_6_.refs_7_, ...), custom_call_target="tpu_custom_call" | custom-call | flops 100663296 | bytes 2621440 | tf_op jit(solution)/shard_map/query_gradient/pallas_call | solution.py:137
  221.3 8.1 %collective-permute-done.10.refs_2_ = bf16[512,512]{1,0:T(8,128)(2,1)} collective-permute-done((bf16[512,512]{1,0:T(8,128)(2,1)}, bf16[512,512]{1,0:T(8,128)(2,1)}, u32[]{:S(2)}, u32[]{:S(2)}) %collective-permute-start.10) | collective-permute-done | bytes 524320 | tf_op jit(solution)/shard_map/ppermute | solution.py:26
  230.4 5.6 %query_gradient.9 = bf16[512,256]{1,0:T(8,128)(2,1)} custom-call(s32[16]{0:T(128)} %copy-done.5, bf16[32,32,512]{2,1,0:T(8,128)(2,1)} %copy-done.2, bf16[32,32,512]{2,1,0:T(8,128)(2,1)} %copy-done.2, bf16[32,32,512]{2,1,0:T(8,128)(2,1)} %copy-done.2, bf16[32,32,512]{2,1,0:T(8,128)(2,1)} %copy-done.2, bf16[32,32,512]{2,1,0:T(8,128)(2,1)} %copy-done.2, ...), custom_call_target="tpu_custom_call" | custom-call | flops 50331648 | bytes 1310720 | tf_op jit(solution)/shard_map/query_gradient/pallas_call | solution.py:137
  236.0 4.6 %collective-permute-done.11.refs_3_ = bf16[512,512]{1,0:T(8,128)(2,1)S(1)} collective-permute-done((bf16[512,512]{1,0:T(8,128)(2,1)}, bf16[512,512]{1,0:T(8,128)(2,1)S(1)}, u32[]{:S(2)}, u32[]{:S(2)}) %collective-permute-start.11) | collective-permute-done | bytes 524320 | tf_op jit(solution)/shard_map/ppermute | solution.py:26
  240.6 4.8 %collective-permute-done.12.refs_4_ = bf16[512,256]{1,0:T(8,128)(2,1)S(1)} collective-permute-done((bf16[512,256]{1,0:T(8,128)(2,1)}, bf16[512,256]{1,0:T(8,128)(2,1)S(1)}, u32[]{:S(2)}, u32[]{:S(2)}) %collective-permute-start.12) | collective-permute-done | bytes 262176 | tf_op jit(solution)/shard_map/ppermute | solution.py:26
  246.1 22.2 %finish.1 = bf16[512,4096]{1,0:T(8,128)(2,1)} custom-call(s32[1]{0:T(128)} %bitcast.2.core, bf16[512,256]{1,0:T(8,128)(2,1)} %collective-permute-done.8.refs_0_, bf16[512,512]{1,0:T(8,128)(2,1)} %collective-permute-done.9.refs_1_, bf16[512,512]{1,0:T(8,128)(2,1)} %collective-permute-done.10.refs_2_, bf16[512,512]{1,0:T(8,128)(2,1)} %copy-done.7, ...), custom_call_target="tpu_custom_call" | custom-call | flops 8589934592 | bytes 33554432 | tf_op jit(solution)/shard_map/finish/pallas_call | solution.py:262
  (60 shorter events, 27.3 us)
Async XLA Ops:
  6.5 191.6 %all-gather.2.cloned.1.call-start = ((), (), s32[]{:S(2)}) async-start(), calls=%async_computation.5 | async-start | bytes 8912896 | tf_op jit(solution)/shard_map/all_gather | solution.py:332
  6.5 15.1 %collective-permute-start = (bf16[128,2048]{1,0:T(8,128)(2,1)}, bf16[128,2048]{1,0:T(8,128)(2,1)S(1)}, u32[]{:S(2)}, u32[]{:S(2)}) collective-permute-start(bf16[128,2048]{1,0:T(8,128)(2,1)} %bitcast.30), channel_id=1, source_target_pairs={{0,3},{1,0},{2,1},{3,2},{4,7},{5,4},{6,5},{7,6},{8,11},{9,8},{10,9... | collective-permute-start | bytes 1572872 | tf_op jit(solution)/shard_map/ppermute | solution.py:26
  8.2 19.2 %copy-start.5 = (s32[16]{0:T(128)}, s32[16]{0:T(128)S(1)}, u32[]{:S(2)}) copy-start(s32[16]{0:T(128)S(1)} %eq.15.owners) | copy-start | bytes 196
  25.8 54.3 %collective-permute-start.4 = (bf16[288,4096]{1,0:T(8,128)(2,1)}, bf16[288,4096]{1,0:T(8,128)(2,1)}, u32[]{:S(2)}, u32[]{:S(2)}) collective-permute-start(bf16[288,4096]{1,0:T(8,128)(2,1)} %slice_bitcast_fusion.1), channel_id=1, source_target_pairs={{0,1},{1,2},{2,3},{3,0},{4,5},{5,6},{6,7},{7,4},{8,9},{9,10},{10,1... | collective-permute-start | bytes 7077896 | tf_op jit(solution)/shard_map/ppermute | solution.py:26
  27.4 52.7 %collective-permute-start.3 = (bf16[224,4096]{1,0:T(8,128)(2,1)S(1)}, bf16[224,4096]{1,0:T(8,128)(2,1)}, u32[]{:S(2)}, u32[]{:S(2)}) collective-permute-start(bf16[224,4096]{1,0:T(8,128)(2,1)S(1)} %slice_bitcast_fusion.2), channel_id=1, source_target_pairs={{0,3},{1,0},{2,1},{3,2},{4,7},{5,4},{6,5},{7,6},{8,11},{9,8},{10,9... | collective-permute-start | bytes 5505032 | tf_op jit(solution)/shard_map/ppermute | solution.py:26
  30.2 14.7 %all-to-all-start = ((s32[32,1,1]{2,1,0:T(1,128)}), s32[32,1,1]{2,1,0:T(1,128)S(1)}, u32[]{:S(2)}, u32[]{:S(2)}) async-start(s32[32,1,1]{2,1,0:T(1,128)} %copy.22), calls=%async_computation | async-start | bytes 32768 | tf_op jit(solution)/shard_map/all_to_all | solution.py:333
  50.8 29.3 %all-to-all-start.1 = ((bf16[32,32,512]{2,1,0:T(8,128)(2,1)}), bf16[32,32,512]{2,1,0:T(8,128)(2,1)S(1)}, u32[]{:S(2)}, u32[]{:S(2)}) async-start(bf16[32,32,512]{2,1,0:T(8,128)(2,1)} %pick_rows.4), calls=%async_computation.1 | async-start | bytes 2097152 | tf_op jit(solution)/shard_map/all_to_all | solution.py:312
  59.2 75.3 %collective-permute-start.2 = (bf16[368,4096]{1,0:T(8,128)(2,1)}, bf16[368,4096]{1,0:T(8,128)(2,1)}, u32[]{:S(2)}, u32[]{:S(2)}) collective-permute-start(bf16[368,4096]{1,0:T(8,128)(2,1)} %slice_bitcast_fusion), channel_id=1, source_target_pairs={{0,3},{1,0},{2,1},{3,2},{4,7},{5,4},{6,5},{7,6},{8,11},{9,8},{10,9... | collective-permute-start | bytes 9043976 | tf_op jit(solution)/shard_map/ppermute | solution.py:26
  64.7 23.5 %copy-start.9 = (f32[1,4096]{1,0:T(1,128)S(1)}, f32[1,4096]{1,0:T(1,128)}, u32[]{:S(2)}) copy-start(f32[1,4096]{1,0:T(1,128)} %param.10) | copy-start | bytes 49156
  80.1 14.8 %copy-start.1 = (bf16[32,32,512]{2,1,0:T(8,128)(2,1)}, bf16[32,32,512]{2,1,0:T(8,128)(2,1)S(1)}, u32[]{:S(2)}) copy-start(bf16[32,32,512]{2,1,0:T(8,128)(2,1)S(1)} %all-to-all-done.1.refs_0_.refs_1_.refs_2_.refs_3_.refs_4_.refs_5_.refs_6_.refs_7_) | copy-start | bytes 3145732
  80.1 54.4 %collective-permute-start.5 = (bf16[288,4096]{1,0:T(8,128)(2,1)}, bf16[288,4096]{1,0:T(8,128)(2,1)}, u32[]{:S(2)}, u32[]{:S(2)}) collective-permute-start(bf16[288,4096]{1,0:T(8,128)(2,1)} %collective-permute-done.4), channel_id=1, source_target_pairs={{0,1},{1,2},{2,3},{3,0},{4,5},{5,6},{6,7},{7,4},{8,9},{9,10},{10,1... | collective-permute-start | bytes 7077896 | tf_op jit(solution)/shard_map/ppermute | solution.py:26
  82.2 52.3 %all-to-all-start.2 = ((bf16[32,32,1024]{2,1,0:T(8,128)(2,1)}), bf16[32,32,1024]{2,1,0:T(8,128)(2,1)S(1)}, u32[]{:S(2)}, u32[]{:S(2)}) async-start(bf16[32,32,1024]{2,1,0:T(8,128)(2,1)} %pick_rows.5), calls=%async_computation.2 | async-start | bytes 4194304 | tf_op jit(solution)/shard_map/all_to_all | solution.py:312
  88.3 46.3 %collective-permute-start.1 = (f32[1,4096]{1,0:T(1,128)S(1)}, f32[1,4096]{1,0:T(1,128)S(1)}, u32[]{:S(2)}, u32[]{:S(2)}) collective-permute-start(f32[1,4096]{1,0:T(1,128)S(1)} %copy-done.9), channel_id=1, source_target_pairs={{0,3},{1,0},{2,1},{3,2},{4,7},{5,4},{6,5},{7,6},{8,11},{9,8},{10,9... | collective-permute-start | bytes 49160 | tf_op jit(solution)/shard_map/ppermute | solution.py:26
  135.9 62.2 %all-to-all-start.3 = ((bf16[32,32,2048]{2,1,0:T(8,128)(2,1)}), bf16[32,32,2048]{2,1,0:T(8,128)(2,1)}, u32[]{:S(2)}, u32[]{:S(2)}) async-start(bf16[32,32,2048]{2,1,0:T(8,128)(2,1)} %pick_rows.6), calls=%async_computation.3 | async-start | bytes 8388608 | tf_op jit(solution)/shard_map/all_to_all | solution.py:312
  144.5 53.6 %collective-permute-start.7 = (bf16[288,4096]{1,0:T(8,128)(2,1)}, bf16[288,4096]{1,0:T(8,128)(2,1)S(1)}, u32[]{:S(2)}, u32[]{:S(2)}) collective-permute-start(bf16[288,4096]{1,0:T(8,128)(2,1)} %collective-permute-done.5), channel_id=1, source_target_pairs={{0,1},{1,2},{2,3},{3,0},{4,5},{5,6},{6,7},{7,4},{8,9},{9,10},{10,1... | collective-permute-start | bytes 7077896 | tf_op jit(solution)/shard_map/ppermute | solution.py:26
  146.0 46.3 %collective-permute-start.6 = (bf16[144,4096]{1,0:T(8,128)(2,1)S(1)}, bf16[144,4096]{1,0:T(8,128)(2,1)}, u32[]{:S(2)}, u32[]{:S(2)}) collective-permute-start(bf16[144,4096]{1,0:T(8,128)(2,1)S(1)} %slice.27), channel_id=1, source_target_pairs={{0,3},{1,0},{2,1},{3,2},{4,7},{5,4},{6,5},{7,6},{8,11},{9,8},{10,9... | collective-permute-start | bytes 3538952 | tf_op jit(solution)/shard_map/ppermute | solution.py:26
  155.4 36.8 %collective-permute-start.9 = (bf16[512,512]{1,0:T(8,128)(2,1)}, bf16[512,512]{1,0:T(8,128)(2,1)}, u32[]{:S(2)}, u32[]{:S(2)}) collective-permute-start(bf16[512,512]{1,0:T(8,128)(2,1)} %query_gradient.6), channel_id=1, source_target_pairs={{0,3},{1,0},{2,1},{3,2},{4,7},{5,4},{6,5},{7,6},{8,11},{9,8},{10,9... | collective-permute-start | bytes 1572872 | tf_op jit(solution)/shard_map/ppermute | solution.py:26
  156.0 36.3 %collective-permute-start.8 = (bf16[512,256]{1,0:T(8,128)(2,1)S(1)}, bf16[512,256]{1,0:T(8,128)(2,1)}, u32[]{:S(2)}, u32[]{:S(2)}) collective-permute-start(bf16[512,256]{1,0:T(8,128)(2,1)S(1)} %copy-done.4), channel_id=1, source_target_pairs={{0,3},{1,0},{2,1},{3,2},{4,7},{5,4},{6,5},{7,6},{8,11},{9,8},{10,9... | collective-permute-start | bytes 786440 | tf_op jit(solution)/shard_map/ppermute | solution.py:26
  198.1 15.0 %copy-start.6 = (bf16[288,4096]{1,0:T(8,128)(2,1)}, bf16[288,4096]{1,0:T(8,128)(2,1)S(1)}, u32[]{:S(2)}) copy-start(bf16[288,4096]{1,0:T(8,128)(2,1)S(1)} %collective-permute-done.7.refs_6_) | copy-start | bytes 7077892
  198.1 47.3 %collective-permute-start.13 = (bf16[2048,2048]{1,0:T(8,128)(2,1)}, bf16[2048,2048]{1,0:T(8,128)(2,1)}, u32[]{:S(2)}, u32[]{:S(2)}) collective-permute-start(bf16[2048,2048]{1,0:T(8,128)(2,1)} %all-gather.2.cloned.1.call-done.refs_9_), channel_id=1, source_target_pairs={{0,4},{4,0},{8,12},{12,8},{16,20},{20,16},{24,28},{28,24},{32,36},... | collective-permute-start | bytes 25165832 | tf_op jit(solution)/shard_map/ppermute | solution.py:365
  198.2 31.3 %all-to-all-start.4 = ((bf16[32,32,512]{2,1,0:T(8,128)(2,1)}), bf16[32,32,512]{2,1,0:T(8,128)(2,1)S(1)}, u32[]{:S(2)}, u32[]{:S(2)}) async-start(bf16[32,32,512]{2,1,0:T(8,128)(2,1)} %pick_rows.7), calls=%async_computation.4 | async-start | bytes 2097152 | tf_op jit(solution)/shard_map/all_to_all | solution.py:312
  213.1 16.4 %collective-permute-start.10 = (bf16[512,512]{1,0:T(8,128)(2,1)}, bf16[512,512]{1,0:T(8,128)(2,1)}, u32[]{:S(2)}, u32[]{:S(2)}) collective-permute-start(bf16[512,512]{1,0:T(8,128)(2,1)} %query_gradient.7), channel_id=1, source_target_pairs={{0,3},{1,0},{2,1},{3,2},{4,7},{5,4},{6,5},{7,6},{8,11},{9,8},{10,9... | collective-permute-start | bytes 1572872 | tf_op jit(solution)/shard_map/ppermute | solution.py:26
  221.1 19.5 %collective-permute-start.11 = (bf16[512,512]{1,0:T(8,128)(2,1)}, bf16[512,512]{1,0:T(8,128)(2,1)S(1)}, u32[]{:S(2)}, u32[]{:S(2)}) collective-permute-start(bf16[512,512]{1,0:T(8,128)(2,1)} %query_gradient.8), channel_id=1, source_target_pairs={{0,3},{1,0},{2,1},{3,2},{4,7},{5,4},{6,5},{7,6},{8,11},{9,8},{10,9... | collective-permute-start | bytes 1572872 | tf_op jit(solution)/shard_map/ppermute | solution.py:26
  236.0 9.4 %collective-permute-start.12 = (bf16[512,256]{1,0:T(8,128)(2,1)}, bf16[512,256]{1,0:T(8,128)(2,1)S(1)}, u32[]{:S(2)}, u32[]{:S(2)}) collective-permute-start(bf16[512,256]{1,0:T(8,128)(2,1)} %query_gradient.9), channel_id=1, source_target_pairs={{0,3},{1,0},{2,1},{3,2},{4,7},{5,4},{6,5},{7,6},{8,11},{9,8},{10,9... | collective-permute-start | bytes 786440 | tf_op jit(solution)/shard_map/ppermute | solution.py:26
  (7 other events, 19.3 us)
Sparse Core Ops, SparseCore 0:
  22.6 103.1 all-gather.1

commit v5 on v4

--- a/solution.py
+++ b/solution.py
@@ -11,8 +11,8 @@
 STRETCH = 64
 norm_eps = 1e-05
 CHUNKS = ((0, 2), (4, 4), (8, 8), (2, 2))
-HIDDEN_SPLIT = 224
-GRAD_SPLIT = 368
+HIDDEN_SPLIT = 240
+GRAD_SPLIT = 352
 PARTS = ((0, 2), (4, 4), (8, 4), (12, 4), (2, 2))
 COLUMNS = 1024
 VMEM = 60 << 20

time: 277 us -> 274 us (0.989)
  Pallas kernels: 76.9 us -> 72.8 us
    pallas_call x4, Pallas kernels: 21.5 us -> 17.5 us  [picked_rows(): pl.pallas_call(functools.partial(pick_kernel, first, qwidth + first, widt...]
  transfers between devices with their start and end apart: 20 -> 20, of which waited for: 9 -> 10; matrix products, arithmetic and copies ran while one was open for 5% -> 5% of each run, Pallas kernels for 20% -> 19%
where the time goes in v5:
time: 274 us; the launch traced here: 272 us
  waiting for transfers between devices  124 us (45%)
  Pallas kernels  72.8 us (27%)
  starting transfers between devices  44 us (16%)
  local copies, waits for them, and re-layouts  16.3 us (6%)
  between operations  13.6 us (5%)
    ppermute x13, waiting for transfers between devices, passed_along(): return lax.ppermute(value, axis, pairs)  102 us
    pallas_call x5, Pallas kernels, query_gradient(): pl.pallas_call(functools.partial(attention_kernel, heads), out_shape=jax....  33.2 us
    all_to_all x4, starting transfers between devices, exchanged(): lax.all_to_all(rows, 'stretch', split_axis=0, concat_axis=0, tiled=True)  26.5 us
    pallas_call x1, Pallas kernels, finished(): pl.pallas_call(functools.partial(finish_kernel, widths, tuple(map(len, (p...  22.1 us
    pallas_call x4, Pallas kernels, picked_rows(): pl.pallas_call(functools.partial(pick_kernel, first, qwidth + first, widt...  17.5 us
    all_to_all x4, waiting for transfers between devices, exchanged(): lax.all_to_all(rows, 'stretch', split_axis=0, concat_axis=0, tiled=True)  16.6 us
    ppermute x13, starting transfers between devices, passed_along(): return lax.ppermute(value, axis, pairs)  8.93 us
    all_to_all x1, starting transfers between devices, local(): lax.all_to_all(wanted, 'stretch', split_axis=0, concat_axis=0, tiled=True)  8.55 us
  transfers between devices with their start and end apart: 20, of which 10 were waited for; matrix products, arithmetic and copies ran while one was open for 5% of the time, Pallas kernels for 19%

profile of v5, /device:TPU:14, one launch (start us, length us, event | category | flops | bytes accessed | tf_op | source)
XLA Modules:
  0.0 272.2 jit_solution(11733514602850509022)
XLA Ops:
  9.1 12.5 %collective-permute-done = bf16[128,2048]{1,0:T(8,128)(2,1)S(1)} collective-permute-done((bf16[128,2048]{1,0:T(8,128)(2,1)}, bf16[128,2048]{1,0:T(8,128)(2,1)S(1)}, u32[]{:S(2)}, u32[]{:S(2)}) %collective-permute-start) | collective-permute-done | bytes 524320 | tf_op jit(solution)/shard_map/ppermute | solution.py:26
  30.1 8.5 %all-to-all-start = ((s32[32,1,1]{2,1,0:T(1,128)}), s32[32,1,1]{2,1,0:T(1,128)S(1)}, u32[]{:S(2)}, u32[]{:S(2)}) async-start(s32[32,1,1]{2,1,0:T(1,128)} %copy.22), calls=%async_computation | async-start | bytes 32768 | tf_op jit(solution)/shard_map/all_to_all | solution.py:333
  38.7 6.2 %all-to-all-done = s32[32,1,1]{2,1,0:T(1,128)S(1)} async-done(((s32[32,1,1]{2,1,0:T(1,128)}), s32[32,1,1]{2,1,0:T(1,128)S(1)}, u32[]{:S(2)}, u32[]{:S(2)}) %all-to-all-start) | async-done | bytes 160 | tf_op jit(solution)/shard_map/all_to_all | solution.py:333
  46.0 3.7 %pick_rows.4 = bf16[32,32,512]{2,1,0:T(8,128)(2,1)} custom-call(s32[32]{0:T(128)} %reduce.picks, bf16[16,32,4096]{2,1,0:T(8,128)(2,1)} %bitcast.14), custom_call_target="tpu_custom_call" | custom-call | bytes 2097152 | tf_op jit(solution)/shard_map/pick_rows/pallas_call | solution.py:59
  49.7 5.3 %all-to-all-start.1 = ((bf16[32,32,512]{2,1,0:T(8,128)(2,1)}), bf16[32,32,512]{2,1,0:T(8,128)(2,1)S(1)}, u32[]{:S(2)}, u32[]{:S(2)}) async-start(bf16[32,32,512]{2,1,0:T(8,128)(2,1)} %pick_rows.4), calls=%async_computation.1 | async-start | bytes 2097152 | tf_op jit(solution)/shard_map/all_to_all | solution.py:312
  55.0 3.7 %slice_bitcast_fusion = bf16[352,4096]{1,0:T(8,128)(2,1)} fusion(bf16[1,512,4096]{2,1,0:T(8,128)(2,1)} %param.16), kind=kLoop, calls=%fused_computation | loop fusion | bytes 5767168 | tf_op jit(solution)/shard_map/slice | solution.py:329
  58.8 4.4 %pick_rows.5 = bf16[32,32,1024]{2,1,0:T(8,128)(2,1)} custom-call(s32[32]{0:T(128)} %reduce.picks, bf16[16,32,4096]{2,1,0:T(8,128)(2,1)} %bitcast.15), custom_call_target="tpu_custom_call" | custom-call | bytes 4194304 | tf_op jit(solution)/shard_map/pick_rows/pallas_call | solution.py:59
  63.2 16.0 %all-to-all-done.1.refs_0_.refs_1_.refs_2_.refs_3_.refs_4_.refs_5_.refs_6_.refs_7_ = bf16[32,32,512]{2,1,0:T(8,128)(2,1)S(1)} async-done(((bf16[32,32,512]{2,1,0:T(8,128)(2,1)}), bf16[32,32,512]{2,1,0:T(8,128)(2,1)S(1)}, u32[]{:S(2)}, u32[]{:S(2)}) %all-to-all-start.1) | async-done | bytes 1048608 | tf_op jit(solution)/shard_map/all_to_all | solution.py:312
  81.1 5.6 %all-to-all-start.2 = ((bf16[32,32,1024]{2,1,0:T(8,128)(2,1)}), bf16[32,32,1024]{2,1,0:T(8,128)(2,1)S(1)}, u32[]{:S(2)}, u32[]{:S(2)}) async-start(bf16[32,32,1024]{2,1,0:T(8,128)(2,1)} %pick_rows.5), calls=%async_computation.2 | async-start | bytes 4194304 | tf_op jit(solution)/shard_map/all_to_all | solution.py:312
  86.9 5.1 %pick_rows.6 = bf16[32,32,2048]{2,1,0:T(8,128)(2,1)} custom-call(s32[32]{0:T(128)} %reduce.picks, bf16[16,32,4096]{2,1,0:T(8,128)(2,1)} %bitcast.16), custom_call_target="tpu_custom_call" | custom-call | bytes 8388608 | tf_op jit(solution)/shard_map/pick_rows/pallas_call | solution.py:59
  92.1 5.5 %query_gradient.5 = bf16[512,256]{1,0:T(8,128)(2,1)} custom-call(s32[16]{0:T(128)} %copy-done.5, bf16[32,32,512]{2,1,0:T(8,128)(2,1)} %copy-done.1, bf16[32,32,512]{2,1,0:T(8,128)(2,1)} %copy-done.1, bf16[32,32,512]{2,1,0:T(8,128)(2,1)} %copy-done.1, bf16[32,32,512]{2,1,0:T(8,128)(2,1)} %copy-done.1, bf16[32,32,512]{2,1,0:T(8,128)(2,1)} %copy-done.1, ...), custom_call_target="tpu_custom_call" | custom-call | flops 50331648 | bytes 1310720 | tf_op jit(solution)/shard_map/query_gradient/pallas_call | solution.py:137
  97.6 36.9 %collective-permute-done.1.refs_11_ = f32[1,4096]{1,0:T(1,128)S(1)} collective-permute-done((f32[1,4096]{1,0:T(1,128)S(1)}, f32[1,4096]{1,0:T(1,128)S(1)}, u32[]{:S(2)}, u32[]{:S(2)}) %collective-permute-start.1) | collective-permute-done | bytes 16416 | tf_op jit(solution)/shard_map/ppermute | solution.py:26
  135.9 8.6 %all-to-all-start.3 = ((bf16[32,32,2048]{2,1,0:T(8,128)(2,1)}), bf16[32,32,2048]{2,1,0:T(8,128)(2,1)}, u32[]{:S(2)}, u32[]{:S(2)}) async-start(bf16[32,32,2048]{2,1,0:T(8,128)(2,1)} %pick_rows.6), calls=%async_computation.3 | async-start | bytes 8388608 | tf_op jit(solution)/shard_map/all_to_all | solution.py:312
  148.1 7.4 %query_gradient.6 = bf16[512,512]{1,0:T(8,128)(2,1)} custom-call(s32[16]{0:T(128)} %copy-done.5, bf16[32,32,1024]{2,1,0:T(8,128)(2,1)} %copy-done, bf16[32,32,1024]{2,1,0:T(8,128)(2,1)} %copy-done, bf16[32,32,1024]{2,1,0:T(8,128)(2,1)} %copy-done, bf16[32,32,1024]{2,1,0:T(8,128)(2,1)} %copy-done, bf16[32,32,1024]{2,1,0:T(8,128)(2,1)} %copy-done, ...), custom_call_target="tpu_custom_call" | custom-call | flops 100663296 | bytes 2621440 | tf_op jit(solution)/shard_map/query_gradient/pallas_call | solution.py:137
  156.3 4.3 %pick_rows.7 = bf16[32,32,512]{2,1,0:T(8,128)(2,1)} custom-call(s32[32]{0:T(128)} %reduce.picks, bf16[16,32,4096]{2,1,0:T(8,128)(2,1)} %bitcast.17), custom_call_target="tpu_custom_call" | custom-call | bytes 2097152 | tf_op jit(solution)/shard_map/pick_rows/pallas_call | solution.py:59
  160.6 34.4 %collective-permute-done.8.refs_0_ = bf16[512,256]{1,0:T(8,128)(2,1)S(1)} collective-permute-done((bf16[512,256]{1,0:T(8,128)(2,1)S(1)}, bf16[512,256]{1,0:T(8,128)(2,1)S(1)}, u32[]{:S(2)}, u32[]{:S(2)}) %collective-permute-start.8) | collective-permute-done | bytes 262176 | tf_op jit(solution)/shard_map/ppermute | solution.py:26
  195.8 7.0 %all-to-all-start.4 = ((bf16[32,32,512]{2,1,0:T(8,128)(2,1)}), bf16[32,32,512]{2,1,0:T(8,128)(2,1)S(1)}, u32[]{:S(2)}, u32[]{:S(2)}) async-start(bf16[32,32,512]{2,1,0:T(8,128)(2,1)} %pick_rows.7), calls=%async_computation.4 | async-start | bytes 2097152 | tf_op jit(solution)/shard_map/all_to_all | solution.py:312
  202.8 7.4 %query_gradient.7 = bf16[512,512]{1,0:T(8,128)(2,1)} custom-call(s32[16]{0:T(128)} %copy-done.5, bf16[32,32,2048]{2,1,0:T(8,128)(2,1)} %all-to-all-done.3.refs_0_.refs_1_.refs_2_.refs_3_.refs_4_.refs_5_.refs_6_.refs_7_, bf16[32,32,2048]{2,1,0:T(8,128)(2,1)} %all-to-all-done.3.refs_0_.refs_1_.refs_2_.refs_3_.refs_4_.refs_5_.refs_6_.refs_7_, ...), custom_call_target="tpu_custom_call" | custom-call | flops 100663296 | bytes 2621440 | tf_op jit(solution)/shard_map/query_gradient/pallas_call | solution.py:137
  210.8 7.4 %query_gradient.8 = bf16[512,512]{1,0:T(8,128)(2,1)} custom-call(s32[16]{0:T(128)} %copy-done.5, bf16[32,32,2048]{2,1,0:T(8,128)(2,1)} %all-to-all-done.3.refs_0_.refs_1_.refs_2_.refs_3_.refs_4_.refs_5_.refs_6_.refs_7_, bf16[32,32,2048]{2,1,0:T(8,128)(2,1)} %all-to-all-done.3.refs_0_.refs_1_.refs_2_.refs_3_.refs_4_.refs_5_.refs_6_.refs_7_, ...), custom_call_target="tpu_custom_call" | custom-call | flops 100663296 | bytes 2621440 | tf_op jit(solution)/shard_map/query_gradient/pallas_call | solution.py:137
  218.5 8.1 %collective-permute-done.10.refs_2_ = bf16[512,512]{1,0:T(8,128)(2,1)} collective-permute-done((bf16[512,512]{1,0:T(8,128)(2,1)}, bf16[512,512]{1,0:T(8,128)(2,1)}, u32[]{:S(2)}, u32[]{:S(2)}) %collective-permute-start.10) | collective-permute-done | bytes 524320 | tf_op jit(solution)/shard_map/ppermute | solution.py:26
  227.6 5.5 %query_gradient.9 = bf16[512,256]{1,0:T(8,128)(2,1)} custom-call(s32[16]{0:T(128)} %copy-done.5, bf16[32,32,512]{2,1,0:T(8,128)(2,1)} %copy-done.2, bf16[32,32,512]{2,1,0:T(8,128)(2,1)} %copy-done.2, bf16[32,32,512]{2,1,0:T(8,128)(2,1)} %copy-done.2, bf16[32,32,512]{2,1,0:T(8,128)(2,1)} %copy-done.2, bf16[32,32,512]{2,1,0:T(8,128)(2,1)} %copy-done.2, ...), custom_call_target="tpu_custom_call" | custom-call | flops 50331648 | bytes 1310720 | tf_op jit(solution)/shard_map/query_gradient/pallas_call | solution.py:137
  233.1 4.6 %collective-permute-done.11.refs_3_ = bf16[512,512]{1,0:T(8,128)(2,1)S(1)} collective-permute-done((bf16[512,512]{1,0:T(8,128)(2,1)}, bf16[512,512]{1,0:T(8,128)(2,1)S(1)}, u32[]{:S(2)}, u32[]{:S(2)}) %collective-permute-start.11) | collective-permute-done | bytes 524320 | tf_op jit(solution)/shard_map/ppermute | solution.py:26
  237.7 4.8 %collective-permute-done.12.refs_4_ = bf16[512,256]{1,0:T(8,128)(2,1)S(1)} collective-permute-done((bf16[512,256]{1,0:T(8,128)(2,1)}, bf16[512,256]{1,0:T(8,128)(2,1)S(1)}, u32[]{:S(2)}, u32[]{:S(2)}) %collective-permute-start.12) | collective-permute-done | bytes 262176 | tf_op jit(solution)/shard_map/ppermute | solution.py:26
  243.3 22.1 %finish.1 = bf16[512,4096]{1,0:T(8,128)(2,1)} custom-call(s32[1]{0:T(128)} %bitcast.2.core, bf16[512,256]{1,0:T(8,128)(2,1)} %copy-done.8, bf16[512,512]{1,0:T(8,128)(2,1)} %collective-permute-done.9.refs_1_, bf16[512,512]{1,0:T(8,128)(2,1)} %collective-permute-done.10.refs_2_, bf16[512,512]{1,0:T(8,128)(2,1)} %copy-done.7, bf16[512,256]{1,0:T(8,128)(2,1)} %copy-done.9, ...), custom_call_target="tpu_custom_call" | custom-call | flops 8589934592 | bytes 33554432 | tf_op jit(solution)/shard_map/finish/pallas_call | solution.py:262
  (62 shorter events, 23.6 us)
Async XLA Ops:
  6.5 189.3 %all-gather.2.cloned.1.call-start = ((), (), s32[]{:S(2)}) async-start(), calls=%async_computation.5 | async-start | bytes 8912896 | tf_op jit(solution)/shard_map/all_gather | solution.py:332
  6.5 15.1 %collective-permute-start = (bf16[128,2048]{1,0:T(8,128)(2,1)}, bf16[128,2048]{1,0:T(8,128)(2,1)S(1)}, u32[]{:S(2)}, u32[]{:S(2)}) collective-permute-start(bf16[128,2048]{1,0:T(8,128)(2,1)} %bitcast.30), channel_id=1, source_target_pairs={{0,3},{1,0},{2,1},{3,2},{4,7},{5,4},{6,5},{7,6},{8,11},{9,8},{10,9... | collective-permute-start | bytes 1572872 | tf_op jit(solution)/shard_map/ppermute | solution.py:26
  8.2 19.2 %copy-start.5 = (s32[16]{0:T(128)}, s32[16]{0:T(128)S(1)}, u32[]{:S(2)}) copy-start(s32[16]{0:T(128)S(1)} %eq.15.owners) | copy-start | bytes 196
  25.7 53.5 %collective-permute-start.4 = (bf16[272,4096]{1,0:T(8,128)(2,1)}, bf16[272,4096]{1,0:T(8,128)(2,1)}, u32[]{:S(2)}, u32[]{:S(2)}) collective-permute-start(bf16[272,4096]{1,0:T(8,128)(2,1)} %slice_bitcast_fusion.1), channel_id=1, source_target_pairs={{0,1},{1,2},{2,3},{3,0},{4,5},{5,6},{6,7},{7,4},{8,9},{9,10},{10,1... | collective-permute-start | bytes 6684680 | tf_op jit(solution)/shard_map/ppermute | solution.py:26
  27.4 51.8 %collective-permute-start.3 = (bf16[240,4096]{1,0:T(8,128)(2,1)S(1)}, bf16[240,4096]{1,0:T(8,128)(2,1)}, u32[]{:S(2)}, u32[]{:S(2)}) collective-permute-start(bf16[240,4096]{1,0:T(8,128)(2,1)S(1)} %slice_bitcast_fusion.2), channel_id=1, source_target_pairs={{0,3},{1,0},{2,1},{3,2},{4,7},{5,4},{6,5},{7,6},{8,11},{9,8},{10,9... | collective-permute-start | bytes 5898248 | tf_op jit(solution)/shard_map/ppermute | solution.py:26
  30.1 14.7 %all-to-all-start = ((s32[32,1,1]{2,1,0:T(1,128)}), s32[32,1,1]{2,1,0:T(1,128)S(1)}, u32[]{:S(2)}, u32[]{:S(2)}) async-start(s32[32,1,1]{2,1,0:T(1,128)} %copy.22), calls=%async_computation | async-start | bytes 32768 | tf_op jit(solution)/shard_map/all_to_all | solution.py:333
  49.7 29.4 %all-to-all-start.1 = ((bf16[32,32,512]{2,1,0:T(8,128)(2,1)}), bf16[32,32,512]{2,1,0:T(8,128)(2,1)S(1)}, u32[]{:S(2)}, u32[]{:S(2)}) async-start(bf16[32,32,512]{2,1,0:T(8,128)(2,1)} %pick_rows.4), calls=%async_computation.1 | async-start | bytes 2097152 | tf_op jit(solution)/shard_map/all_to_all | solution.py:312
  58.7 75.7 %collective-permute-start.2 = (bf16[352,4096]{1,0:T(8,128)(2,1)}, bf16[352,4096]{1,0:T(8,128)(2,1)}, u32[]{:S(2)}, u32[]{:S(2)}) collective-permute-start(bf16[352,4096]{1,0:T(8,128)(2,1)} %slice_bitcast_fusion), channel_id=1, source_target_pairs={{0,3},{1,0},{2,1},{3,2},{4,7},{5,4},{6,5},{7,6},{8,11},{9,8},{10,9... | collective-permute-start | bytes 8650760 | tf_op jit(solution)/shard_map/ppermute | solution.py:26
  63.2 23.6 %copy-start.10 = (f32[1,4096]{1,0:T(1,128)S(1)}, f32[1,4096]{1,0:T(1,128)}, u32[]{:S(2)}) copy-start(f32[1,4096]{1,0:T(1,128)} %param.10) | copy-start | bytes 49156
  79.1 55.4 %collective-permute-start.5 = (bf16[272,4096]{1,0:T(8,128)(2,1)}, bf16[272,4096]{1,0:T(8,128)(2,1)}, u32[]{:S(2)}, u32[]{:S(2)}) collective-permute-start(bf16[272,4096]{1,0:T(8,128)(2,1)} %collective-permute-done.4), channel_id=1, source_target_pairs={{0,1},{1,2},{2,3},{3,0},{4,5},{5,6},{6,7},{7,4},{8,9},{9,10},{10,1... | collective-permute-start | bytes 6684680 | tf_op jit(solution)/shard_map/ppermute | solution.py:26
  81.1 53.4 %all-to-all-start.2 = ((bf16[32,32,1024]{2,1,0:T(8,128)(2,1)}), bf16[32,32,1024]{2,1,0:T(8,128)(2,1)S(1)}, u32[]{:S(2)}, u32[]{:S(2)}) async-start(bf16[32,32,1024]{2,1,0:T(8,128)(2,1)} %pick_rows.5), calls=%async_computation.2 | async-start | bytes 4194304 | tf_op jit(solution)/shard_map/all_to_all | solution.py:312
  86.8 47.7 %collective-permute-start.1 = (f32[1,4096]{1,0:T(1,128)S(1)}, f32[1,4096]{1,0:T(1,128)S(1)}, u32[]{:S(2)}, u32[]{:S(2)}) collective-permute-start(f32[1,4096]{1,0:T(1,128)S(1)} %copy-done.10), channel_id=1, source_target_pairs={{0,3},{1,0},{2,1},{3,2},{4,7},{5,4},{6,5},{7,6},{8,11},{9,8},{10,9... | collective-permute-start | bytes 49160 | tf_op jit(solution)/shard_map/ppermute | solution.py:26
  135.9 60.0 %all-to-all-start.3 = ((bf16[32,32,2048]{2,1,0:T(8,128)(2,1)}), bf16[32,32,2048]{2,1,0:T(8,128)(2,1)}, u32[]{:S(2)}, u32[]{:S(2)}) async-start(bf16[32,32,2048]{2,1,0:T(8,128)(2,1)} %pick_rows.6), calls=%async_computation.3 | async-start | bytes 8388608 | tf_op jit(solution)/shard_map/all_to_all | solution.py:312
  144.5 50.8 %collective-permute-start.7 = (bf16[272,4096]{1,0:T(8,128)(2,1)}, bf16[272,4096]{1,0:T(8,128)(2,1)S(1)}, u32[]{:S(2)}, u32[]{:S(2)}) collective-permute-start(bf16[272,4096]{1,0:T(8,128)(2,1)} %collective-permute-done.5), channel_id=1, source_target_pairs={{0,1},{1,2},{2,3},{3,0},{4,5},{5,6},{6,7},{7,4},{8,9},{9,10},{10,1... | collective-permute-start | bytes 6684680 | tf_op jit(solution)/shard_map/ppermute | solution.py:26
  146.0 49.0 %collective-permute-start.6 = (bf16[160,4096]{1,0:T(8,128)(2,1)S(1)}, bf16[160,4096]{1,0:T(8,128)(2,1)}, u32[]{:S(2)}, u32[]{:S(2)}) collective-permute-start(bf16[160,4096]{1,0:T(8,128)(2,1)S(1)} %slice.27), channel_id=1, source_target_pairs={{0,3},{1,0},{2,1},{3,2},{4,7},{5,4},{6,5},{7,6},{8,11},{9,8},{10,9... | collective-permute-start | bytes 3932168 | tf_op jit(solution)/shard_map/ppermute | solution.py:26
  155.4 39.5 %collective-permute-start.9 = (bf16[512,512]{1,0:T(8,128)(2,1)}, bf16[512,512]{1,0:T(8,128)(2,1)}, u32[]{:S(2)}, u32[]{:S(2)}) collective-permute-start(bf16[512,512]{1,0:T(8,128)(2,1)} %query_gradient.6), channel_id=1, source_target_pairs={{0,3},{1,0},{2,1},{3,2},{4,7},{5,4},{6,5},{7,6},{8,11},{9,8},{10,9... | collective-permute-start | bytes 1572872 | tf_op jit(solution)/shard_map/ppermute | solution.py:26
  156.0 39.0 %collective-permute-start.8 = (bf16[512,256]{1,0:T(8,128)(2,1)S(1)}, bf16[512,256]{1,0:T(8,128)(2,1)S(1)}, u32[]{:S(2)}, u32[]{:S(2)}) collective-permute-start(bf16[512,256]{1,0:T(8,128)(2,1)S(1)} %copy-done.4), channel_id=1, source_target_pairs={{0,3},{1,0},{2,1},{3,2},{4,7},{5,4},{6,5},{7,6},{8,11},{9,8},{10,9... | collective-permute-start | bytes 786440 | tf_op jit(solution)/shard_map/ppermute | solution.py:26
  195.0 15.3 %copy-start.8 = (bf16[512,256]{1,0:T(8,128)(2,1)}, bf16[512,256]{1,0:T(8,128)(2,1)S(1)}, u32[]{:S(2)}) copy-start(bf16[512,256]{1,0:T(8,128)(2,1)S(1)} %collective-permute-done.8.refs_0_) | copy-start | bytes 786436
  195.2 15.0 %copy-start.6 = (bf16[272,4096]{1,0:T(8,128)(2,1)}, bf16[272,4096]{1,0:T(8,128)(2,1)S(1)}, u32[]{:S(2)}) copy-start(bf16[272,4096]{1,0:T(8,128)(2,1)S(1)} %collective-permute-done.7.refs_6_) | copy-start | bytes 6684676
  195.8 46.7 %collective-permute-start.13 = (bf16[2048,2048]{1,0:T(8,128)(2,1)}, bf16[2048,2048]{1,0:T(8,128)(2,1)}, u32[]{:S(2)}, u32[]{:S(2)}) collective-permute-start(bf16[2048,2048]{1,0:T(8,128)(2,1)} %all-gather.2.cloned.1.call-done.refs_9_), channel_id=1, source_target_pairs={{0,4},{4,0},{8,12},{12,8},{16,20},{20,16},{24,28},{28,24},{32,36},... | collective-permute-start | bytes 25165832 | tf_op jit(solution)/shard_map/ppermute | solution.py:365
  195.8 30.8 %all-to-all-start.4 = ((bf16[32,32,512]{2,1,0:T(8,128)(2,1)}), bf16[32,32,512]{2,1,0:T(8,128)(2,1)S(1)}, u32[]{:S(2)}, u32[]{:S(2)}) async-start(bf16[32,32,512]{2,1,0:T(8,128)(2,1)} %pick_rows.7), calls=%async_computation.4 | async-start | bytes 2097152 | tf_op jit(solution)/shard_map/all_to_all | solution.py:312
  210.2 16.4 %collective-permute-start.10 = (bf16[512,512]{1,0:T(8,128)(2,1)}, bf16[512,512]{1,0:T(8,128)(2,1)}, u32[]{:S(2)}, u32[]{:S(2)}) collective-permute-start(bf16[512,512]{1,0:T(8,128)(2,1)} %query_gradient.7), channel_id=1, source_target_pairs={{0,3},{1,0},{2,1},{3,2},{4,7},{5,4},{6,5},{7,6},{8,11},{9,8},{10,9... | collective-permute-start | bytes 1572872 | tf_op jit(solution)/shard_map/ppermute | solution.py:26
  218.2 19.5 %collective-permute-start.11 = (bf16[512,512]{1,0:T(8,128)(2,1)}, bf16[512,512]{1,0:T(8,128)(2,1)S(1)}, u32[]{:S(2)}, u32[]{:S(2)}) collective-permute-start(bf16[512,512]{1,0:T(8,128)(2,1)} %query_gradient.8), channel_id=1, source_target_pairs={{0,3},{1,0},{2,1},{3,2},{4,7},{5,4},{6,5},{7,6},{8,11},{9,8},{10,9... | collective-permute-start | bytes 1572872 | tf_op jit(solution)/shard_map/ppermute | solution.py:26
  233.1 9.4 %collective-permute-start.12 = (bf16[512,256]{1,0:T(8,128)(2,1)}, bf16[512,256]{1,0:T(8,128)(2,1)S(1)}, u32[]{:S(2)}, u32[]{:S(2)}) collective-permute-start(bf16[512,256]{1,0:T(8,128)(2,1)} %query_gradient.9), channel_id=1, source_target_pairs={{0,3},{1,0},{2,1},{3,2},{4,7},{5,4},{6,5},{7,6},{8,11},{9,8},{10,9... | collective-permute-start | bytes 786440 | tf_op jit(solution)/shard_map/ppermute | solution.py:26
  (8 other events, 32.2 us)
Sparse Core Ops, SparseCore 0:
  22.6 102.7 all-gather.1

commit v6 on v5

--- a/solution.py
+++ b/solution.py
@@ -356,7 +356,7 @@
     )
     held = fetched
     local2 = query_gradient(owners, held, queries[0], grad_heads[0], 8 * HEAD_DIM, 4)
-    fetched = exchanged(rows)
+    fetched = exchanged(after(rows, local2))
     part2 = back(local2)
     local3 = query_gradient(
         owners, after(held, local2), queries[0], grad_heads[0], 12 * HEAD_DIM, 4, 4 * HEAD_DIM

time: 274 us -> 275 us (level)
  transfers between devices with their start and end apart: 20 -> 20, of which waited for: 10 -> 10; matrix products, arithmetic and copies ran while one was open for 5% -> 5% of each run, Pallas kernels for 19% -> 18%
where the time goes in v6:
time: 275 us; the launch traced here: 272 us
  waiting for transfers between devices  124 us (45%)
  Pallas kernels  72.4 us (26%)
  starting transfers between devices  44.4 us (16%)
  local copies, waits for them, and re-layouts  16.4 us (6%)
  between operations  13.6 us (5%)
    ppermute x13, waiting for transfers between devices, passed_along(): return lax.ppermute(value, axis, pairs)  102 us
    pallas_call x5, Pallas kernels, query_gradient(): pl.pallas_call(functools.partial(attention_kernel, heads), out_shape=jax....  33.2 us
    all_to_all x4, starting transfers between devices, exchanged(): lax.all_to_all(rows, 'stretch', split_axis=0, concat_axis=0, tiled=True)  26.6 us
    pallas_call x1, Pallas kernels, finished(): pl.pallas_call(functools.partial(finish_kernel, widths, tuple(map(len, (p...  22.1 us
    pallas_call x4, Pallas kernels, picked_rows(): pl.pallas_call(functools.partial(pick_kernel, first, qwidth + first, widt...  17.1 us
    all_to_all x4, waiting for transfers between devices, exchanged(): lax.all_to_all(rows, 'stretch', split_axis=0, concat_axis=0, tiled=True)  16.6 us
    ppermute x13, starting transfers between devices, passed_along(): return lax.ppermute(value, axis, pairs)  9.26 us
    all_to_all x1, starting transfers between devices, local(): lax.all_to_all(wanted, 'stretch', split_axis=0, concat_axis=0, tiled=True)  8.55 us
  transfers between devices with their start and end apart: 20, of which 10 were waited for; matrix products, arithmetic and copies ran while one was open for 5% of the time, Pallas kernels for 18%

profile of v6, /device:TPU:14, one launch (start us, length us, event | category | flops | bytes accessed | tf_op | source)
XLA Modules:
  0.0 272.3 jit_solution(10942435129488232096)
XLA Ops:
  9.1 12.5 %collective-permute-done = bf16[128,2048]{1,0:T(8,128)(2,1)S(1)} collective-permute-done((bf16[128,2048]{1,0:T(8,128)(2,1)}, bf16[128,2048]{1,0:T(8,128)(2,1)S(1)}, u32[]{:S(2)}, u32[]{:S(2)}) %collective-permute-start) | collective-permute-done | bytes 524320 | tf_op jit(solution)/shard_map/ppermute | solution.py:26
  30.1 8.5 %all-to-all-start = ((s32[32,1,1]{2,1,0:T(1,128)}), s32[32,1,1]{2,1,0:T(1,128)S(1)}, u32[]{:S(2)}, u32[]{:S(2)}) async-start(s32[32,1,1]{2,1,0:T(1,128)} %copy.22), calls=%async_computation | async-start | bytes 32768 | tf_op jit(solution)/shard_map/all_to_all | solution.py:333
  38.7 6.2 %all-to-all-done = s32[32,1,1]{2,1,0:T(1,128)S(1)} async-done(((s32[32,1,1]{2,1,0:T(1,128)}), s32[32,1,1]{2,1,0:T(1,128)S(1)}, u32[]{:S(2)}, u32[]{:S(2)}) %all-to-all-start) | async-done | bytes 160 | tf_op jit(solution)/shard_map/all_to_all | solution.py:333
  46.0 3.6 %pick_rows.4 = bf16[32,32,512]{2,1,0:T(8,128)(2,1)} custom-call(s32[32]{0:T(128)} %reduce.picks, bf16[16,32,4096]{2,1,0:T(8,128)(2,1)} %bitcast.14), custom_call_target="tpu_custom_call" | custom-call | bytes 2097152 | tf_op jit(solution)/shard_map/pick_rows/pallas_call | solution.py:59
  49.7 5.3 %all-to-all-start.1 = ((bf16[32,32,512]{2,1,0:T(8,128)(2,1)}), bf16[32,32,512]{2,1,0:T(8,128)(2,1)S(1)}, u32[]{:S(2)}, u32[]{:S(2)}) async-start(bf16[32,32,512]{2,1,0:T(8,128)(2,1)} %pick_rows.4), calls=%async_computation.1 | async-start | bytes 2097152 | tf_op jit(solution)/shard_map/all_to_all | solution.py:312
  55.0 3.8 %slice_bitcast_fusion = bf16[352,4096]{1,0:T(8,128)(2,1)} fusion(bf16[1,512,4096]{2,1,0:T(8,128)(2,1)} %param.16), kind=kLoop, calls=%fused_computation | loop fusion | bytes 5767168 | tf_op jit(solution)/shard_map/slice | solution.py:329
  58.8 4.3 %pick_rows.5 = bf16[32,32,1024]{2,1,0:T(8,128)(2,1)} custom-call(s32[32]{0:T(128)} %reduce.picks, bf16[16,32,4096]{2,1,0:T(8,128)(2,1)} %bitcast.15), custom_call_target="tpu_custom_call" | custom-call | bytes 4194304 | tf_op jit(solution)/shard_map/pick_rows/pallas_call | solution.py:59
  63.2 16.0 %all-to-all-done.1.refs_0_.refs_1_.refs_2_.refs_3_.refs_4_.refs_5_.refs_6_.refs_7_ = bf16[32,32,512]{2,1,0:T(8,128)(2,1)S(1)} async-done(((bf16[32,32,512]{2,1,0:T(8,128)(2,1)}), bf16[32,32,512]{2,1,0:T(8,128)(2,1)S(1)}, u32[]{:S(2)}, u32[]{:S(2)}) %all-to-all-start.1) | async-done | bytes 1048608 | tf_op jit(solution)/shard_map/all_to_all | solution.py:312
  81.2 5.6 %all-to-all-start.2 = ((bf16[32,32,1024]{2,1,0:T(8,128)(2,1)}), bf16[32,32,1024]{2,1,0:T(8,128)(2,1)S(1)}, u32[]{:S(2)}, u32[]{:S(2)}) async-start(bf16[32,32,1024]{2,1,0:T(8,128)(2,1)} %pick_rows.5), calls=%async_computation.2 | async-start | bytes 4194304 | tf_op jit(solution)/shard_map/all_to_all | solution.py:312
  87.0 5.1 %pick_rows.6 = bf16[32,32,2048]{2,1,0:T(8,128)(2,1)} custom-call(s32[32]{0:T(128)} %reduce.picks, bf16[16,32,4096]{2,1,0:T(8,128)(2,1)} %bitcast.16), custom_call_target="tpu_custom_call" | custom-call | bytes 8388608 | tf_op jit(solution)/shard_map/pick_rows/pallas_call | solution.py:59
  92.1 5.5 %query_gradient.5 = bf16[512,256]{1,0:T(8,128)(2,1)} custom-call(s32[16]{0:T(128)} %copy-done.5, bf16[32,32,512]{2,1,0:T(8,128)(2,1)} %copy-done.1, bf16[32,32,512]{2,1,0:T(8,128)(2,1)} %copy-done.1, bf16[32,32,512]{2,1,0:T(8,128)(2,1)} %copy-done.1, bf16[32,32,512]{2,1,0:T(8,128)(2,1)} %copy-done.1, bf16[32,32,512]{2,1,0:T(8,128)(2,1)} %copy-done.1, ...), custom_call_target="tpu_custom_call" | custom-call | flops 50331648 | bytes 1310720 | tf_op jit(solution)/shard_map/query_gradient/pallas_call | solution.py:137
  97.6 36.9 %collective-permute-done.1.refs_11_ = f32[1,4096]{1,0:T(1,128)S(1)} collective-permute-done((f32[1,4096]{1,0:T(1,128)S(1)}, f32[1,4096]{1,0:T(1,128)S(1)}, u32[]{:S(2)}, u32[]{:S(2)}) %collective-permute-start.1) | collective-permute-done | bytes 16416 | tf_op jit(solution)/shard_map/ppermute | solution.py:26
  135.9 8.6 %all-to-all-start.3 = ((bf16[32,32,2048]{2,1,0:T(8,128)(2,1)}), bf16[32,32,2048]{2,1,0:T(8,128)(2,1)}, u32[]{:S(2)}, u32[]{:S(2)}) async-start(bf16[32,32,2048]{2,1,0:T(8,128)(2,1)} %pick_rows.6), calls=%async_computation.3 | async-start | bytes 8388608 | tf_op jit(solution)/shard_map/all_to_all | solution.py:312
  148.1 7.4 %query_gradient.6 = bf16[512,512]{1,0:T(8,128)(2,1)} custom-call(s32[16]{0:T(128)} %copy-done.5, bf16[32,32,1024]{2,1,0:T(8,128)(2,1)} %copy-done, bf16[32,32,1024]{2,1,0:T(8,128)(2,1)} %copy-done, bf16[32,32,1024]{2,1,0:T(8,128)(2,1)} %copy-done, bf16[32,32,1024]{2,1,0:T(8,128)(2,1)} %copy-done, bf16[32,32,1024]{2,1,0:T(8,128)(2,1)} %copy-done, ...), custom_call_target="tpu_custom_call" | custom-call | flops 100663296 | bytes 2621440 | tf_op jit(solution)/shard_map/query_gradient/pallas_call | solution.py:137
  156.3 4.0 %pick_rows.7 = bf16[32,32,512]{2,1,0:T(8,128)(2,1)} custom-call(s32[32]{0:T(128)} %reduce.picks, bf16[16,32,4096]{2,1,0:T(8,128)(2,1)} %bitcast.17), custom_call_target="tpu_custom_call" | custom-call | bytes 2097152 | tf_op jit(solution)/shard_map/pick_rows/pallas_call | solution.py:59
  160.3 34.6 %collective-permute-done.8.refs_0_ = bf16[512,256]{1,0:T(8,128)(2,1)S(1)} collective-permute-done((bf16[512,256]{1,0:T(8,128)(2,1)S(1)}, bf16[512,256]{1,0:T(8,128)(2,1)S(1)}, u32[]{:S(2)}, u32[]{:S(2)}) %collective-permute-start.8) | collective-permute-done | bytes 262176 | tf_op jit(solution)/shard_map/ppermute | solution.py:26
  195.8 7.4 %query_gradient.7 = bf16[512,512]{1,0:T(8,128)(2,1)} custom-call(s32[16]{0:T(128)} %copy-done.5, bf16[32,32,2048]{2,1,0:T(8,128)(2,1)} %all-to-all-done.3.refs_0_.refs_1_.refs_2_.refs_3_.refs_4_.refs_5_.refs_6_.refs_7_, bf16[32,32,2048]{2,1,0:T(8,128)(2,1)} %all-to-all-done.3.refs_0_.refs_1_.refs_2_.refs_3_.refs_4_.refs_5_.refs_6_.refs_7_, ...), custom_call_target="tpu_custom_call" | custom-call | flops 100663296 | bytes 2621440 | tf_op jit(solution)/shard_map/query_gradient/pallas_call | solution.py:137
  203.2 7.0 %all-to-all-start.4 = ((bf16[32,32,512]{2,1,0:T(8,128)(2,1)}), bf16[32,32,512]{2,1,0:T(8,128)(2,1)S(1)}, u32[]{:S(2)}, u32[]{:S(2)}) async-start(bf16[32,32,512]{2,1,0:T(8,128)(2,1)} %pick_rows.7), calls=%async_computation.4 | async-start | bytes 2097152 | tf_op jit(solution)/shard_map/all_to_all | solution.py:312
  210.8 7.4 %query_gradient.8 = bf16[512,512]{1,0:T(8,128)(2,1)} custom-call(s32[16]{0:T(128)} %copy-done.5, bf16[32,32,2048]{2,1,0:T(8,128)(2,1)} %all-to-all-done.3.refs_0_.refs_1_.refs_2_.refs_3_.refs_4_.refs_5_.refs_6_.refs_7_, bf16[32,32,2048]{2,1,0:T(8,128)(2,1)} %all-to-all-done.3.refs_0_.refs_1_.refs_2_.refs_3_.refs_4_.refs_5_.refs_6_.refs_7_, ...), custom_call_target="tpu_custom_call" | custom-call | flops 100663296 | bytes 2621440 | tf_op jit(solution)/shard_map/query_gradient/pallas_call | solution.py:137
  218.5 8.0 %collective-permute-done.10.refs_2_ = bf16[512,512]{1,0:T(8,128)(2,1)S(1)} collective-permute-done((bf16[512,512]{1,0:T(8,128)(2,1)}, bf16[512,512]{1,0:T(8,128)(2,1)S(1)}, u32[]{:S(2)}, u32[]{:S(2)}) %collective-permute-start.10) | collective-permute-done | bytes 524320 | tf_op jit(solution)/shard_map/ppermute | solution.py:26
  227.5 5.5 %query_gradient.9 = bf16[512,256]{1,0:T(8,128)(2,1)} custom-call(s32[16]{0:T(128)} %copy-done.5, bf16[32,32,512]{2,1,0:T(8,128)(2,1)} %copy-done.2, bf16[32,32,512]{2,1,0:T(8,128)(2,1)} %copy-done.2, bf16[32,32,512]{2,1,0:T(8,128)(2,1)} %copy-done.2, bf16[32,32,512]{2,1,0:T(8,128)(2,1)} %copy-done.2, bf16[32,32,512]{2,1,0:T(8,128)(2,1)} %copy-done.2, ...), custom_call_target="tpu_custom_call" | custom-call | flops 50331648 | bytes 1310720 | tf_op jit(solution)/shard_map/query_gradient/pallas_call | solution.py:137
  233.4 3.5 %collective-permute-done.11.refs_3_ = bf16[512,512]{1,0:T(8,128)(2,1)S(1)} collective-permute-done((bf16[512,512]{1,0:T(8,128)(2,1)}, bf16[512,512]{1,0:T(8,128)(2,1)S(1)}, u32[]{:S(2)}, u32[]{:S(2)}) %collective-permute-start.11) | collective-permute-done | bytes 524320 | tf_op jit(solution)/shard_map/ppermute | solution.py:26
  236.9 5.7 %collective-permute-done.12.refs_4_ = bf16[512,256]{1,0:T(8,128)(2,1)S(1)} collective-permute-done((bf16[512,256]{1,0:T(8,128)(2,1)}, bf16[512,256]{1,0:T(8,128)(2,1)S(1)}, u32[]{:S(2)}, u32[]{:S(2)}) %collective-permute-start.12) | collective-permute-done | bytes 262176 | tf_op jit(solution)/shard_map/ppermute | solution.py:26
  243.4 22.1 %finish.1 = bf16[512,4096]{1,0:T(8,128)(2,1)} custom-call(s32[1]{0:T(128)} %bitcast.2.core, bf16[512,256]{1,0:T(8,128)(2,1)} %copy-done.9, bf16[512,512]{1,0:T(8,128)(2,1)} %collective-permute-done.9.refs_1_, bf16[512,512]{1,0:T(8,128)(2,1)} %copy-done.7, bf16[512,512]{1,0:T(8,128)(2,1)} %copy-done.8, bf16[512,256]{1,0:T(8,128)(2,1)} %copy-done.10, ...), custom_call_target="tpu_custom_call" | custom-call | flops 8589934592 | bytes 33554432 | tf_op jit(solution)/shard_map/finish/pallas_call | solution.py:262
  (64 shorter events, 24.0 us)
Async XLA Ops:
  6.5 189.3 %all-gather.2.cloned.1.call-start = ((), (), s32[]{:S(2)}) async-start(), calls=%async_computation.5 | async-start | bytes 8912896 | tf_op jit(solution)/shard_map/all_gather | solution.py:332
  6.5 15.1 %collective-permute-start = (bf16[128,2048]{1,0:T(8,128)(2,1)}, bf16[128,2048]{1,0:T(8,128)(2,1)S(1)}, u32[]{:S(2)}, u32[]{:S(2)}) collective-permute-start(bf16[128,2048]{1,0:T(8,128)(2,1)} %bitcast.30), channel_id=1, source_target_pairs={{0,3},{1,0},{2,1},{3,2},{4,7},{5,4},{6,5},{7,6},{8,11},{9,8},{10,9... | collective-permute-start | bytes 1572872 | tf_op jit(solution)/shard_map/ppermute | solution.py:26
  8.2 19.1 %copy-start.5 = (s32[16]{0:T(128)}, s32[16]{0:T(128)S(1)}, u32[]{:S(2)}) copy-start(s32[16]{0:T(128)S(1)} %eq.15.owners) | copy-start | bytes 196
  25.7 53.6 %collective-permute-start.4 = (bf16[272,4096]{1,0:T(8,128)(2,1)}, bf16[272,4096]{1,0:T(8,128)(2,1)}, u32[]{:S(2)}, u32[]{:S(2)}) collective-permute-start(bf16[272,4096]{1,0:T(8,128)(2,1)} %slice_bitcast_fusion.1), channel_id=1, source_target_pairs={{0,1},{1,2},{2,3},{3,0},{4,5},{5,6},{6,7},{7,4},{8,9},{9,10},{10,1... | collective-permute-start | bytes 6684680 | tf_op jit(solution)/shard_map/ppermute | solution.py:26
  27.4 51.9 %collective-permute-start.3 = (bf16[240,4096]{1,0:T(8,128)(2,1)S(1)}, bf16[240,4096]{1,0:T(8,128)(2,1)}, u32[]{:S(2)}, u32[]{:S(2)}) collective-permute-start(bf16[240,4096]{1,0:T(8,128)(2,1)S(1)} %slice_bitcast_fusion.2), channel_id=1, source_target_pairs={{0,3},{1,0},{2,1},{3,2},{4,7},{5,4},{6,5},{7,6},{8,11},{9,8},{10,9... | collective-permute-start | bytes 5898248 | tf_op jit(solution)/shard_map/ppermute | solution.py:26
  30.1 14.7 %all-to-all-start = ((s32[32,1,1]{2,1,0:T(1,128)}), s32[32,1,1]{2,1,0:T(1,128)S(1)}, u32[]{:S(2)}, u32[]{:S(2)}) async-start(s32[32,1,1]{2,1,0:T(1,128)} %copy.22), calls=%async_computation | async-start | bytes 32768 | tf_op jit(solution)/shard_map/all_to_all | solution.py:333
  49.7 29.5 %all-to-all-start.1 = ((bf16[32,32,512]{2,1,0:T(8,128)(2,1)}), bf16[32,32,512]{2,1,0:T(8,128)(2,1)S(1)}, u32[]{:S(2)}, u32[]{:S(2)}) async-start(bf16[32,32,512]{2,1,0:T(8,128)(2,1)} %pick_rows.4), calls=%async_computation.1 | async-start | bytes 2097152 | tf_op jit(solution)/shard_map/all_to_all | solution.py:312
  58.8 75.7 %collective-permute-start.2 = (bf16[352,4096]{1,0:T(8,128)(2,1)}, bf16[352,4096]{1,0:T(8,128)(2,1)}, u32[]{:S(2)}, u32[]{:S(2)}) collective-permute-start(bf16[352,4096]{1,0:T(8,128)(2,1)} %slice_bitcast_fusion), channel_id=1, source_target_pairs={{0,3},{1,0},{2,1},{3,2},{4,7},{5,4},{6,5},{7,6},{8,11},{9,8},{10,9... | collective-permute-start | bytes 8650760 | tf_op jit(solution)/shard_map/ppermute | solution.py:26
  63.2 23.7 %copy-start.11 = (f32[1,4096]{1,0:T(1,128)S(1)}, f32[1,4096]{1,0:T(1,128)}, u32[]{:S(2)}) copy-start(f32[1,4096]{1,0:T(1,128)} %param.10) | copy-start | bytes 49156
  79.2 12.9 %copy-start.1 = (bf16[32,32,512]{2,1,0:T(8,128)(2,1)}, bf16[32,32,512]{2,1,0:T(8,128)(2,1)S(1)}, u32[]{:S(2)}) copy-start(bf16[32,32,512]{2,1,0:T(8,128)(2,1)S(1)} %all-to-all-done.1.refs_0_.refs_1_.refs_2_.refs_3_.refs_4_.refs_5_.refs_6_.refs_7_) | copy-start | bytes 3145732
  79.2 55.3 %collective-permute-start.5 = (bf16[272,4096]{1,0:T(8,128)(2,1)}, bf16[272,4096]{1,0:T(8,128)(2,1)}, u32[]{:S(2)}, u32[]{:S(2)}) collective-permute-start(bf16[272,4096]{1,0:T(8,128)(2,1)} %collective-permute-done.4), channel_id=1, source_target_pairs={{0,1},{1,2},{2,3},{3,0},{4,5},{5,6},{6,7},{7,4},{8,9},{9,10},{10,1... | collective-permute-start | bytes 6684680 | tf_op jit(solution)/shard_map/ppermute | solution.py:26
  81.2 53.3 %all-to-all-start.2 = ((bf16[32,32,1024]{2,1,0:T(8,128)(2,1)}), bf16[32,32,1024]{2,1,0:T(8,128)(2,1)S(1)}, u32[]{:S(2)}, u32[]{:S(2)}) async-start(bf16[32,32,1024]{2,1,0:T(8,128)(2,1)} %pick_rows.5), calls=%async_computation.2 | async-start | bytes 4194304 | tf_op jit(solution)/shard_map/all_to_all | solution.py:312
  86.9 47.6 %collective-permute-start.1 = (f32[1,4096]{1,0:T(1,128)S(1)}, f32[1,4096]{1,0:T(1,128)S(1)}, u32[]{:S(2)}, u32[]{:S(2)}) collective-permute-start(f32[1,4096]{1,0:T(1,128)S(1)} %copy-done.11), channel_id=1, source_target_pairs={{0,3},{1,0},{2,1},{3,2},{4,7},{5,4},{6,5},{7,6},{8,11},{9,8},{10,9... | collective-permute-start | bytes 49160 | tf_op jit(solution)/shard_map/ppermute | solution.py:26
  135.9 60.0 %all-to-all-start.3 = ((bf16[32,32,2048]{2,1,0:T(8,128)(2,1)}), bf16[32,32,2048]{2,1,0:T(8,128)(2,1)}, u32[]{:S(2)}, u32[]{:S(2)}) async-start(bf16[32,32,2048]{2,1,0:T(8,128)(2,1)} %pick_rows.6), calls=%async_computation.3 | async-start | bytes 8388608 | tf_op jit(solution)/shard_map/all_to_all | solution.py:312
  144.5 50.8 %collective-permute-start.7 = (bf16[272,4096]{1,0:T(8,128)(2,1)}, bf16[272,4096]{1,0:T(8,128)(2,1)S(1)}, u32[]{:S(2)}, u32[]{:S(2)}) collective-permute-start(bf16[272,4096]{1,0:T(8,128)(2,1)} %collective-permute-done.5), channel_id=1, source_target_pairs={{0,1},{1,2},{2,3},{3,0},{4,5},{5,6},{6,7},{7,4},{8,9},{9,10},{10,1... | collective-permute-start | bytes 6684680 | tf_op jit(solution)/shard_map/ppermute | solution.py:26
  146.0 49.0 %collective-permute-start.6 = (bf16[160,4096]{1,0:T(8,128)(2,1)S(1)}, bf16[160,4096]{1,0:T(8,128)(2,1)}, u32[]{:S(2)}, u32[]{:S(2)}) collective-permute-start(bf16[160,4096]{1,0:T(8,128)(2,1)S(1)} %slice.27), channel_id=1, source_target_pairs={{0,3},{1,0},{2,1},{3,2},{4,7},{5,4},{6,5},{7,6},{8,11},{9,8},{10,9... | collective-permute-start | bytes 3932168 | tf_op jit(solution)/shard_map/ppermute | solution.py:26
  155.5 39.5 %collective-permute-start.9 = (bf16[512,512]{1,0:T(8,128)(2,1)}, bf16[512,512]{1,0:T(8,128)(2,1)}, u32[]{:S(2)}, u32[]{:S(2)}) collective-permute-start(bf16[512,512]{1,0:T(8,128)(2,1)} %query_gradient.6), channel_id=1, source_target_pairs={{0,3},{1,0},{2,1},{3,2},{4,7},{5,4},{6,5},{7,6},{8,11},{9,8},{10,9... | collective-permute-start | bytes 1572872 | tf_op jit(solution)/shard_map/ppermute | solution.py:26
  156.0 39.0 %collective-permute-start.8 = (bf16[512,256]{1,0:T(8,128)(2,1)S(1)}, bf16[512,256]{1,0:T(8,128)(2,1)S(1)}, u32[]{:S(2)}, u32[]{:S(2)}) collective-permute-start(bf16[512,256]{1,0:T(8,128)(2,1)S(1)} %copy-done.4), channel_id=1, source_target_pairs={{0,3},{1,0},{2,1},{3,2},{4,7},{5,4},{6,5},{7,6},{8,11},{9,8},{10,9... | collective-permute-start | bytes 786440 | tf_op jit(solution)/shard_map/ppermute | solution.py:26
  195.8 46.8 %collective-permute-start.13 = (bf16[2048,2048]{1,0:T(8,128)(2,1)}, bf16[2048,2048]{1,0:T(8,128)(2,1)}, u32[]{:S(2)}, u32[]{:S(2)}) collective-permute-start(bf16[2048,2048]{1,0:T(8,128)(2,1)} %all-gather.2.cloned.1.call-done.refs_9_), channel_id=1, source_target_pairs={{0,4},{4,0},{8,12},{12,8},{16,20},{20,16},{24,28},{28,24},{32,36},... | collective-permute-start | bytes 25165832 | tf_op jit(solution)/shard_map/ppermute | solution.py:365
  203.2 23.3 %all-to-all-start.4 = ((bf16[32,32,512]{2,1,0:T(8,128)(2,1)}), bf16[32,32,512]{2,1,0:T(8,128)(2,1)S(1)}, u32[]{:S(2)}, u32[]{:S(2)}) async-start(bf16[32,32,512]{2,1,0:T(8,128)(2,1)} %pick_rows.7), calls=%async_computation.4 | async-start | bytes 2097152 | tf_op jit(solution)/shard_map/all_to_all | solution.py:312
  210.2 16.3 %collective-permute-start.10 = (bf16[512,512]{1,0:T(8,128)(2,1)}, bf16[512,512]{1,0:T(8,128)(2,1)S(1)}, u32[]{:S(2)}, u32[]{:S(2)}) collective-permute-start(bf16[512,512]{1,0:T(8,128)(2,1)} %query_gradient.7), channel_id=1, source_target_pairs={{0,3},{1,0},{2,1},{3,2},{4,7},{5,4},{6,5},{7,6},{8,11},{9,8},{10,9... | collective-permute-start | bytes 1572872 | tf_op jit(solution)/shard_map/ppermute | solution.py:26
  218.2 18.7 %collective-permute-start.11 = (bf16[512,512]{1,0:T(8,128)(2,1)}, bf16[512,512]{1,0:T(8,128)(2,1)S(1)}, u32[]{:S(2)}, u32[]{:S(2)}) collective-permute-start(bf16[512,512]{1,0:T(8,128)(2,1)} %query_gradient.8), channel_id=1, source_target_pairs={{0,3},{1,0},{2,1},{3,2},{4,7},{5,4},{6,5},{7,6},{8,11},{9,8},{10,9... | collective-permute-start | bytes 1572872 | tf_op jit(solution)/shard_map/ppermute | solution.py:26
  226.5 16.2 %copy-start.7 = (bf16[512,512]{1,0:T(8,128)(2,1)}, bf16[512,512]{1,0:T(8,128)(2,1)S(1)}, u32[]{:S(2)}) copy-start(bf16[512,512]{1,0:T(8,128)(2,1)S(1)} %collective-permute-done.10.refs_2_) | copy-start | bytes 1572868
  233.1 9.6 %collective-permute-start.12 = (bf16[512,256]{1,0:T(8,128)(2,1)}, bf16[512,256]{1,0:T(8,128)(2,1)S(1)}, u32[]{:S(2)}, u32[]{:S(2)}) collective-permute-start(bf16[512,256]{1,0:T(8,128)(2,1)} %query_gradient.9), channel_id=1, source_target_pairs={{0,3},{1,0},{2,1},{3,2},{4,7},{5,4},{6,5},{7,6},{8,11},{9,8},{10,9... | collective-permute-start | bytes 786440 | tf_op jit(solution)/shard_map/ppermute | solution.py:26
  (9 other events, 36.5 us)
Sparse Core Ops, SparseCore 0:
  22.6 102.7 all-gather.1
